TPU v7x, 512 devices: a whole 4x4x16 slice. The times are simulated.
512 devices in a mesh: dp: 64 (over x, z), tensor: 8 (over y, core).
Axes of the slice: x: 4, y: 4, z: 16, core: 2. Of those that a mesh axis runs over, the one named last changes fastest.
Arguments:
- residual: bfloat16 [2048, 6144], P('dp', 'tensor'), may hold values from -16 to 16
- queries: bfloat16 [2048, 6144], P('dp', 'tensor'), may hold values from -4.5 to 4.5
- keys: bfloat16 [2048, 128, 1024], P('dp', None, 'tensor'), may hold values from -4.5 to 4.5
- values: bfloat16 [2048, 128, 1024], P('dp', None, 'tensor'), may hold values from -6 to 6
- lengths: int32 [2048], P('dp'), may hold values from 2 to 128
- norm_gain: bfloat16 [6144], P('tensor'), may hold values from 0.099609375 to 1.8984375
- expert_ids: int32 [2048, 2], P('dp'), may hold values from 0 to 7, all different within a row; in each aligned block of 32 rows (0 to 31, 32 to 63, ...) at most 16 rows name the same one
- expert_weights: float32 [2048, 2], P('dp'), may hold values from 0.2 to 1
- w_in: bfloat16 [6144, 65536], P('tensor', 'dp'), may hold values from -0.078125 to 0.078125
- w_out: bfloat16 [65536, 6144], P('dp', 'tensor'), may hold values from -0.0625 to 0.0625
Outputs:
- output: bfloat16 [2048, 6144], P('dp', 'tensor')
Inputs may be any that keep to these rules, and one draw needn't show every extreme that they name: `expert_ids`: each token names 2 different experts; at most 16 of the tokens of one index of dp name one expert, and in every draw some expert is named by exactly 16 of them.
All inputs are finite; a program needn't handle non-finite values.
Results may differ from a plain program's by a relative error of at most 0.008.
Values may be sent and summed in bfloat16 or wider, within the bound.
No kernel may reach another device: no remote copies, remote signals or barrier semaphores. Data moves between devices by JAX's collectives and lax.ppermute only.
A program may use at most 64 MiB of HBM per device.

v0:
```python
import jax
import jax.numpy as jnp
from jax import lax
from jax.sharding import PartitionSpec as P

D = 6144
HEADS = 48
KV = 8
HEAD = 128
EXPERTS = 8
TOPK = 2
CACHE = 128
SRC_CAP = 16


NORM_EPSILON = 1e-05


def cut_along(value, dim, peers):
    before, after = (value.shape[:dim], value.shape[dim + 1 :])
    return jnp.moveaxis(value.reshape(*before, peers, -1, *after), dim, 0)


def sum_at_owner(value, axis, dim):
    peers = lax.axis_size(axis)
    tiles = lax.all_to_all(cut_along(value, dim, peers), axis, 0, 0, tiled=True)
    return jnp.sum(tiles.astype(jnp.float32), axis=0)


def copy_for_each(value, axis):
    copies = jnp.broadcast_to(value, (lax.axis_size(axis), *value.shape))
    return lax.all_to_all(copies, axis, split_axis=0, concat_axis=0, tiled=True)


def in_order(tiles, dim):
    tiles = jnp.moveaxis(tiles, 0, dim)
    dims = tiles.shape
    return tiles.reshape(*dims[:dim], dims[dim] * dims[dim + 1], *dims[dim + 2 :])


def collect(value, axis, dim):
    tiles = copy_for_each(value, axis)
    return in_order(tiles, dim)


def of_everyone(value, axis):
    everything = copy_for_each(value, axis)
    return jnp.sum(everything, axis=0)


def joined_by_halves(pieces, combine):
    while len(jax.tree.leaves(pieces)[0]) > 1:
        pieces = jax.vmap(combine)(*(pieces[side::2] for side in (0, 1)))
    return pieces[0]


def entering(value, axis, combine, identity):
    peers, here = (lax.axis_size(axis), lax.axis_index(axis))
    passed = jnp.arange(peers) < here

    def kept(part, zero, own):
        part = jnp.where(
            passed.reshape(-1, *(1 for _ in own.shape)), part, jnp.asarray(zero, own.dtype)
        )
        return part

    pieces = copy_for_each(value, axis)
    return joined_by_halves(kept(pieces, identity, value), combine)


def add_counts(earlier, later):
    return earlier + later


def expert_rows(tok_rows, w_in, w_out):
    weight_block = w_in
    own_hidden = sum_at_owner(
        jnp.einsum("df,rd->fr", weight_block, tok_rows, preferred_element_type=jnp.float32).astype(
            jnp.bfloat16
        ),
        "tensor",
        0,
    )
    hidden = jax.nn.silu(own_hidden).astype(jnp.bfloat16)
    weight_block = w_out
    return jnp.einsum(
        "fr,fd->rd", collect(hidden, "tensor", 0), weight_block, preferred_element_type=jnp.float32
    )


def shards(
    residual, queries, keys, values, lengths, norm_gain, expert_ids, expert_weights, w_in, w_out
):
    tokens = residual.shape[0]
    width_local = residual.shape[1]
    head_groups = keys.shape[2] // HEAD
    group_size = HEADS // KV
    query_rows = queries.reshape(tokens, head_groups, group_size, HEAD)
    key_rows = keys.reshape(tokens, CACHE, head_groups, HEAD)
    value_rows = values.reshape(tokens, CACHE, head_groups, HEAD)
    scores = jnp.einsum(
        "tgjd,tlgd->tgjl", query_rows, key_rows, preferred_element_type=jnp.float32
    ) * HEAD ** (-0.5)
    live_mask = (jnp.arange(CACHE, dtype=jnp.int32)[None, :] < lengths[:, None])[:, None, None, :]
    scores = jnp.where(live_mask, scores, -1e30)
    peak_score = jnp.max(scores, axis=-1, keepdims=True)
    powered = jnp.exp(scores - peak_score)
    attention_probs = (powered / jnp.sum(powered, axis=-1, keepdims=True)).astype(jnp.bfloat16)
    attended = jnp.einsum(
        "tgjl,tlgd->tgjd", attention_probs, value_rows, preferred_element_type=jnp.float32
    )
    summed = residual.astype(jnp.float32) + attended.reshape(tokens, width_local)
    square_sums = of_everyone(jnp.sum(summed * summed, axis=1), "tensor")
    normed = (
        summed
        * lax.rsqrt(square_sums[:, None] / D + NORM_EPSILON)
        * norm_gain.astype(jnp.float32)[None, :]
    ).astype(jnp.bfloat16)
    flat_ids = expert_ids.reshape(-1)
    expert_iota = jnp.arange(EXPERTS, dtype=jnp.int32)
    onehot = (flat_ids[:, None] == expert_iota[None, :]).astype(jnp.int32)
    local_rank = jnp.sum(
        (jnp.cumsum(onehot, axis=0, dtype=jnp.int32) - onehot) * onehot, axis=1, dtype=jnp.int32
    )
    counts = jnp.sum(onehot, axis=0, dtype=jnp.int32)
    offsets = entering(counts, "dp", add_counts, jnp.zeros_like(counts))
    slot_index = local_rank + jnp.sum(onehot * offsets[None, :], axis=1, dtype=jnp.int32)
    capacity = tokens * lax.axis_size("dp") * TOPK * 3 // (4 * EXPERTS)
    keep_mask = slot_index < capacity
    owners = lax.axis_size("dp") // EXPERTS
    slot_total = EXPERTS * SRC_CAP
    pair_target = flat_ids * SRC_CAP + local_rank
    pick_pairs = pair_target[None, :] == jnp.arange(slot_total, dtype=jnp.int32)[:, None]
    pick_tokens = jnp.sum(
        pick_pairs.reshape(slot_total, tokens, TOPK).astype(jnp.float32), axis=2
    ).astype(jnp.bfloat16)
    packed = jnp.dot(pick_tokens, normed, preferred_element_type=jnp.float32).astype(jnp.bfloat16)
    outgoing = jnp.broadcast_to(
        packed.reshape(EXPERTS, 1, SRC_CAP, width_local), (EXPERTS, owners, SRC_CAP, width_local)
    )
    outgoing = outgoing.reshape(EXPERTS * owners, SRC_CAP, width_local)
    received = lax.all_to_all(outgoing, "dp", split_axis=0, concat_axis=0, tiled=True)
    total_rows = received.shape[0] * received.shape[1]
    results = expert_rows(received.reshape(total_rows, width_local), w_in, w_out)
    returned = results.reshape(received.shape[0], SRC_CAP, width_local)
    combined = lax.all_to_all(
        returned.astype(jnp.bfloat16), "dp", split_axis=0, concat_axis=0, tiled=True
    ).astype(returned.dtype)
    per_expert = jnp.sum(combined.reshape(EXPERTS, owners, SRC_CAP, width_local), axis=1).reshape(
        slot_total, width_local
    )
    pair_weight = expert_weights.reshape(-1) * keep_mask.astype(jnp.float32)
    mix_rows = jnp.sum(
        (pick_pairs.astype(jnp.float32) * pair_weight[None, :]).reshape(slot_total, tokens, TOPK),
        axis=2,
    )
    addition = jnp.einsum("st,sd->td", mix_rows, per_expert, precision=lax.Precision.HIGHEST)
    return (summed + addition).astype(jnp.bfloat16)


def solution(mesh):
    in_specs = (
        P("dp", "tensor"),
        P("dp", "tensor"),
        P("dp", None, "tensor"),
        P("dp", None, "tensor"),
        P("dp"),
        P("tensor"),
        P("dp", None),
        P("dp", None),
        P("tensor", "dp"),
        P("dp", "tensor"),
    )
    out_specs = P("dp", "tensor")
    return jax.shard_map(shards, mesh=mesh, in_specs=in_specs, out_specs=out_specs, check_vma=False)
```

profile of v0, /device:TPU:6, one launch (start us, length us, event | category | flops | bytes accessed | tf_op | source)
XLA Modules:
  0.0 287.5 jit_solution(13341060529650670605)
XLA Ops:
  0.0 0.0 copy-start
  0.0 0.0 copy-start.1
  0.0 0.0 copy-start.2
  0.0 0.0 copy-start.3
  0.0 0.0 copy-start.4
  0.0 0.9 iota_compare_fusion.2
  0.9 0.9 reshape.147
  1.8 0.0 copy-start.5
  1.8 1.9 fusion.4
  3.7 0.2 fusion.13
  3.9 0.0 copy-done.1
  3.9 0.6 fusion.6
  4.5 0.0 copy-done.2
  4.5 0.1 multiply_reduce_fusion
  4.6 0.6 broadcast_in_dim.53
  5.2 4.5 %all-to-all-start.1 = ((f32[8,1,32]{2,1,0:T(1,128)}), f32[8,1,32]{2,1,0:T(1,128)S(1)}, u32[]{:S(2)}, u32[]{:S(2)}) async-start(f32[8,1,32]{2,1,0:T(1,128)} %broadcast_in_dim.53), calls=%async_computation.1 | async-start | bytes 8192 | tf_op jit(solution)/shard_map/all_to_all | solution.py:32
  9.7 0.0 copy-done.3
  9.7 0.1 copy.58
  9.8 0.1 eq.30
  9.9 0.1 fusion.11
  10.0 0.1 fusion.10
  10.1 0.0 copy-done.4
  10.1 0.1 reduce_window_sum.11
  10.2 4.7 %all-to-all-done.1 = f32[8,1,32]{2,1,0:T(1,128)S(1)} async-done(((f32[8,1,32]{2,1,0:T(1,128)}), f32[8,1,32]{2,1,0:T(1,128)S(1)}, u32[]{:S(2)}, u32[]{:S(2)}) %all-to-all-start.1) | async-done | bytes 1056 | tf_op jit(solution)/shard_map/all_to_all | solution.py:32
  14.9 0.6 broadcast_in_dim.52
  15.5 18.8 %all-to-all-start = ((s32[64,1,8]{2,1,0:T(1,128)}), s32[64,1,8]{2,1,0:T(1,128)S(1)}, u32[]{:S(2)}, u32[]{:S(2)}) async-start(s32[64,1,8]{2,1,0:T(1,128)} %broadcast_in_dim.52), calls=%async_computation | async-start | bytes 65536 | tf_op jit(solution)/shard_map/all_to_all | solution.py:32
  34.4 12.4 %all-to-all-done = s32[64,1,8]{2,1,0:T(1,128)S(1)} async-done(((s32[64,1,8]{2,1,0:T(1,128)}), s32[64,1,8]{2,1,0:T(1,128)S(1)}, u32[]{:S(2)}, u32[]{:S(2)}) %all-to-all-start) | async-done | bytes 2080 | tf_op jit(solution)/shard_map/all_to_all | solution.py:32
  46.8 0.1 broadcast_select_fusion
  47.1 0.2 select_reduce_fusion.1
  47.3 0.1 reduce_sum.99
  47.4 0.1 copy.61
  47.5 0.1 reduce_sum.96
  47.6 0.1 copy.59
  47.7 0.0 copy-done.5
  47.7 0.1 convert_reduce_fusion.2
  47.8 0.3 convolution_convert_fusion.2
  48.1 0.1 broadcast_in_dim.55
  48.2 80.8 %all_to_all.35 = bf16[64,16,768]{2,1,0:T(8,128)(2,1)S(1)} all-to-all(bf16[64,16,768]{2,1,0:T(8,128)(2,1)S(1)} %bitcast.43), channel_id=1, replica_groups=mesh['dp'=64,'tensor'=8] {'dp'}, dimensions={0} | all-to-all | bytes 3145728 | tf_op jit(solution)/shard_map/all_to_all | solution.py:142
  128.9 0.0 copy-done
  128.9 1.9 convolution_convert_fusion
  130.8 30.0 %all_to_all.36 = bf16[8,128,1024]{2,1,0:T(8,128)(2,1)S(1)} all-to-all(bf16[8,128,1024]{2,1,0:T(8,128)(2,1)S(1)} %bitcast.44), channel_id=1, replica_groups=mesh['dp'=64,'tensor'=8] {'tensor'}, dimensions={0} | all-to-all | bytes 4194304 | tf_op jit(solution)/shard_map/all_to_all | solution.py:26
  160.8 0.4 convert_reduce_fusion
  161.1 0.1 multiply_convert_fusion
  161.3 0.2 copy.63
  161.4 0.3 broadcast_in_dim.56
  161.7 30.7 %all_to_all.37 = bf16[8,128,1024]{1,2,0:T(8,128)(2,1)} all-to-all(bf16[8,128,1024]{1,2,0:T(8,128)(2,1)S(1)} %broadcast_in_dim.56), channel_id=1, replica_groups=mesh['dp'=64,'tensor'=8] {'tensor'}, dimensions={0} | all-to-all | bytes 4194304 | tf_op jit(solution)/shard_map/all_to_all | solution.py:32
  192.4 3.9 %copy.64 = bf16[8,128,1024]{2,1,0:T(8,128)(2,1)} copy(bf16[8,128,1024]{1,2,0:T(8,128)(2,1)} %all_to_all.37) | data formatting | bytes 4194304 | tf_op jit(solution)/shard_map/all_to_all | solution.py:32
  196.3 0.0 copy-start.6
  196.3 4.1 %copy.65 = bf16[1024,1024]{1,0:T(8,128)(2,1)} copy(bf16[1024,1024]{0,1:T(8,128)(2,1)} %bitcast.42) | data formatting | bytes 4194304 | tf_op jit(solution)/shard_map/fr,fd->rd/dot_general | solution.py:86
  200.4 0.0 copy-done.6
  200.4 3.4 %convolution_convert_fusion.1 = bf16[64,16,768]{2,1,0:T(8,128)(2,1)S(1)} fusion(bf16[64,16,1024]{2,1,0:T(8,128)(2,1)} %bitcast.45, bf16[1024,768]{1,0:T(8,128)(2,1)S(1)} %copy-done.6), kind=kOutput, calls=%fused_computation.4 | convolution fusion | flops 1611399168 | bytes 5242880 | tf_op jit(solution)/shard_map/fr,fd->rd/dot_general | solution.py:86
  203.8 82.5 %all_to_all.38 = bf16[64,16,768]{2,1,0:T(8,128)(2,1)S(1)} all-to-all(bf16[64,16,768]{2,1,0:T(8,128)(2,1)S(1)} %convolution_convert_fusion.1), channel_id=1, replica_groups=mesh['dp'=64,'tensor'=8] {'dp'}, dimensions={0} | all-to-all | bytes 3145728 | tf_op jit(solution)/shard_map/all_to_all | solution.py:146
  286.3 0.2 convert_reduce_fusion.1
  286.5 1.0 fusion.5
  (22 shorter events, 0.3 us)
Async XLA Ops:
  0.0 128.9 %copy-start = (bf16[768,1024]{1,0:T(8,128)(2,1)S(1)}, bf16[768,1024]{1,0:T(8,128)(2,1)}, u32[]{:S(2)}) copy-start(bf16[768,1024]{1,0:T(8,128)(2,1)} %param.18) | copy-start | bytes 4718596
  0.0 3.9 %copy-start.1 = (bf16[32,128,128]{2,1,0:T(8,128)(2,1)S(1)}, bf16[32,128,128]{2,1,0:T(8,128)(2,1)}, u32[]{:S(2)}) copy-start(bf16[32,128,128]{2,1,0:T(8,128)(2,1)} %param.13) | copy-start | bytes 3145732
  0.0 4.5 %copy-start.2 = (bf16[32,768]{1,0:T(8,128)(2,1)S(1)}, bf16[32,768]{1,0:T(8,128)(2,1)}, u32[]{:S(2)}) copy-start(bf16[32,768]{1,0:T(8,128)(2,1)} %param.10) | copy-start | bytes 147460
  0.0 9.7 %copy-start.3 = (s32[32,2]{0,1:T(2,128)S(1)}, s32[32,2]{0,1:T(2,128)}, u32[]{:S(2)}) copy-start(s32[32,2]{0,1:T(2,128)} %param.16) | copy-start | bytes 772
  0.0 10.1 %copy-start.4 = (bf16[768]{0:T(1024)(128)(2,1)S(1)}, bf16[768]{0:T(1024)(128)(2,1)}, u32[]{:S(2)}) copy-start(bf16[768]{0:T(1024)(128)(2,1)} %param.15) | copy-start | bytes 4612
  1.8 45.9 %copy-start.5 = (f32[32,2]{0,1:T(2,128)S(1)}, f32[32,2]{0,1:T(2,128)}, u32[]{:S(2)}) copy-start(f32[32,2]{0,1:T(2,128)} %param.17) | copy-start | bytes 772
  5.2 9.7 %all-to-all-start.1 = ((f32[8,1,32]{2,1,0:T(1,128)}), f32[8,1,32]{2,1,0:T(1,128)S(1)}, u32[]{:S(2)}, u32[]{:S(2)}) async-start(f32[8,1,32]{2,1,0:T(1,128)} %broadcast_in_dim.53), calls=%async_computation.1 | async-start | bytes 8192 | tf_op jit(solution)/shard_map/all_to_all | solution.py:32
  15.5 31.3 %all-to-all-start = ((s32[64,1,8]{2,1,0:T(1,128)}), s32[64,1,8]{2,1,0:T(1,128)S(1)}, u32[]{:S(2)}, u32[]{:S(2)}) async-start(s32[64,1,8]{2,1,0:T(1,128)} %broadcast_in_dim.52), calls=%async_computation | async-start | bytes 65536 | tf_op jit(solution)/shard_map/all_to_all | solution.py:32
  196.3 4.1 %copy-start.6 = (bf16[1024,768]{1,0:T(8,128)(2,1)S(1)}, bf16[1024,768]{1,0:T(8,128)(2,1)}, u32[]{:S(2)}) copy-start(bf16[1024,768]{1,0:T(8,128)(2,1)} %param.19) | copy-start | bytes 4718596
where the time goes:
time: 288 us; the launch traced here: 287 us
  blocking collectives  224 us (78%)
  starting transfers between devices  23.3 us (8%)
  waiting for transfers between devices  17.1 us (6%)
  local copies, waits for them, and re-layouts  11.4 us (4%)
  matrix products  8.9 us (3%)
    all_to_all x1, blocking collectives, shards(): lax.all_to_all(returned.astype(jnp.bfloat16), 'dp', split_axis=0, concat_...  82.5 us
    all_to_all x1, blocking collectives, shards(): lax.all_to_all(outgoing, 'dp', split_axis=0, concat_axis=0, tiled=True)  80.8 us
    all_to_all x1, blocking collectives, copy_for_each(): return lax.all_to_all(copies, axis, split_axis=0, concat_axis=0, tiled=True)  30.7 us
    all_to_all x1, blocking collectives, sum_at_owner(): tiles = lax.all_to_all(cut_along(value, dim, peers), axis, 0, 0, tiled=True)  30 us
    all_to_all x2, starting transfers between devices, copy_for_each(): return lax.all_to_all(copies, axis, split_axis=0, concat_axis=0, tiled=True)  23.3 us
    all_to_all x2, waiting for transfers between devices, copy_for_each(): return lax.all_to_all(copies, axis, split_axis=0, concat_axis=0, tiled=True)  17.1 us
  transfers between devices with their start and end apart: 2, of which 2 were waited for; matrix products, arithmetic and copies ran while one was open for 0% of the time, Pallas kernels for 0%

commit v1 on v0

v1 whole, which is shorter than its diff:
```python
import jax
import jax.numpy as jnp
from jax import lax
from jax.sharding import Mesh, PartitionSpec as P

HEADS = 48
KV = 8
HEAD = 128
D = 6144
EXPERTS = 8
TOPK = 2
CACHE = 128
SRC_CAP = 16
BLOCKS = 64
CLASSES = 4
PER_CLASS = SRC_CAP // CLASSES
CAPACITY = 384
CLASS_ROWS = CAPACITY // CLASSES + BLOCKS * 6 // (4 * CLASSES)
META = 128

NORM_EPSILON = 1e-05

DP = ("x", "zh", "zq", "zn")
TENSOR = ("y", "core")


def attend(residual, queries, keys, values, lengths):
    tokens, width = residual.shape
    group_size = HEADS // KV
    query_rows = queries.reshape(tokens, group_size, HEAD)
    scores = jnp.einsum(
        "tjd,tld->tjl", query_rows, keys, preferred_element_type=jnp.float32
    ) * HEAD ** (-0.5)
    live_mask = (jnp.arange(CACHE, dtype=jnp.int32)[None, :] < lengths[:, None])[:, None, :]
    scores = jnp.where(live_mask, scores, -1e30)
    peak_score = jnp.max(scores, axis=-1, keepdims=True)
    powered = jnp.exp(scores - peak_score)
    probs = (powered / jnp.sum(powered, axis=-1, keepdims=True)).astype(jnp.bfloat16)
    attended = jnp.einsum("tjl,tld->tjd", probs, values, preferred_element_type=jnp.float32)
    return residual.astype(jnp.float32) + attended.reshape(tokens, width)


def copies_to(value, axis, peers):
    copies = jnp.broadcast_to(value, (peers, *value.shape))
    return lax.all_to_all(copies, axis, split_axis=0, concat_axis=0, tiled=True)


def summed_at_owner(pieces, axis):
    return jnp.sum(
        lax.all_to_all(pieces, axis, split_axis=0, concat_axis=0, tiled=True).astype(jnp.float32), axis=0
    )


def earlier_sum(counts):
    before = jnp.arange(BLOCKS)[:, None] > jnp.arange(BLOCKS)[None, :]
    return jnp.sum(jnp.where(before, counts[None, :], 0), axis=1)


def shards(
    residual, queries, keys, values, lengths, norm_gain, expert_ids, expert_weights, w_in, w_out
):
    tokens, width = residual.shape
    block = ((lax.axis_index("x") * 2 + lax.axis_index("zh")) * 2 + lax.axis_index("zq")) * 4 + lax.axis_index("zn")
    own_class = lax.axis_index("zn")

    summed = attend(residual, queries, keys, values, lengths)
    square_sums = lax.psum(jnp.sum(summed * summed, axis=1), TENSOR)
    normed = (
        summed
        * lax.rsqrt(square_sums[:, None] / D + NORM_EPSILON)
        * norm_gain.astype(jnp.float32)[None, :]
    ).astype(jnp.bfloat16)

    flat_ids = expert_ids.reshape(-1)
    pairs = flat_ids.shape[0]
    same = flat_ids[:, None] == flat_ids[None, :]
    earlier = jnp.arange(pairs)[:, None] > jnp.arange(pairs)[None, :]
    rank = jnp.sum((same & earlier).astype(jnp.int32), axis=1)
    slots = EXPERTS * SRC_CAP
    target = flat_ids * SRC_CAP + (rank + block) % CLASSES * PER_CLASS + rank // CLASSES
    pick_pairs = target[None, :] == jnp.arange(slots, dtype=jnp.int32)[:, None]
    pick_tokens = jnp.sum(
        pick_pairs.reshape(slots, tokens, TOPK).astype(jnp.float32), axis=2
    ).astype(jnp.bfloat16)
    counts = jnp.sum(
        (flat_ids[None, :] == jnp.arange(EXPERTS, dtype=jnp.int32)[:, None]).astype(jnp.float32), axis=1
    ).astype(jnp.bfloat16)

    packed = jnp.dot(pick_tokens, normed, preferred_element_type=jnp.float32).astype(jnp.bfloat16)
    packed = packed.reshape(EXPERTS, 1, CLASSES, PER_CLASS, width)
    meta = jnp.broadcast_to(counts[:, None, None, None, None], (EXPERTS, 1, CLASSES, PER_CLASS, META))
    outgoing = jnp.concatenate([packed, meta], axis=-1)
    outgoing = jnp.broadcast_to(outgoing, (EXPERTS, 2, CLASSES, PER_CLASS, width + META))
    received = lax.all_to_all(
        outgoing.reshape(BLOCKS, PER_CLASS, width + META), DP, split_axis=0, concat_axis=0, tiled=True
    )

    named = received[:, 0, width].astype(jnp.int32)
    kept = jnp.clip(CAPACITY - earlier_sum(named), 0, named)
    shift = (own_class - jnp.arange(BLOCKS, dtype=jnp.int32)) % CLASSES
    in_class = (kept - shift + CLASSES - 1) // CLASSES
    first = earlier_sum(in_class)
    place = jnp.arange(PER_CLASS, dtype=jnp.int32)[None, :]
    spot = jnp.where(place < in_class[:, None], first[:, None] + place, -1).reshape(-1)
    compact = (spot[None, :] == jnp.arange(CLASS_ROWS, dtype=jnp.int32)[:, None]).astype(jnp.bfloat16)
    class_rows = jnp.dot(
        compact,
        received[:, :, :width].reshape(BLOCKS * PER_CLASS, width),
        preferred_element_type=jnp.float32,
    ).astype(jnp.bfloat16)

    rows = copies_to(class_rows, "zn", CLASSES).reshape(CLASSES * CLASS_ROWS, width)
    total = rows.shape[0]
    hidden_parts = jnp.dot(rows, w_in, preferred_element_type=jnp.float32).astype(jnp.bfloat16)
    unit = hidden_parts.shape[1] // 8
    pieces = jnp.moveaxis(hidden_parts.reshape(total, 2, 4, unit), 0, 2)
    core_sums = summed_at_owner(pieces, "core").astype(jnp.bfloat16)
    hidden = jax.nn.silu(summed_at_owner(core_sums.reshape(4, total, unit), "y")).astype(jnp.bfloat16)
    gathered = copies_to(hidden, "y", 4)
    gathered = lax.all_gather(gathered, "core", axis=0, tiled=True)
    hidden_all = jnp.moveaxis(gathered, 0, 1).reshape(total, 8 * unit)
    results = jnp.dot(hidden_all, w_out, preferred_element_type=jnp.float32).astype(jnp.bfloat16)

    class_out = summed_at_owner(results.reshape(CLASSES, CLASS_ROWS, width), "zn").astype(jnp.bfloat16)
    spread = (spot[:, None] == jnp.arange(CLASS_ROWS, dtype=jnp.int32)[None, :]).astype(jnp.bfloat16)
    returned = jnp.dot(spread, class_out, preferred_element_type=jnp.float32).astype(jnp.bfloat16)
    combined = lax.all_to_all(
        returned.reshape(BLOCKS, PER_CLASS, width), DP, split_axis=0, concat_axis=0, tiled=True
    )
    per_expert = jnp.sum(
        combined.reshape(EXPERTS, 2, SRC_CAP, width).astype(jnp.float32), axis=1
    ).reshape(slots, width)
    mix_rows = jnp.sum(
        (pick_pairs.astype(jnp.float32) * expert_weights.reshape(-1)[None, :]).reshape(slots, tokens, TOPK),
        axis=2,
    )
    addition = jnp.einsum("st,sd->td", mix_rows, per_expert, precision=lax.Precision.HIGHEST)
    return (summed + addition).astype(jnp.bfloat16)


def solution(mesh):
    fine = Mesh(mesh.devices.reshape(4, 2, 2, 4, 4, 2), (*DP, *TENSOR))
    in_specs = (
        P(DP, TENSOR),
        P(DP, TENSOR),
        P(DP, None, TENSOR),
        P(DP, None, TENSOR),
        P(DP),
        P(TENSOR),
        P(DP, None),
        P(DP, None),
        P(TENSOR, DP),
        P(DP, TENSOR),
    )
    return jax.shard_map(shards, mesh=fine, in_specs=in_specs, out_specs=P(DP, TENSOR), check_vma=False)
```

time: 288 us -> 186 us (0.65)
  blocking collectives: 224 us -> 168 us
  starting transfers between devices: 23.3 us -> 0 us
  waiting for transfers between devices: 17.1 us -> 0 us
  local copies, waits for them, and re-layouts: 11.4 us -> 5.51 us
    all_to_all x4 -> x7, blocking collectives: 224 us -> 150 us  [the longest x1 45.3 us: shards(): lax.all_to_all(outgoing.reshape(BLOCKS, PER_CLASS, width + META), DP, spl...]
    all_to_all x2 -> x0, starting transfers between devices: 23.3 us -> none  [copy_for_each(): return lax.all_to_all(copies, axis, split_axis=0, concat_axis=0, tiled=True)]
    all_to_all x2 -> x0, waiting for transfers between devices: 17.1 us -> none  [copy_for_each(): return lax.all_to_all(copies, axis, split_axis=0, concat_axis=0, tiled=True)]
    psum x0 -> x1, blocking collectives: none -> 14.9 us  [shards(): square_sums = lax.psum(jnp.sum(summed * summed, axis=1), TENSOR)]
    dot_general x1 -> x0, local copies, waits for them, and re-layouts: 4.07 us -> none  [expert_rows(): jnp.einsum('fr,fd->rd', collect(hidden, 'tensor', 0), weight_block, prefe...]
    all_to_all x1 -> x0, local copies, waits for them, and re-layouts: 3.93 us -> none  [copy_for_each(): return lax.all_to_all(copies, axis, split_axis=0, concat_axis=0, tiled=True)]
    reshape x0 -> x6, local copies, waits for them, and re-layouts: none -> 3.63 us  [the longest x2 2.5 us: shards(): pieces = jnp.moveaxis(hidden_parts.reshape(total, 2, 4, unit), 0, 2)]
    dot_general x4 -> x6, matrix products: 7.69 us -> 5.78 us  [the longest x1 1.89 us: shards(): jnp.dot(rows, w_in, preferred_element_type=jnp.float32).astype(jnp.bfloat16)]
  transfers between devices with their start and end apart: 2 -> 0, of which waited for: 2 -> 0; matrix products, arithmetic and copies ran while one was open for 0% -> 0% of each run, Pallas kernels for 0% -> 0%
where the time goes in v1:
time: 186 us
  blocking collectives  168 us (90%)
  matrix products  6.99 us (4%)
  local copies, waits for them, and re-layouts  5.51 us (3%)
  other arithmetic  5.19 us (3%)
    all_to_all x1, blocking collectives, shards(): lax.all_to_all(outgoing.reshape(BLOCKS, PER_CLASS, width + META), DP, spl...  45.3 us
    all_to_all x3, blocking collectives, summed_at_owner(): lax.all_to_all(pieces, axis, split_axis=0, concat_axis=0, tiled=True)  42.6 us
    all_to_all x1, blocking collectives, shards(): lax.all_to_all(returned.reshape(BLOCKS, PER_CLASS, width), DP, split_axis...  33.2 us
    all_to_all x2, blocking collectives, copies_to(): return lax.all_to_all(copies, axis, split_axis=0, concat_axis=0, tiled=True)  29.3 us
    psum x1, blocking collectives, shards(): square_sums = lax.psum(jnp.sum(summed * summed, axis=1), TENSOR)  14.9 us

profile of v1, /device:TPU:6, one launch (start us, length us, event | category | flops | bytes accessed | tf_op | source)
XLA Modules:
  0.0 185.7 jit_solution(11705358472968257919)
XLA Ops:
  0.0 0.0 copy-start
  0.0 0.0 copy-start.3
  0.0 0.0 copy-start.1
  0.0 0.0 copy-start.2
  0.0 0.0 copy-start.4
  0.0 0.9 copy.57
  0.9 0.1 eq.72
  1.1 0.2 convert_reduce_fusion.2
  1.2 0.1 convert_reduce_fusion.3
  1.4 0.7 iota_compare_fusion.7
  2.1 0.7 convert_element_type.90
  2.8 0.1 reduce_sum.118
  2.9 0.1 copy.58
  3.0 0.9 reshape.277
  3.8 1.9 %fusion.3 = f32[32,6,128]{2,1,0:T(8,128)S(1)} fusion(bf16[32,6,128]{2,1,0:T(8,128)(2,1)S(1)} %reshape.277, bf16[32,128,128]{2,1,0:T(8,128)(2,1)} %param.12, pred[32,128]{1,0:T(8,128)(4,1)S(1)} %iota_compare_fusion.7), kind=kOutput, calls=%fused_computation.9 | convolution fusion | flops 6340608 | bytes 1200128 | tf_op jit(solution)/shard_map/tjd,tld->tjl/dot_general | solution.py:31
  5.7 0.2 fusion.22
  5.9 0.0 copy-done.1
  5.9 0.6 fusion.7
  6.5 0.0 copy-done.2
  6.5 0.1 multiply_reduce_fusion
  6.7 14.9 %psum.7 = f32[32]{0:T(128)S(1)} all-reduce(f32[32]{0:T(128)S(1)} %multiply_reduce_fusion), channel_id=1, replica_groups=mesh['x'=4,'zh'=2,'zq'=2,'zn'=4,'y'=4,'core'=2] {'y','core'}, use_global_device_ids=true, to_apply=%region_6.7 | all-reduce | flops 32 | bytes 256 | tf_op jit(solution)/shard_map/psum | solution.py:67
  21.5 0.0 copy-done.3
  21.6 0.0 copy-done.4
  21.6 0.1 convert_reduce_fusion.1
  21.7 0.3 convolution_convert_fusion.3
  21.9 0.1 reshape.279
  22.0 0.1 broadcast_in_dim.46
  22.1 0.1 maximum_bitcast_fusion
  22.2 0.1 broadcast_in_dim.48
  22.3 45.3 %all_to_all.35 = bf16[64,4,896]{2,1,0:T(4,128)(2,1)S(1)} all-to-all(bf16[64,4,896]{2,1,0:T(4,128)(2,1)S(1)} %bitcast.41), channel_id=1, replica_groups=mesh['x'=4,'zh'=2,'zq'=2,'zn'=4,'y'=4,'core'=2] {'x','zh','zq','zn'}, dimensions={0} | all-to-all | bytes 917504 | tf_op jit(solution)/shard_map/all_to_all | solution.py:94
  67.6 0.1 slice.9
  67.8 0.1 reshape.281
  67.9 1.2 fusion.13
  69.1 0.1 select_reduce_fusion.1
  69.2 0.1 select_reduce_fusion
  69.3 0.1 add_select_fusion
  69.4 0.1 select_n.77
  69.6 0.2 convolution_convert_fusion.4
  69.8 18.4 %all_to_all.36 = bf16[4,120,768]{2,1,0:T(8,128)(2,1)S(1)} all-to-all(bf16[4,120,768]{2,1,0:T(8,128)(2,1)S(1)} %broadcast_in_dim.85), channel_id=1, replica_groups=mesh['x'=4,'zh'=2,'zq'=2,'zn'=4,'y'=4,'core'=2] {'zn'}, dimensions={0} | all-to-all | bytes 1474560 | tf_op jit(solution)/shard_map/all_to_all | solution.py:45
  88.3 0.0 copy-done
  88.3 1.9 %convolution_convert_fusion = bf16[480,1024]{1,0:T(8,128)(2,1)} fusion(bf16[480,768]{1,0:T(8,128)(2,1)S(1)} %bitcast.46, bf16[768,1024]{1,0:T(8,128)(2,1)S(1)} %copy-done), kind=kOutput, calls=%fused_computation.1 | convolution fusion | flops 755466240 | bytes 3293184 | tf_op jit(solution)/shard_map/dot_general | solution.py:114
  90.2 2.2 %reshape.283 = bf16[480,2,4,128]{3,2,1,0:T(4,128)(2,1)S(1)} reshape(bf16[480,1024]{1,0:T(8,128)(2,1)} %convolution_convert_fusion) | data formatting | bytes 1966080 | tf_op jit(solution)/shard_map/reshape | solution.py:116
  92.3 0.3 copy.83
  92.7 4.5 %all_to_all.37 = bf16[2,4,480,128]{3,1,2,0:T(4,128)(2,1)S(1)} all-to-all(bf16[2,4,480,128]{3,1,2,0:T(4,128)(2,1)S(1)} %bitcast.40), channel_id=1, replica_groups=mesh['x'=4,'zh'=2,'zq'=2,'zn'=4,'y'=4,'core'=2] {'core'}, dimensions={0} | all-to-all | bytes 1966080 | tf_op jit(solution)/shard_map/all_to_all | solution.py:50
  97.2 1.1 reduce_sum.125
  98.3 0.1 copy.65
  98.3 16.0 %all_to_all.38 = bf16[4,480,128]{2,1,0:T(8,128)(2,1)S(1)} all-to-all(bf16[4,480,128]{2,1,0:T(8,128)(2,1)S(1)} %copy.65), channel_id=1, replica_groups=mesh['x'=4,'zh'=2,'zq'=2,'zn'=4,'y'=4,'core'=2] {'y'}, dimensions={0} | all-to-all | bytes 983040 | tf_op jit(solution)/shard_map/all_to_all | solution.py:50
  114.3 0.1 convert_reduce_fusion
  114.4 0.1 multiply_convert_fusion
  114.5 0.0 copy-start.5
  114.5 0.1 broadcast_in_dim.86
  114.6 10.9 %all_to_all.39 = bf16[4,480,128]{2,1,0:T(8,128)(2,1)S(1)} all-to-all(bf16[4,480,128]{2,1,0:T(8,128)(2,1)S(1)} %broadcast_in_dim.86), channel_id=1, replica_groups=mesh['x'=4,'zh'=2,'zq'=2,'zn'=4,'y'=4,'core'=2] {'y'}, dimensions={0} | all-to-all | bytes 983040 | tf_op jit(solution)/shard_map/all_to_all | solution.py:45
  125.5 2.5 %all_gather.3 = bf16[8,480,128]{2,1,0:T(8,128)(2,1)S(1)} all-gather(bf16[4,480,128]{2,1,0:T(8,128)(2,1)S(1)} %all_to_all.39), channel_id=1, replica_groups=mesh['x'=4,'zh'=2,'zq'=2,'zn'=4,'y'=4,'core'=2] {'core'}, dimensions={0}, use_global_device_ids=true | all-gather | bytes 1474560 | tf_op jit(solution)/shard_map/all_gather | solution.py:120
  128.0 0.0 copy-done.5
  128.0 0.9 convolution_convert_fusion.1
  128.9 22.0 %all_to_all.40 = bf16[4,120,768]{2,1,0:T(8,128)(2,1)S(1)} all-to-all(bf16[4,120,768]{2,1,0:T(8,128)(2,1)S(1)} %bitcast.47), channel_id=1, replica_groups=mesh['x'=4,'zh'=2,'zq'=2,'zn'=4,'y'=4,'core'=2] {'zn'}, dimensions={0} | all-to-all | bytes 1474560 | tf_op jit(solution)/shard_map/all_to_all | solution.py:50
  150.9 0.1 reduce_sum.127
  151.0 0.3 convolution_convert_fusion.2
  151.3 0.1 reshape.286
  151.4 33.2 %all_to_all.41 = bf16[64,4,768]{2,1,0:T(4,128)(2,1)S(1)} all-to-all(bf16[64,4,768]{2,1,0:T(4,128)(2,1)S(1)} %reshape.286), channel_id=1, replica_groups=mesh['x'=4,'zh'=2,'zq'=2,'zn'=4,'y'=4,'core'=2] {'x','zh','zq','zn'}, dimensions={0} | all-to-all | bytes 786432 | tf_op jit(solution)/shard_map/all_to_all | solution.py:127
  184.7 0.1 reshape.289
  184.7 0.1 reduce_sum.128
  184.8 1.0 fusion.4
  (4 shorter events, 0.1 us)
Async XLA Ops:
  0.0 88.3 %copy-start = (bf16[768,1024]{1,0:T(8,128)(2,1)S(1)}, bf16[768,1024]{1,0:T(8,128)(2,1)}, u32[]{:S(2)}) copy-start(bf16[768,1024]{1,0:T(8,128)(2,1)} %param.18) | copy-start | bytes 4718596
  0.0 21.5 %copy-start.3 = (s32[32,2]{0,1:T(2,128)S(1)}, s32[32,2]{0,1:T(2,128)}, u32[]{:S(2)}) copy-start(s32[32,2]{0,1:T(2,128)} %param.16) | copy-start | bytes 772
  0.0 5.9 %copy-start.1 = (bf16[32,128,128]{2,1,0:T(8,128)(2,1)S(1)}, bf16[32,128,128]{2,1,0:T(8,128)(2,1)}, u32[]{:S(2)}) copy-start(bf16[32,128,128]{2,1,0:T(8,128)(2,1)} %param.13) | copy-start | bytes 3145732
  0.0 6.5 %copy-start.2 = (bf16[32,768]{1,0:T(8,128)(2,1)S(1)}, bf16[32,768]{1,0:T(8,128)(2,1)}, u32[]{:S(2)}) copy-start(bf16[32,768]{1,0:T(8,128)(2,1)} %param.10) | copy-start | bytes 147460
  0.0 21.5 %copy-start.4 = (f32[32,2]{0,1:T(2,128)S(1)}, f32[32,2]{0,1:T(2,128)}, u32[]{:S(2)}) copy-start(f32[32,2]{0,1:T(2,128)} %param.17) | copy-start | bytes 772
  114.5 13.5 %copy-start.5 = (bf16[1024,768]{1,0:T(8,128)(2,1)S(1)}, bf16[1024,768]{1,0:T(8,128)(2,1)}, u32[]{:S(2)}) copy-start(bf16[1024,768]{1,0:T(8,128)(2,1)} %param.19) | copy-start | bytes 4718596

commit v2 on v1

--- a/solution.py
+++ b/solution.py
@@ -1,6 +1,8 @@
 import jax
 import jax.numpy as jnp
 from jax import lax
+from jax.experimental import pallas as pl
+from jax.experimental.pallas import tpu as pltpu
 from jax.sharding import Mesh, PartitionSpec as P
 
 HEADS = 48
@@ -17,6 +19,9 @@
 CAPACITY = 384
 CLASS_ROWS = CAPACITY // CLASSES + BLOCKS * 6 // (4 * CLASSES)
 META = 128
+ROWS = CLASSES * CLASS_ROWS
+SQUARES = 16
+UNIT = 128
 
 NORM_EPSILON = 1e-05
 
@@ -51,6 +56,101 @@
     )
 
 
+def diagonal():
+    row = lax.broadcasted_iota(jnp.int32, (CLASS_ROWS, UNIT), 0)
+    return row == lax.broadcasted_iota(jnp.int32, (CLASS_ROWS, UNIT), 1)
+
+
+def leading_and_rest(sums):
+    leading = sums.astype(jnp.bfloat16)
+    return jnp.concatenate([leading, (sums - leading.astype(jnp.float32)).astype(jnp.bfloat16)], axis=0)
+
+
+def hidden_kernel(rows_ref, gain_ref, w_ref, out_ref, scaled_ref, squares_ref):
+    @pl.when(pl.program_id(0) == 0)
+    def _():
+        wide = rows_ref[...].astype(jnp.float32)
+        scaled_ref[...] = (wide * gain_ref[...].astype(jnp.float32)).astype(jnp.bfloat16)
+        sums = jnp.sum(wide * wide, axis=1, keepdims=True)
+        lines = [
+            jnp.sum(
+                jnp.where(diagonal(), sums[c * CLASS_ROWS : (c + 1) * CLASS_ROWS], 0.0),
+                axis=0,
+                keepdims=True,
+            )
+            for c in range(CLASSES)
+        ]
+        lines.append(jnp.zeros((SQUARES // 2 - CLASSES, UNIT), jnp.float32))
+        squares_ref[...] = leading_and_rest(jnp.concatenate(lines, axis=0))
+
+    sums = jnp.dot(scaled_ref[...], w_ref[...], preferred_element_type=jnp.float32)
+    for half in range(2):
+        out_ref[half, :ROWS] = sums[:, half * UNIT : (half + 1) * UNIT].astype(jnp.bfloat16)
+        out_ref[half, ROWS:] = squares_ref[...]
+
+
+def hidden_pieces(rows, norm_gain, w_in):
+    width, units = w_in.shape
+    return pl.pallas_call(
+        hidden_kernel,
+        grid=(units // (2 * UNIT),),
+        in_specs=[
+            pl.BlockSpec((ROWS, width), lambda i: (0, 0)),
+            pl.BlockSpec((1, width), lambda i: (0, 0)),
+            pl.BlockSpec((width, 2 * UNIT), lambda i: (0, i)),
+        ],
+        out_specs=pl.BlockSpec((2, ROWS + SQUARES, UNIT), lambda i: (i, 0, 0)),
+        out_shape=jax.ShapeDtypeStruct((units // UNIT, ROWS + SQUARES, UNIT), jnp.bfloat16),
+        scratch_shapes=[
+            pltpu.VMEM((ROWS, width), jnp.bfloat16),
+            pltpu.VMEM((SQUARES, UNIT), jnp.bfloat16),
+        ],
+        compiler_params=pltpu.CompilerParams(vmem_limit_bytes=32 << 20),
+        name="hidden_pieces",
+    )(rows, norm_gain.reshape(1, width), w_in)
+
+
+def core_kernel(in_ref, out_ref):
+    out_ref[:, :ROWS] = (
+        in_ref[0, :, :ROWS].astype(jnp.float32) + in_ref[1, :, :ROWS].astype(jnp.float32)
+    ).astype(jnp.bfloat16)
+    both = in_ref[0, 0, ROWS:].astype(jnp.float32) + in_ref[1, 0, ROWS:].astype(jnp.float32)
+    split = leading_and_rest(both[: SQUARES // 2] + both[SQUARES // 2 :])
+    for piece in range(out_ref.shape[0]):
+        out_ref[piece, ROWS:] = split
+
+
+def core_summed(pieces):
+    return pl.pallas_call(
+        core_kernel,
+        out_shape=jax.ShapeDtypeStruct(pieces.shape[1:], jnp.bfloat16),
+        compiler_params=pltpu.CompilerParams(vmem_limit_bytes=32 << 20),
+        name="core_summed",
+    )(pieces)
+
+
+def silu_kernel(in_ref, out_ref):
+    total = in_ref[0].astype(jnp.float32)
+    for piece in range(1, in_ref.shape[0]):
+        total = total + in_ref[piece].astype(jnp.float32)
+    squares = total[ROWS : ROWS + SQUARES // 2] + total[ROWS + SQUARES // 2 :]
+    for c in range(CLASSES):
+        own = jnp.sum(jnp.where(diagonal(), squares[c : c + 1], 0.0), axis=1, keepdims=True)
+        scaled = total[c * CLASS_ROWS : (c + 1) * CLASS_ROWS] * lax.rsqrt(own / D + NORM_EPSILON)
+        hidden = (scaled / (1.0 + jnp.exp(-scaled))).astype(jnp.bfloat16)
+        for piece in range(out_ref.shape[0]):
+            out_ref[piece, c * CLASS_ROWS : (c + 1) * CLASS_ROWS] = hidden
+
+
+def silu_copies(pieces):
+    return pl.pallas_call(
+        silu_kernel,
+        out_shape=jax.ShapeDtypeStruct((pieces.shape[0], ROWS, UNIT), jnp.bfloat16),
+        compiler_params=pltpu.CompilerParams(vmem_limit_bytes=32 << 20),
+        name="silu_copies",
+    )(pieces)
+
+
 def earlier_sum(counts):
     before = jnp.arange(BLOCKS)[:, None] > jnp.arange(BLOCKS)[None, :]
     return jnp.sum(jnp.where(before, counts[None, :], 0), axis=1)
@@ -64,12 +164,7 @@
     own_class = lax.axis_index("zn")
 
     summed = attend(residual, queries, keys, values, lengths)
-    square_sums = lax.psum(jnp.sum(summed * summed, axis=1), TENSOR)
-    normed = (
-        summed
-        * lax.rsqrt(square_sums[:, None] / D + NORM_EPSILON)
-        * norm_gain.astype(jnp.float32)[None, :]
-    ).astype(jnp.bfloat16)
+    unscaled = summed.astype(jnp.bfloat16)
 
     flat_ids = expert_ids.reshape(-1)
     pairs = flat_ids.shape[0]
@@ -86,7 +181,7 @@
         (flat_ids[None, :] == jnp.arange(EXPERTS, dtype=jnp.int32)[:, None]).astype(jnp.float32), axis=1
     ).astype(jnp.bfloat16)
 
-    packed = jnp.dot(pick_tokens, normed, preferred_element_type=jnp.float32).astype(jnp.bfloat16)
+    packed = jnp.dot(pick_tokens, unscaled, preferred_element_type=jnp.float32).astype(jnp.bfloat16)
     packed = packed.reshape(EXPERTS, 1, CLASSES, PER_CLASS, width)
     meta = jnp.broadcast_to(counts[:, None, None, None, None], (EXPERTS, 1, CLASSES, PER_CLASS, META))
     outgoing = jnp.concatenate([packed, meta], axis=-1)
@@ -109,17 +204,16 @@
         preferred_element_type=jnp.float32,
     ).astype(jnp.bfloat16)
 
-    rows = copies_to(class_rows, "zn", CLASSES).reshape(CLASSES * CLASS_ROWS, width)
-    total = rows.shape[0]
-    hidden_parts = jnp.dot(rows, w_in, preferred_element_type=jnp.float32).astype(jnp.bfloat16)
-    unit = hidden_parts.shape[1] // 8
-    pieces = jnp.moveaxis(hidden_parts.reshape(total, 2, 4, unit), 0, 2)
-    core_sums = summed_at_owner(pieces, "core").astype(jnp.bfloat16)
-    hidden = jax.nn.silu(summed_at_owner(core_sums.reshape(4, total, unit), "y")).astype(jnp.bfloat16)
-    gathered = copies_to(hidden, "y", 4)
+    rows = copies_to(class_rows, "zn", CLASSES).reshape(ROWS, width)
+    pieces = hidden_pieces(rows, norm_gain, w_in)
+    pieces = lax.all_to_all(
+        pieces.reshape(2, 4, ROWS + SQUARES, UNIT), "core", split_axis=0, concat_axis=0, tiled=True
+    )
+    pieces = lax.all_to_all(core_summed(pieces), "y", split_axis=0, concat_axis=0, tiled=True)
+    gathered = lax.all_to_all(silu_copies(pieces), "y", split_axis=0, concat_axis=0, tiled=True)
     gathered = lax.all_gather(gathered, "core", axis=0, tiled=True)
-    hidden_all = jnp.moveaxis(gathered, 0, 1).reshape(total, 8 * unit)
-    results = jnp.dot(hidden_all, w_out, preferred_element_type=jnp.float32).astype(jnp.bfloat16)
+    hidden = jnp.moveaxis(gathered, 0, 1).reshape(ROWS, 8 * UNIT)
+    results = jnp.dot(hidden, w_out, preferred_element_type=jnp.float32).astype(jnp.bfloat16)
 
     class_out = summed_at_owner(results.reshape(CLASSES, CLASS_ROWS, width), "zn").astype(jnp.bfloat16)
     spread = (spot[:, None] == jnp.arange(CLASS_ROWS, dtype=jnp.int32)[None, :]).astype(jnp.bfloat16)

time: 186 us -> 173 us (0.930)
  blocking collectives: 168 us -> 135 us
  waiting for transfers between devices: 0 us -> 17.5 us
  starting transfers between devices: 0 us -> 3.49 us
  Pallas kernels: 0 us -> 2.35 us
  other arithmetic: 5.19 us -> 3.17 us
  matrix products: 6.99 us -> 5.1 us
    all_to_all x3 -> x1, blocking collectives: 42.6 us -> 22.6 us  [summed_at_owner(): lax.all_to_all(pieces, axis, split_axis=0, concat_axis=0, tiled=True)]
    all_to_all x0 -> x1, waiting for transfers between devices: none -> 17.5 us  [copies_to(): return lax.all_to_all(copies, axis, split_axis=0, concat_axis=0, tiled=True)]
    psum x1 -> x0, blocking collectives: 14.9 us -> none  [shards(): square_sums = lax.psum(jnp.sum(summed * summed, axis=1), TENSOR)]
    all_to_all x0 -> x1, starting transfers between devices: none -> 3.49 us  [copies_to(): return lax.all_to_all(copies, axis, split_axis=0, concat_axis=0, tiled=True)]
    reshape x2 -> x1, local copies, waits for them, and re-layouts: 2.5 us -> 0.01 us  [hidden_pieces(): norm_gain.reshape(1, width)]
    pallas_call x0 -> x3, Pallas kernels: none -> 2.35 us  [the longest x1 2.03 us: hidden_pieces(): pl.pallas_call(hidden_kernel, grid=(units // (2 * UNIT),), in_specs=[pl.B...]
    all_to_all x1, blocking collectives: 45.3 us -> 47.5 us  [shards(): lax.all_to_all(outgoing.reshape(BLOCKS, PER_CLASS, width + META), DP, spl...]
    dot_general x3 -> x2, matrix products: 3.07 us -> 1.17 us  [the longest x1 0.92 us: shards(): jnp.dot(hidden, w_out, preferred_element_type=jnp.float32)]
  transfers between devices with their start and end apart: 0 -> 1, of which waited for: 0 -> 1; matrix products, arithmetic and copies ran while one was open for 0% -> 0% of each run, Pallas kernels for 0% -> 0%
where the time goes in v2:
time: 173 us; the launch traced here: 172 us
  blocking collectives  135 us (78%)
  waiting for transfers between devices  17.5 us (10%)
  local copies, waits for them, and re-layouts  5.16 us (3%)
  matrix products  5.1 us (3%)
  starting transfers between devices  3.49 us (2%)
  other arithmetic  3.17 us (2%)
  Pallas kernels  2.35 us (1%)
    all_to_all x1, blocking collectives, shards(): lax.all_to_all(outgoing.reshape(BLOCKS, PER_CLASS, width + META), DP, spl...  47.5 us
    all_to_all x1, blocking collectives, shards(): lax.all_to_all(returned.reshape(BLOCKS, PER_CLASS, width), DP, split_axis...  33.5 us
    all_to_all x1, blocking collectives, summed_at_owner(): lax.all_to_all(pieces, axis, split_axis=0, concat_axis=0, tiled=True)  22.6 us
    all_to_all x1, waiting for transfers between devices, copies_to(): return lax.all_to_all(copies, axis, split_axis=0, concat_axis=0, tiled=True)  17.5 us
    all_to_all x1, blocking collectives, shards(): lax.all_to_all(core_summed(pieces), 'y', split_axis=0, concat_axis=0, til...  13.9 us
    all_to_all x1, blocking collectives, shards(): lax.all_to_all(silu_copies(pieces), 'y', split_axis=0, concat_axis=0, til...  10.7 us
    all_to_all x1, blocking collectives, shards(): lax.all_to_all(pieces.reshape(2, 4, ROWS + SQUARES, UNIT), 'core', split_...  4.53 us
    all_to_all x1, starting transfers between devices, copies_to(): return lax.all_to_all(copies, axis, split_axis=0, concat_axis=0, tiled=True)  3.49 us
  transfers between devices with their start and end apart: 1, of which 1 were waited for; matrix products, arithmetic and copies ran while one was open for 0% of the time, Pallas kernels for 0%

profile of v2, /device:TPU:6, one launch (start us, length us, event | category | flops | bytes accessed | tf_op | source)
XLA Modules:
  0.0 172.2 jit_solution(14296676682650491614)
XLA Ops:
  0.0 0.0 copy-start
  0.0 0.0 copy-start.4
  0.0 0.0 copy-start.6
  0.0 0.0 copy-start.2
  0.0 0.0 copy-start.3
  0.0 0.9 copy.44
  0.9 0.1 eq.72
  1.1 0.2 convert_reduce_fusion.1
  1.2 0.1 convert_reduce_fusion.2
  1.4 0.7 iota_compare_fusion.7
  2.1 0.1 reduce_sum.88
  2.2 0.1 copy.45
  2.3 0.9 reshape.275
  3.2 1.9 %fusion.3 = f32[32,6,128]{2,1,0:T(8,128)S(1)} fusion(bf16[32,6,128]{2,1,0:T(8,128)(2,1)S(1)} %reshape.275, bf16[32,128,128]{2,1,0:T(8,128)(2,1)} %param.12, pred[32,128]{1,0:T(8,128)(4,1)S(1)} %iota_compare_fusion.7), kind=kOutput, calls=%fused_computation.8 | convolution fusion | flops 6340608 | bytes 1200128 | tf_op jit(solution)/shard_map/tjd,tld->tjl/dot_general | solution.py:36
  5.0 0.2 fusion.21
  5.3 0.0 copy-done.4
  5.3 0.0 copy-done.6
  5.3 0.1 convert_reduce_fusion
  5.4 0.0 copy-done.2
  5.4 0.6 fusion.7
  6.0 0.0 copy-done.3
  6.0 0.2 convolution_convert_fusion.2
  6.2 0.1 reshape.277
  6.3 0.1 broadcast_in_dim.44
  6.4 0.1 maximum_bitcast_fusion
  6.5 0.1 broadcast_in_dim.46
  6.6 47.5 %all_to_all.35 = bf16[64,4,896]{2,1,0:T(4,128)(2,1)S(1)} all-to-all(bf16[64,4,896]{2,1,0:T(4,128)(2,1)S(1)} %bitcast.36), channel_id=1, replica_groups=mesh['x'=4,'zh'=2,'zq'=2,'zn'=4,'y'=4,'core'=2] {'x','zh','zq','zn'}, dimensions={0} | all-to-all | bytes 917504 | tf_op jit(solution)/shard_map/all_to_all | solution.py:189
  54.1 0.1 slice.9
  54.2 0.1 reshape.279
  54.3 0.0 copy-start.5
  54.3 1.2 fusion.12
  55.5 0.1 select_reduce_fusion.1
  55.7 0.1 select_reduce_fusion
  55.8 0.1 add_select_fusion
  55.9 0.1 select_n.77
  56.0 0.2 convolution_convert_fusion.3
  56.2 0.9 broadcast_in_dim.80
  57.2 3.5 %all-to-all-start.1 = ((bf16[4,120,768]{2,1,0:T(8,128)(2,1)}), bf16[4,120,768]{2,1,0:T(8,128)(2,1)S(1)}, u32[]{:S(2)}, u32[]{:S(2)}) async-start(bf16[4,120,768]{2,1,0:T(8,128)(2,1)} %broadcast_in_dim.80), calls=%async_computation.1 | async-start | bytes 1474560 | tf_op jit(solution)/shard_map/all_to_all | solution.py:50
  60.7 0.0 copy-done.5
  60.7 17.5 %all-to-all-done.1 = bf16[4,120,768]{2,1,0:T(8,128)(2,1)S(1)} async-done(((bf16[4,120,768]{2,1,0:T(8,128)(2,1)}), bf16[4,120,768]{2,1,0:T(8,128)(2,1)S(1)}, u32[]{:S(2)}, u32[]{:S(2)}) %all-to-all-start.1) | async-done | bytes 737312 | tf_op jit(solution)/shard_map/all_to_all | solution.py:50
  78.2 0.0 copy-start.1
  78.2 1.4 copy-done.1
  79.6 2.0 %hidden_pieces.1 = bf16[8,496,128]{2,1,0:T(8,128)(2,1)S(1)} custom-call(bf16[480,768]{1,0:T(8,128)(2,1)S(1)} %bitcast.35, bf16[1,768]{1,0:T(2,128)(2,1)S(1)} %reshape.281.gain_ref, bf16[768,1024]{1,0:T(8,128)(2,1)S(1)} %copy-done.1), custom_call_target="tpu_custom_call" | custom-call | tf_op jit(solution)/shard_map/hidden_pieces/pallas_call | solution.py:94
  81.6 4.5 %all_to_all.36.in_ref = bf16[2,4,496,128]{3,2,1,0:T(8,128)(2,1)S(1)} all-to-all(bf16[2,4,496,128]{3,2,1,0:T(8,128)(2,1)S(1)} %bitcast.34), channel_id=1, replica_groups=mesh['x'=4,'zh'=2,'zq'=2,'zn'=4,'y'=4,'core'=2] {'core'}, dimensions={0} | all-to-all | bytes 2031616 | tf_op jit(solution)/shard_map/all_to_all | solution.py:209
  86.2 0.1 core_summed.1
  86.3 13.9 %all_to_all.37.in_ref = bf16[4,496,128]{2,1,0:T(8,128)(2,1)S(1)} all-to-all(bf16[4,496,128]{2,1,0:T(8,128)(2,1)S(1)} %core_summed.1), channel_id=1, replica_groups=mesh['x'=4,'zh'=2,'zq'=2,'zn'=4,'y'=4,'core'=2] {'y'}, dimensions={0} | all-to-all | bytes 1015808 | tf_op jit(solution)/shard_map/all_to_all | solution.py:212
  100.1 0.2 silu_copies.1
  100.3 10.7 %all_to_all.38 = bf16[4,480,128]{2,1,0:T(8,128)(2,1)S(1)} all-to-all(bf16[4,480,128]{2,1,0:T(8,128)(2,1)S(1)} %silu_copies.1), channel_id=1, replica_groups=mesh['x'=4,'zh'=2,'zq'=2,'zn'=4,'y'=4,'core'=2] {'y'}, dimensions={0} | all-to-all | bytes 983040 | tf_op jit(solution)/shard_map/all_to_all | solution.py:213
  111.0 2.5 %all_gather.3 = bf16[8,480,128]{2,1,0:T(8,128)(2,1)S(1)} all-gather(bf16[4,480,128]{2,1,0:T(8,128)(2,1)S(1)} %all_to_all.38), channel_id=1, replica_groups=mesh['x'=4,'zh'=2,'zq'=2,'zn'=4,'y'=4,'core'=2] {'core'}, dimensions={0}, use_global_device_ids=true | all-gather | bytes 1474560 | tf_op jit(solution)/shard_map/all_gather | solution.py:214
  113.5 0.0 copy-done
  113.5 0.9 convolution_convert_fusion
  114.4 22.6 %all_to_all.39 = bf16[4,120,768]{2,1,0:T(8,128)(2,1)S(1)} all-to-all(bf16[4,120,768]{2,1,0:T(8,128)(2,1)S(1)} %bitcast.40), channel_id=1, replica_groups=mesh['x'=4,'zh'=2,'zq'=2,'zn'=4,'y'=4,'core'=2] {'zn'}, dimensions={0} | all-to-all | bytes 1474560 | tf_op jit(solution)/shard_map/all_to_all | solution.py:55
  137.0 0.1 reduce_sum.94
  137.2 0.3 convolution_convert_fusion.1
  137.5 0.1 reshape.285
  137.6 33.5 %all_to_all.40 = bf16[64,4,768]{2,1,0:T(4,128)(2,1)S(1)} all-to-all(bf16[64,4,768]{2,1,0:T(4,128)(2,1)S(1)} %reshape.285), channel_id=1, replica_groups=mesh['x'=4,'zh'=2,'zq'=2,'zn'=4,'y'=4,'core'=2] {'x','zh','zq','zn'}, dimensions={0} | all-to-all | bytes 786432 | tf_op jit(solution)/shard_map/all_to_all | solution.py:221
  171.1 0.1 reshape.288
  171.1 0.1 reduce_sum.95
  171.2 1.0 fusion.4
  (3 shorter events, 0.0 us)
Async XLA Ops:
  0.0 113.5 %copy-start = (bf16[1024,768]{1,0:T(8,128)(2,1)S(1)}, bf16[1024,768]{1,0:T(8,128)(2,1)}, u32[]{:S(2)}) copy-start(bf16[1024,768]{1,0:T(8,128)(2,1)} %param.19) | copy-start | bytes 4718596
  0.0 5.3 %copy-start.4 = (s32[32,2]{0,1:T(2,128)S(1)}, s32[32,2]{0,1:T(2,128)}, u32[]{:S(2)}) copy-start(s32[32,2]{0,1:T(2,128)} %param.16) | copy-start | bytes 772
  0.0 5.3 %copy-start.6 = (f32[32,2]{0,1:T(2,128)S(1)}, f32[32,2]{0,1:T(2,128)}, u32[]{:S(2)}) copy-start(f32[32,2]{0,1:T(2,128)} %param.17) | copy-start | bytes 772
  0.0 5.4 %copy-start.2 = (bf16[32,128,128]{2,1,0:T(8,128)(2,1)S(1)}, bf16[32,128,128]{2,1,0:T(8,128)(2,1)}, u32[]{:S(2)}) copy-start(bf16[32,128,128]{2,1,0:T(8,128)(2,1)} %param.13) | copy-start | bytes 3145732
  0.0 6.0 %copy-start.3 = (bf16[32,768]{1,0:T(8,128)(2,1)S(1)}, bf16[32,768]{1,0:T(8,128)(2,1)}, u32[]{:S(2)}) copy-start(bf16[32,768]{1,0:T(8,128)(2,1)} %param.10) | copy-start | bytes 147460
  54.3 6.3 %copy-start.5 = (bf16[768]{0:T(1024)(128)(2,1)S(1)}, bf16[768]{0:T(1024)(128)(2,1)}, u32[]{:S(2)}) copy-start(bf16[768]{0:T(1024)(128)(2,1)} %param.15) | copy-start | bytes 4612
  57.2 21.0 %all-to-all-start.1 = ((bf16[4,120,768]{2,1,0:T(8,128)(2,1)}), bf16[4,120,768]{2,1,0:T(8,128)(2,1)S(1)}, u32[]{:S(2)}, u32[]{:S(2)}) async-start(bf16[4,120,768]{2,1,0:T(8,128)(2,1)} %broadcast_in_dim.80), calls=%async_computation.1 | async-start | bytes 1474560 | tf_op jit(solution)/shard_map/all_to_all | solution.py:50
  78.2 1.4 copy-start.1

commit v3 on v2

--- a/solution.py
+++ b/solution.py
@@ -45,11 +45,6 @@
     return residual.astype(jnp.float32) + attended.reshape(tokens, width)
 
 
-def copies_to(value, axis, peers):
-    copies = jnp.broadcast_to(value, (peers, *value.shape))
-    return lax.all_to_all(copies, axis, split_axis=0, concat_axis=0, tiled=True)
-
-
 def summed_at_owner(pieces, axis):
     return jnp.sum(
         lax.all_to_all(pieces, axis, split_axis=0, concat_axis=0, tiled=True).astype(jnp.float32), axis=0
@@ -66,8 +61,10 @@
     return jnp.concatenate([leading, (sums - leading.astype(jnp.float32)).astype(jnp.bfloat16)], axis=0)
 
 
-def hidden_kernel(rows_ref, gain_ref, w_ref, out_ref, scaled_ref, squares_ref):
-    @pl.when(pl.program_id(0) == 0)
+def hidden_kernel(core_ref, rows_ref, gain_ref, w_ref, send_ref, keep_ref, scaled_ref, squares_ref):
+    step = pl.program_id(0)
+
+    @pl.when(step == 0)
     def _():
         wide = rows_ref[...].astype(jnp.float32)
         scaled_ref[...] = (wide * gain_ref[...].astype(jnp.float32)).astype(jnp.bfloat16)
@@ -84,49 +81,67 @@
         squares_ref[...] = leading_and_rest(jnp.concatenate(lines, axis=0))
 
     sums = jnp.dot(scaled_ref[...], w_ref[...], preferred_element_type=jnp.float32)
-    for half in range(2):
-        out_ref[half, :ROWS] = sums[:, half * UNIT : (half + 1) * UNIT].astype(jnp.bfloat16)
-        out_ref[half, ROWS:] = squares_ref[...]
-
-
-def hidden_pieces(rows, norm_gain, w_in):
+
+    def write(out_ref):
+        for half in range(2):
+            out_ref[half, :ROWS] = sums[:, half * UNIT : (half + 1) * UNIT].astype(jnp.bfloat16)
+            out_ref[half, ROWS:] = squares_ref[...]
+
+    @pl.when(step < 2)
+    def _():
+        write(send_ref)
+
+    @pl.when(step >= 2)
+    def _():
+        write(keep_ref)
+
+
+def hidden_pieces(rows, norm_gain, w_in, core):
     width, units = w_in.shape
+    half = jax.ShapeDtypeStruct((units // (2 * UNIT), ROWS + SQUARES, UNIT), jnp.bfloat16)
+    block = (2, ROWS + SQUARES, UNIT)
     return pl.pallas_call(
         hidden_kernel,
-        grid=(units // (2 * UNIT),),
-        in_specs=[
-            pl.BlockSpec((ROWS, width), lambda i: (0, 0)),
-            pl.BlockSpec((1, width), lambda i: (0, 0)),
-            pl.BlockSpec((width, 2 * UNIT), lambda i: (0, i)),
-        ],
-        out_specs=pl.BlockSpec((2, ROWS + SQUARES, UNIT), lambda i: (i, 0, 0)),
-        out_shape=jax.ShapeDtypeStruct((units // UNIT, ROWS + SQUARES, UNIT), jnp.bfloat16),
-        scratch_shapes=[
-            pltpu.VMEM((ROWS, width), jnp.bfloat16),
-            pltpu.VMEM((SQUARES, UNIT), jnp.bfloat16),
-        ],
+        grid_spec=pltpu.PrefetchScalarGridSpec(
+            num_scalar_prefetch=1,
+            grid=(4,),
+            in_specs=[
+                pl.BlockSpec((ROWS, width), lambda i, c: (0, 0)),
+                pl.BlockSpec((1, width), lambda i, c: (0, 0)),
+                pl.BlockSpec((width, 2 * UNIT), lambda i, c: (0, (i + 2 - 2 * c[0]) % 4)),
+            ],
+            out_specs=[
+                pl.BlockSpec(block, lambda i, c: (jnp.minimum(i, 1), 0, 0)),
+                pl.BlockSpec(block, lambda i, c: (jnp.maximum(i - 2, 0), 0, 0)),
+            ],
+            scratch_shapes=[
+                pltpu.VMEM((ROWS, width), jnp.bfloat16),
+                pltpu.VMEM((SQUARES, UNIT), jnp.bfloat16),
+            ],
+        ),
+        out_shape=[half, half],
         compiler_params=pltpu.CompilerParams(vmem_limit_bytes=32 << 20),
         name="hidden_pieces",
-    )(rows, norm_gain.reshape(1, width), w_in)
-
-
-def core_kernel(in_ref, out_ref):
+    )(core.reshape(1), rows, norm_gain.reshape(1, width), pltpu.with_memory_space_constraint(w_in, pltpu.HBM))
+
+
+def core_kernel(own_ref, other_ref, out_ref):
     out_ref[:, :ROWS] = (
-        in_ref[0, :, :ROWS].astype(jnp.float32) + in_ref[1, :, :ROWS].astype(jnp.float32)
-    ).astype(jnp.bfloat16)
-    both = in_ref[0, 0, ROWS:].astype(jnp.float32) + in_ref[1, 0, ROWS:].astype(jnp.float32)
+        own_ref[:, :ROWS].astype(jnp.float32) + other_ref[:, :ROWS].astype(jnp.float32)
+    ).astype(jnp.bfloat16)
+    both = own_ref[0, ROWS:].astype(jnp.float32) + other_ref[0, ROWS:].astype(jnp.float32)
     split = leading_and_rest(both[: SQUARES // 2] + both[SQUARES // 2 :])
     for piece in range(out_ref.shape[0]):
         out_ref[piece, ROWS:] = split
 
 
-def core_summed(pieces):
+def core_summed(own, other):
     return pl.pallas_call(
         core_kernel,
-        out_shape=jax.ShapeDtypeStruct(pieces.shape[1:], jnp.bfloat16),
+        out_shape=jax.ShapeDtypeStruct(own.shape, jnp.bfloat16),
         compiler_params=pltpu.CompilerParams(vmem_limit_bytes=32 << 20),
         name="core_summed",
-    )(pieces)
+    )(own, other)
 
 
 def silu_kernel(in_ref, out_ref):
@@ -151,9 +166,51 @@
     )(pieces)
 
 
-def earlier_sum(counts):
-    before = jnp.arange(BLOCKS)[:, None] > jnp.arange(BLOCKS)[None, :]
-    return jnp.sum(jnp.where(before, counts[None, :], 0), axis=1)
+def compact_kernel(class_ref, received_ref, rows_ref, place_ref):
+    slots = received_ref.shape[0]
+    width = rows_ref.shape[1]
+    own_class = class_ref[0]
+    row = lax.broadcasted_iota(jnp.int32, (slots, slots), 0)
+    column = lax.broadcasted_iota(jnp.int32, (slots, slots), 1)
+    earlier = (column // PER_CLASS < row // PER_CLASS) & (column % PER_CLASS == 0)
+    earlier = earlier.astype(jnp.float32).astype(jnp.bfloat16)
+
+    def earlier_sum(counts):
+        return jnp.dot(earlier, counts, preferred_element_type=jnp.float32).astype(jnp.int32)
+
+    counts = received_ref[:, width:]
+    named = counts.astype(jnp.float32).astype(jnp.int32)
+    kept = jnp.clip(CAPACITY - earlier_sum(counts), 0, named)
+    line = lax.broadcasted_iota(jnp.int32, named.shape, 0)
+    block, place = line // PER_CLASS, line % PER_CLASS
+    shift = (own_class + BLOCKS - block) % CLASSES
+    in_class = (kept - shift + CLASSES - 1) // CLASSES
+    first = earlier_sum(in_class.astype(jnp.float32).astype(jnp.bfloat16))
+    spot = jnp.where(place < in_class, first + place, -1)
+    chosen = spot == lax.broadcasted_iota(jnp.int32, named.shape, 1)
+    chosen = chosen.astype(jnp.float32).astype(jnp.bfloat16)
+    place_ref[...] = chosen
+    rows = lax.dot_general(
+        chosen, received_ref[:, :width], (((0,), (0,)), ((), ())), preferred_element_type=jnp.float32
+    )
+    rows_ref[...] = rows[: rows_ref.shape[0]].astype(jnp.bfloat16)
+
+
+def compacted(received, own_class):
+    slots, wide = received.shape
+    return pl.pallas_call(
+        compact_kernel,
+        in_specs=[
+            pl.BlockSpec(memory_space=pltpu.SMEM),
+            pl.BlockSpec(memory_space=pltpu.VMEM),
+        ],
+        out_shape=[
+            jax.ShapeDtypeStruct((CLASS_ROWS, wide - META), jnp.bfloat16),
+            jax.ShapeDtypeStruct((slots, META), jnp.bfloat16),
+        ],
+        compiler_params=pltpu.CompilerParams(vmem_limit_bytes=32 << 20),
+        name="compacted",
+    )(own_class.reshape(1), received)
 
 
 def shards(
@@ -190,34 +247,20 @@
         outgoing.reshape(BLOCKS, PER_CLASS, width + META), DP, split_axis=0, concat_axis=0, tiled=True
     )
 
-    named = received[:, 0, width].astype(jnp.int32)
-    kept = jnp.clip(CAPACITY - earlier_sum(named), 0, named)
-    shift = (own_class - jnp.arange(BLOCKS, dtype=jnp.int32)) % CLASSES
-    in_class = (kept - shift + CLASSES - 1) // CLASSES
-    first = earlier_sum(in_class)
-    place = jnp.arange(PER_CLASS, dtype=jnp.int32)[None, :]
-    spot = jnp.where(place < in_class[:, None], first[:, None] + place, -1).reshape(-1)
-    compact = (spot[None, :] == jnp.arange(CLASS_ROWS, dtype=jnp.int32)[:, None]).astype(jnp.bfloat16)
-    class_rows = jnp.dot(
-        compact,
-        received[:, :, :width].reshape(BLOCKS * PER_CLASS, width),
-        preferred_element_type=jnp.float32,
-    ).astype(jnp.bfloat16)
-
-    rows = copies_to(class_rows, "zn", CLASSES).reshape(ROWS, width)
-    pieces = hidden_pieces(rows, norm_gain, w_in)
-    pieces = lax.all_to_all(
-        pieces.reshape(2, 4, ROWS + SQUARES, UNIT), "core", split_axis=0, concat_axis=0, tiled=True
-    )
-    pieces = lax.all_to_all(core_summed(pieces), "y", split_axis=0, concat_axis=0, tiled=True)
+    class_rows, chosen = compacted(received.reshape(BLOCKS * PER_CLASS, width + META), own_class)
+    rows = lax.all_gather(class_rows, "zn", axis=0, tiled=True)
+    send, own = hidden_pieces(rows, norm_gain, w_in, lax.axis_index("core"))
+    other = lax.ppermute(send, "core", ((0, 1), (1, 0)))
+    pieces = lax.all_to_all(core_summed(own, other), "y", split_axis=0, concat_axis=0, tiled=True)
     gathered = lax.all_to_all(silu_copies(pieces), "y", split_axis=0, concat_axis=0, tiled=True)
     gathered = lax.all_gather(gathered, "core", axis=0, tiled=True)
     hidden = jnp.moveaxis(gathered, 0, 1).reshape(ROWS, 8 * UNIT)
     results = jnp.dot(hidden, w_out, preferred_element_type=jnp.float32).astype(jnp.bfloat16)
 
     class_out = summed_at_owner(results.reshape(CLASSES, CLASS_ROWS, width), "zn").astype(jnp.bfloat16)
-    spread = (spot[:, None] == jnp.arange(CLASS_ROWS, dtype=jnp.int32)[None, :]).astype(jnp.bfloat16)
-    returned = jnp.dot(spread, class_out, preferred_element_type=jnp.float32).astype(jnp.bfloat16)
+    returned = jnp.dot(
+        chosen[:, :CLASS_ROWS], class_out, preferred_element_type=jnp.float32
+    ).astype(jnp.bfloat16)
     combined = lax.all_to_all(
         returned.reshape(BLOCKS, PER_CLASS, width), DP, split_axis=0, concat_axis=0, tiled=True
     )

time: 173 us -> 166 us (0.960)
  blocking collectives: 135 us -> 99.7 us
  starting transfers between devices: 3.49 us -> 20.7 us
  waiting for transfers between devices: 17.5 us -> 30.7 us
  Pallas kernels: 2.35 us -> 4.57 us
  local copies, waits for them, and re-layouts: 5.16 us -> 3.38 us
    all_to_all x3 -> x1, blocking collectives: 65.8 us -> 13.9 us  [shards(): lax.all_to_all(core_summed(own, other), 'y', split_axis=0, concat_axis=0,...]
    all_gather x0 -> x1, blocking collectives: none -> 17.4 us  [shards(): rows = lax.all_gather(class_rows, 'zn', axis=0, tiled=True)]
    all_to_all x1, starting transfers between devices: 3.49 us -> 18.8 us  [shards(): lax.all_to_all(outgoing.reshape(BLOCKS, PER_CLASS, width + META), DP, spl...]
    all_to_all x1, waiting for transfers between devices: 17.5 us -> 28.8 us  [shards(): lax.all_to_all(outgoing.reshape(BLOCKS, PER_CLASS, width + META), DP, spl...]
    pallas_call x2 -> x3, Pallas kernels: 2.16 us -> 4.37 us  [the longest x1 3.53 us: hidden_pieces(): pl.pallas_call(hidden_kernel, grid_spec=pltpu.PrefetchScalarGridSpec(num_...]
    ppermute x0 -> x1, starting transfers between devices: none -> 1.92 us  [shards(): other = lax.ppermute(send, 'core', ((0, 1), (1, 0)))]
    ppermute x0 -> x1, waiting for transfers between devices: none -> 1.85 us  [shards(): other = lax.ppermute(send, 'core', ((0, 1), (1, 0)))]
  transfers between devices with their start and end apart: 1 -> 2, of which waited for: 1 -> 2; matrix products, arithmetic and copies ran while one was open for 0% -> 0% of each run, Pallas kernels for 0% -> 0%
where the time goes in v3:
time: 166 us
  blocking collectives  99.7 us (60%)
  waiting for transfers between devices  30.7 us (18%)
  starting transfers between devices  20.7 us (12%)
  matrix products  4.83 us (3%)
  Pallas kernels  4.57 us (3%)
  local copies, waits for them, and re-layouts  3.38 us (2%)
    all_to_all x1, blocking collectives, shards(): lax.all_to_all(returned.reshape(BLOCKS, PER_CLASS, width), DP, split_axis...  33.2 us
    all_to_all x1, waiting for transfers between devices, shards(): lax.all_to_all(outgoing.reshape(BLOCKS, PER_CLASS, width + META), DP, spl...  28.8 us
    all_to_all x1, blocking collectives, summed_at_owner(): lax.all_to_all(pieces, axis, split_axis=0, concat_axis=0, tiled=True)  22.1 us
    all_to_all x1, starting transfers between devices, shards(): lax.all_to_all(outgoing.reshape(BLOCKS, PER_CLASS, width + META), DP, spl...  18.8 us
    all_gather x1, blocking collectives, shards(): rows = lax.all_gather(class_rows, 'zn', axis=0, tiled=True)  17.4 us
    all_to_all x1, blocking collectives, shards(): lax.all_to_all(core_summed(own, other), 'y', split_axis=0, concat_axis=0,...  13.9 us
    all_to_all x1, blocking collectives, shards(): lax.all_to_all(silu_copies(pieces), 'y', split_axis=0, concat_axis=0, til...  10.7 us
    pallas_call x1, Pallas kernels, hidden_pieces(): pl.pallas_call(hidden_kernel, grid_spec=pltpu.PrefetchScalarGridSpec(num_...  3.53 us
  transfers between devices with their start and end apart: 2, of which 2 were waited for; matrix products, arithmetic and copies ran while one was open for 0% of the time, Pallas kernels for 0%

profile of v3, /device:TPU:6, one launch (start us, length us, event | category | flops | bytes accessed | tf_op | source)
XLA Modules:
  0.0 165.7 jit_solution(14393286682231959827)
XLA Ops:
  0.0 0.0 copy-start
  0.0 0.0 copy-start.3
  0.0 0.0 copy-start.5
  0.0 0.0 copy-start.1
  0.0 0.0 copy-start.2
  0.0 0.9 copy.36
  0.9 0.1 eq.45
  1.1 0.2 convert_reduce_fusion.1
  1.2 0.1 convert_reduce_fusion.2
  1.4 0.7 iota_compare_fusion.2
  2.1 0.1 reduce_sum.70
  2.2 0.1 copy.37
  2.3 0.9 reshape.127
  3.2 1.9 %fusion.3 = f32[32,6,128]{2,1,0:T(8,128)S(1)} fusion(bf16[32,6,128]{2,1,0:T(8,128)(2,1)S(1)} %reshape.127, bf16[32,128,128]{2,1,0:T(8,128)(2,1)} %param.12, pred[32,128]{1,0:T(8,128)(4,1)S(1)} %iota_compare_fusion.2), kind=kOutput, calls=%fused_computation.7 | convolution fusion | flops 6340608 | bytes 1200128 | tf_op jit(solution)/shard_map/tjd,tld->tjl/dot_general | solution.py:36
  5.0 0.2 fusion.17
  5.3 0.0 copy-done.3
  5.3 0.0 copy-done.5
  5.3 0.1 convert_reduce_fusion
  5.4 0.0 copy-done.1
  5.4 0.6 fusion.7
  6.0 0.0 copy-start.4
  6.0 0.0 copy-done.2
  6.0 0.3 convolution_convert_fusion.2
  6.2 0.1 reshape.130
  6.3 0.1 broadcast_in_dim.20
  6.4 0.1 maximum_bitcast_fusion
  6.5 0.9 broadcast_in_dim.22
  7.4 18.8 %all-to-all-start = ((bf16[64,4,896]{2,1,0:T(4,128)(2,1)}), bf16[64,4,896]{2,1,0:T(4,128)(2,1)S(1)}, u32[]{:S(2)}, u32[]{:S(2)}) async-start(bf16[64,4,896]{2,1,0:T(4,128)(2,1)} %bitcast.2), calls=%async_computation | async-start | bytes 917504 | tf_op jit(solution)/shard_map/all_to_all | solution.py:246
  26.2 0.0 copy-done.4
  26.2 28.8 %all-to-all-done = bf16[64,4,896]{2,1,0:T(4,128)(2,1)S(1)} async-done(((bf16[64,4,896]{2,1,0:T(4,128)(2,1)}), bf16[64,4,896]{2,1,0:T(4,128)(2,1)S(1)}, u32[]{:S(2)}, u32[]{:S(2)}) %all-to-all-start) | async-done | bytes 458784 | tf_op jit(solution)/shard_map/all_to_all | solution.py:246
  55.0 0.1 reshape.132.received_ref
  55.2 0.7 compacted.1
  55.9 17.4 %all_gather.6.rows_ref = bf16[480,768]{1,0:T(8,128)(2,1)S(1)} all-gather(bf16[120,768]{1,0:T(8,128)(2,1)S(1)} %get-tuple-element.10), channel_id=1, replica_groups=mesh['x'=4,'zh'=2,'zq'=2,'zn'=4,'y'=4,'core'=2] {'zn'}, dimensions={0}, use_global_device_ids=true | all-gather | bytes 921600 | tf_op jit(solution)/shard_map/all_gather | solution.py:251
  73.3 3.5 %hidden_pieces.1 = (bf16[4,496,128]{2,1,0:T(8,128)(2,1)S(1)}, bf16[4,496,128]{2,1,0:T(8,128)(2,1)S(1)}) custom-call(s32[1]{0:T(128)} %bitcast.3.core_ref, bf16[480,768]{1,0:T(8,128)(2,1)S(1)} %all_gather.6.rows_ref, bf16[1,768]{1,0:T(2,128)(2,1)S(1)} %reshape.134.gain_ref, bf16[768,1024]{1,0:T(8,128)(2,1)} %w_ref.1), custom_call_target="tpu_custom_call" | custom-call | tf_op jit(solution)/shard_map/hidden_pieces/pallas_call | solution.py:103
  76.8 1.9 %collective-permute-start = (bf16[4,496,128]{2,1,0:T(8,128)(2,1)S(1)}, bf16[4,496,128]{2,1,0:T(8,128)(2,1)S(1)}, u32[]{:S(2)}, u32[]{:S(2)}) collective-permute-start(bf16[4,496,128]{2,1,0:T(8,128)(2,1)S(1)} %get-tuple-element.12), channel_id=1, source_target_pairs={{0,1},{1,0},{2,3},{3,2},{4,5},{5,4},{6,7},{7,6},{8,9},{9,8},{10,11... | collective-permute-start | bytes 1523720 | tf_op jit(solution)/shard_map/ppermute | solution.py:253
  78.7 1.9 %collective-permute-done.other_ref = bf16[4,496,128]{2,1,0:T(8,128)(2,1)S(1)} collective-permute-done((bf16[4,496,128]{2,1,0:T(8,128)(2,1)S(1)}, bf16[4,496,128]{2,1,0:T(8,128)(2,1)S(1)}, u32[]{:S(2)}, u32[]{:S(2)}) %collective-permute-start) | collective-permute-done | bytes 507936 | tf_op jit(solution)/shard_map/ppermute | solution.py:253
  80.6 0.1 core_summed.1
  80.7 13.9 %all_to_all.25.in_ref = bf16[4,496,128]{2,1,0:T(8,128)(2,1)S(1)} all-to-all(bf16[4,496,128]{2,1,0:T(8,128)(2,1)S(1)} %core_summed.1), channel_id=1, replica_groups=mesh['x'=4,'zh'=2,'zq'=2,'zn'=4,'y'=4,'core'=2] {'y'}, dimensions={0} | all-to-all | bytes 1015808 | tf_op jit(solution)/shard_map/all_to_all | solution.py:254
  94.6 0.2 silu_copies.1
  94.8 10.7 %all_to_all.26 = bf16[4,480,128]{2,1,0:T(8,128)(2,1)S(1)} all-to-all(bf16[4,480,128]{2,1,0:T(8,128)(2,1)S(1)} %silu_copies.1), channel_id=1, replica_groups=mesh['x'=4,'zh'=2,'zq'=2,'zn'=4,'y'=4,'core'=2] {'y'}, dimensions={0} | all-to-all | bytes 983040 | tf_op jit(solution)/shard_map/all_to_all | solution.py:255
  105.4 2.5 %all_gather.7 = bf16[8,480,128]{2,1,0:T(8,128)(2,1)S(1)} all-gather(bf16[4,480,128]{2,1,0:T(8,128)(2,1)S(1)} %all_to_all.26), channel_id=1, replica_groups=mesh['x'=4,'zh'=2,'zq'=2,'zn'=4,'y'=4,'core'=2] {'core'}, dimensions={0}, use_global_device_ids=true | all-gather | bytes 1474560 | tf_op jit(solution)/shard_map/all_gather | solution.py:256
  107.9 0.0 copy-done
  107.9 0.9 convolution_convert_fusion
  108.9 22.1 %all_to_all.27 = bf16[4,120,768]{2,1,0:T(8,128)(2,1)S(1)} all-to-all(bf16[4,120,768]{2,1,0:T(8,128)(2,1)S(1)} %bitcast.36), channel_id=1, replica_groups=mesh['x'=4,'zh'=2,'zq'=2,'zn'=4,'y'=4,'core'=2] {'zn'}, dimensions={0} | all-to-all | bytes 1474560 | tf_op jit(solution)/shard_map/all_to_all | solution.py:50
  131.0 0.1 reduce_sum.74
  131.1 0.2 convolution_convert_fusion.1
  131.4 0.1 reshape.137
  131.5 33.2 %all_to_all.28 = bf16[64,4,768]{2,1,0:T(4,128)(2,1)S(1)} all-to-all(bf16[64,4,768]{2,1,0:T(4,128)(2,1)S(1)} %reshape.137), channel_id=1, replica_groups=mesh['x'=4,'zh'=2,'zq'=2,'zn'=4,'y'=4,'core'=2] {'x','zh','zq','zn'}, dimensions={0} | all-to-all | bytes 786432 | tf_op jit(solution)/shard_map/all_to_all | solution.py:264
  164.6 0.1 reshape.139
  164.7 0.1 reduce_sum.75
  164.8 1.0 fusion.4
  (2 shorter events, 0.0 us)
Async XLA Ops:
  0.0 107.9 %copy-start = (bf16[1024,768]{1,0:T(8,128)(2,1)S(1)}, bf16[1024,768]{1,0:T(8,128)(2,1)}, u32[]{:S(2)}) copy-start(bf16[1024,768]{1,0:T(8,128)(2,1)} %param.19) | copy-start | bytes 4718596
  0.0 5.3 %copy-start.3 = (s32[32,2]{0,1:T(2,128)S(1)}, s32[32,2]{0,1:T(2,128)}, u32[]{:S(2)}) copy-start(s32[32,2]{0,1:T(2,128)} %param.16) | copy-start | bytes 772
  0.0 5.3 %copy-start.5 = (f32[32,2]{0,1:T(2,128)S(1)}, f32[32,2]{0,1:T(2,128)}, u32[]{:S(2)}) copy-start(f32[32,2]{0,1:T(2,128)} %param.17) | copy-start | bytes 772
  0.0 5.4 %copy-start.1 = (bf16[32,128,128]{2,1,0:T(8,128)(2,1)S(1)}, bf16[32,128,128]{2,1,0:T(8,128)(2,1)}, u32[]{:S(2)}) copy-start(bf16[32,128,128]{2,1,0:T(8,128)(2,1)} %param.13) | copy-start | bytes 3145732
  0.0 6.0 %copy-start.2 = (bf16[32,768]{1,0:T(8,128)(2,1)S(1)}, bf16[32,768]{1,0:T(8,128)(2,1)}, u32[]{:S(2)}) copy-start(bf16[32,768]{1,0:T(8,128)(2,1)} %param.10) | copy-start | bytes 147460
  6.0 20.2 %copy-start.4 = (bf16[768]{0:T(1024)(128)(2,1)S(1)}, bf16[768]{0:T(1024)(128)(2,1)}, u32[]{:S(2)}) copy-start(bf16[768]{0:T(1024)(128)(2,1)} %param.15) | copy-start | bytes 4612
  7.4 47.7 %all-to-all-start = ((bf16[64,4,896]{2,1,0:T(4,128)(2,1)}), bf16[64,4,896]{2,1,0:T(4,128)(2,1)S(1)}, u32[]{:S(2)}, u32[]{:S(2)}) async-start(bf16[64,4,896]{2,1,0:T(4,128)(2,1)} %bitcast.2), calls=%async_computation | async-start | bytes 917504 | tf_op jit(solution)/shard_map/all_to_all | solution.py:246
  76.8 3.8 %collective-permute-start = (bf16[4,496,128]{2,1,0:T(8,128)(2,1)S(1)}, bf16[4,496,128]{2,1,0:T(8,128)(2,1)S(1)}, u32[]{:S(2)}, u32[]{:S(2)}) collective-permute-start(bf16[4,496,128]{2,1,0:T(8,128)(2,1)S(1)} %get-tuple-element.12), channel_id=1, source_target_pairs={{0,1},{1,0},{2,3},{3,2},{4,5},{5,4},{6,7},{7,6},{8,9},{9,8},{10,11... | collective-permute-start | bytes 1523720 | tf_op jit(solution)/shard_map/ppermute | solution.py:253

commit v4 on v3

--- a/solution.py
+++ b/solution.py
@@ -29,20 +29,121 @@
 TENSOR = ("y", "core")
 
 
-def attend(residual, queries, keys, values, lengths):
+TOKENS = 32
+STEP = 16
+GROUP = HEADS // KV
+
+
+def route(block, ids_ref, weights_ref):
+    ids = ids_ref[...]
+    experts = lax.broadcasted_iota(jnp.int32, (EXPERTS, TOKENS), 0)
+    names = [(ids[k : k + 1] == experts).astype(jnp.float32) for k in range(TOPK)]
+    named = names[0] + names[1]
+    before = lax.broadcasted_iota(jnp.int32, (TOKENS, TOKENS), 0) < lax.broadcasted_iota(
+        jnp.int32, (TOKENS, TOKENS), 1
+    )
+    earlier = jnp.dot(named, before.astype(jnp.float32), preferred_element_type=jnp.float32)
+    slot = lax.broadcasted_iota(jnp.int32, (EXPERTS * SRC_CAP, TOKENS), 0)
+    pick = jnp.zeros(slot.shape, jnp.float32)
+    mix = jnp.zeros(slot.shape, jnp.float32)
+    for k in range(TOPK):
+        rank = jnp.sum(earlier * names[k], axis=0, keepdims=True).astype(jnp.int32)
+        target = ids[k : k + 1] * SRC_CAP + (rank + block) % CLASSES * PER_CLASS + rank // CLASSES
+        here = slot == target
+        pick = jnp.where(here, 1.0, pick)
+        mix = jnp.where(here, weights_ref[k : k + 1], mix)
+    return pick, mix, jnp.sum(named, axis=1, keepdims=True)
+
+
+def tokens_kernel(
+    block_ref, lengths_ref, ids_ref, weights_ref, residual_ref, queries_ref, keys_ref, values_ref,
+    summed_ref, out_ref, mix_ref, query_ref, attended_ref, all_ref,
+):
+    step = pl.program_id(0)
+
+    @pl.when(step == 0)
+    def _():
+        query_ref[...] = jnp.zeros_like(query_ref)
+
+    for h in range(GROUP):
+        query_ref[:, h, :] = queries_ref[:, h * HEAD : (h + 1) * HEAD].astype(jnp.float32)
+    position = lax.broadcasted_iota(jnp.int32, (8, CACHE), 1)
+    for t in range(STEP):
+        scores = lax.dot_general(
+            query_ref[t].astype(jnp.bfloat16),
+            keys_ref[t],
+            (((1,), (1,)), ((), ())),
+            preferred_element_type=jnp.float32,
+        ) * HEAD ** (-0.5)
+        scores = jnp.where(position < lengths_ref[step * STEP + t], scores, -1e30)
+        powered = jnp.exp(scores - jnp.max(scores, axis=1, keepdims=True))
+        probs = (powered / jnp.sum(powered, axis=1, keepdims=True)).astype(jnp.bfloat16)
+        attended_ref[t] = jnp.dot(probs, values_ref[t], preferred_element_type=jnp.float32)
+    for h in range(GROUP):
+        lanes = slice(h * HEAD, (h + 1) * HEAD)
+        total = residual_ref[:, lanes].astype(jnp.float32) + attended_ref[:, h, :]
+        summed_ref[:, lanes] = total
+        all_ref[pl.ds(pl.multiple_of(step * STEP, STEP), STEP), lanes] = total
+
+    @pl.when(step == TOKENS // STEP - 1)
+    def _():
+        pick, mix, counts = route(block_ref[0], ids_ref, weights_ref)
+        mix_ref[...] = mix
+        packed = jnp.dot(
+            pick.astype(jnp.bfloat16), all_ref[...].astype(jnp.bfloat16), preferred_element_type=jnp.float32
+        )
+        width = packed.shape[1]
+        for e in range(EXPERTS):
+            meta = jnp.broadcast_to(counts[e : e + 1], (PER_CLASS, META)).astype(jnp.bfloat16)
+            for c in range(CLASSES):
+                first = e * SRC_CAP + c * PER_CLASS
+                rows = packed[first : first + PER_CLASS].astype(jnp.bfloat16)
+                for group in range(2):
+                    peer = (e * 2 + group) * CLASSES + c
+                    out_ref[peer, :, :width] = rows
+                    out_ref[peer, :, width:] = meta
+
+
+def tokens_packed(block, lengths, expert_ids, expert_weights, residual, queries, keys, values):
     tokens, width = residual.shape
-    group_size = HEADS // KV
-    query_rows = queries.reshape(tokens, group_size, HEAD)
-    scores = jnp.einsum(
-        "tjd,tld->tjl", query_rows, keys, preferred_element_type=jnp.float32
-    ) * HEAD ** (-0.5)
-    live_mask = (jnp.arange(CACHE, dtype=jnp.int32)[None, :] < lengths[:, None])[:, None, :]
-    scores = jnp.where(live_mask, scores, -1e30)
-    peak_score = jnp.max(scores, axis=-1, keepdims=True)
-    powered = jnp.exp(scores - peak_score)
-    probs = (powered / jnp.sum(powered, axis=-1, keepdims=True)).astype(jnp.bfloat16)
-    attended = jnp.einsum("tjl,tld->tjd", probs, values, preferred_element_type=jnp.float32)
-    return residual.astype(jnp.float32) + attended.reshape(tokens, width)
+    whole = lambda *shape: pl.BlockSpec(shape, lambda i: (0,) * len(shape))
+    return pl.pallas_call(
+        tokens_kernel,
+        grid=(TOKENS // STEP,),
+        in_specs=[
+            pl.BlockSpec(memory_space=pltpu.SMEM),
+            pl.BlockSpec(memory_space=pltpu.SMEM),
+            whole(TOPK, TOKENS),
+            whole(TOPK, TOKENS),
+            pl.BlockSpec((STEP, width), lambda i: (i, 0)),
+            pl.BlockSpec((STEP, width), lambda i: (i, 0)),
+            pl.BlockSpec((STEP, CACHE, HEAD), lambda i: (i, 0, 0)),
+            pl.BlockSpec((STEP, CACHE, HEAD), lambda i: (i, 0, 0)),
+        ],
+        out_specs=[
+            pl.BlockSpec((STEP, width), lambda i: (i, 0)),
+            whole(BLOCKS, PER_CLASS, width + META),
+            whole(EXPERTS * SRC_CAP, TOKENS),
+        ],
+        out_shape=[
+            jax.ShapeDtypeStruct((tokens, width), jnp.float32),
+            jax.ShapeDtypeStruct((BLOCKS, PER_CLASS, width + META), jnp.bfloat16),
+            jax.ShapeDtypeStruct((EXPERTS * SRC_CAP, TOKENS), jnp.float32),
+        ],
+        scratch_shapes=[
+            pltpu.VMEM((STEP, 8, HEAD), jnp.float32),
+            pltpu.VMEM((STEP, 8, HEAD), jnp.float32),
+            pltpu.VMEM((TOKENS, width), jnp.float32),
+        ],
+        compiler_params=pltpu.CompilerParams(vmem_limit_bytes=32 << 20),
+        name="tokens_packed",
+    )(
+        block.reshape(1),
+        *(
+            pltpu.with_memory_space_constraint(operand, pltpu.HBM)
+            for operand in (lengths, expert_ids.T, expert_weights.T, residual, queries, keys, values)
+        ),
+    )
 
 
 def summed_at_owner(pieces, axis):
@@ -61,65 +162,56 @@
     return jnp.concatenate([leading, (sums - leading.astype(jnp.float32)).astype(jnp.bfloat16)], axis=0)
 
 
-def hidden_kernel(core_ref, rows_ref, gain_ref, w_ref, send_ref, keep_ref, scaled_ref, squares_ref):
-    step = pl.program_id(0)
-
-    @pl.when(step == 0)
-    def _():
-        wide = rows_ref[...].astype(jnp.float32)
-        scaled_ref[...] = (wide * gain_ref[...].astype(jnp.float32)).astype(jnp.bfloat16)
-        sums = jnp.sum(wide * wide, axis=1, keepdims=True)
-        lines = [
-            jnp.sum(
-                jnp.where(diagonal(), sums[c * CLASS_ROWS : (c + 1) * CLASS_ROWS], 0.0),
-                axis=0,
-                keepdims=True,
+def hidden_kernel(core_ref, rows_ref, gain_ref, w_ref, send_ref, keep_ref, held_ref, sems):
+    columns = 2 * UNIT
+    copies = []
+    for k in range(4):
+        source = (k + 2 - 2 * core_ref[0]) % 4 * columns
+        copies.append(
+            pltpu.make_async_copy(
+                w_ref.at[:, pl.ds(pl.multiple_of(source, columns), columns)], held_ref.at[k], sems.at[k]
             )
-            for c in range(CLASSES)
-        ]
-        lines.append(jnp.zeros((SQUARES // 2 - CLASSES, UNIT), jnp.float32))
-        squares_ref[...] = leading_and_rest(jnp.concatenate(lines, axis=0))
-
-    sums = jnp.dot(scaled_ref[...], w_ref[...], preferred_element_type=jnp.float32)
-
-    def write(out_ref):
+        )
+        copies[k].start()
+
+    wide = rows_ref[...].astype(jnp.float32)
+    scaled = (wide * gain_ref[...].astype(jnp.float32)).astype(jnp.bfloat16)
+    sums = jnp.sum(wide * wide, axis=1, keepdims=True)
+    lines = [
+        jnp.sum(
+            jnp.where(diagonal(), sums[c * CLASS_ROWS : (c + 1) * CLASS_ROWS], 0.0), axis=0, keepdims=True
+        )
+        for c in range(CLASSES)
+    ]
+    lines.append(jnp.zeros((SQUARES // 2 - CLASSES, UNIT), jnp.float32))
+    squares = leading_and_rest(jnp.concatenate(lines, axis=0))
+
+    for k in range(4):
+        out_ref = send_ref if k < 2 else keep_ref
+        copies[k].wait()
+        parts = jnp.dot(scaled, held_ref[k], preferred_element_type=jnp.float32)
         for half in range(2):
-            out_ref[half, :ROWS] = sums[:, half * UNIT : (half + 1) * UNIT].astype(jnp.bfloat16)
-            out_ref[half, ROWS:] = squares_ref[...]
-
-    @pl.when(step < 2)
-    def _():
-        write(send_ref)
-
-    @pl.when(step >= 2)
-    def _():
-        write(keep_ref)
+            piece = k % 2 * 2 + half
+            out_ref[piece, :ROWS] = parts[:, half * UNIT : (half + 1) * UNIT].astype(jnp.bfloat16)
+            out_ref[piece, ROWS:] = squares
 
 
 def hidden_pieces(rows, norm_gain, w_in, core):
     width, units = w_in.shape
     half = jax.ShapeDtypeStruct((units // (2 * UNIT), ROWS + SQUARES, UNIT), jnp.bfloat16)
-    block = (2, ROWS + SQUARES, UNIT)
     return pl.pallas_call(
         hidden_kernel,
-        grid_spec=pltpu.PrefetchScalarGridSpec(
-            num_scalar_prefetch=1,
-            grid=(4,),
-            in_specs=[
-                pl.BlockSpec((ROWS, width), lambda i, c: (0, 0)),
-                pl.BlockSpec((1, width), lambda i, c: (0, 0)),
-                pl.BlockSpec((width, 2 * UNIT), lambda i, c: (0, (i + 2 - 2 * c[0]) % 4)),
-            ],
-            out_specs=[
-                pl.BlockSpec(block, lambda i, c: (jnp.minimum(i, 1), 0, 0)),
-                pl.BlockSpec(block, lambda i, c: (jnp.maximum(i - 2, 0), 0, 0)),
-            ],
-            scratch_shapes=[
-                pltpu.VMEM((ROWS, width), jnp.bfloat16),
-                pltpu.VMEM((SQUARES, UNIT), jnp.bfloat16),
-            ],
-        ),
+        in_specs=[
+            pl.BlockSpec(memory_space=pltpu.SMEM),
+            pl.BlockSpec(memory_space=pltpu.VMEM),
+            pl.BlockSpec(memory_space=pltpu.VMEM),
+            pl.BlockSpec(memory_space=pl.ANY),
+        ],
         out_shape=[half, half],
+        scratch_shapes=[
+            pltpu.VMEM((4, width, 2 * UNIT), jnp.bfloat16),
+            pltpu.SemaphoreType.DMA((4,)),
+        ],
         compiler_params=pltpu.CompilerParams(vmem_limit_bytes=32 << 20),
         name="hidden_pieces",
     )(core.reshape(1), rows, norm_gain.reshape(1, width), pltpu.with_memory_space_constraint(w_in, pltpu.HBM))
@@ -220,33 +312,10 @@
     block = ((lax.axis_index("x") * 2 + lax.axis_index("zh")) * 2 + lax.axis_index("zq")) * 4 + lax.axis_index("zn")
     own_class = lax.axis_index("zn")
 
-    summed = attend(residual, queries, keys, values, lengths)
-    unscaled = summed.astype(jnp.bfloat16)
-
-    flat_ids = expert_ids.reshape(-1)
-    pairs = flat_ids.shape[0]
-    same = flat_ids[:, None] == flat_ids[None, :]
-    earlier = jnp.arange(pairs)[:, None] > jnp.arange(pairs)[None, :]
-    rank = jnp.sum((same & earlier).astype(jnp.int32), axis=1)
-    slots = EXPERTS * SRC_CAP
-    target = flat_ids * SRC_CAP + (rank + block) % CLASSES * PER_CLASS + rank // CLASSES
-    pick_pairs = target[None, :] == jnp.arange(slots, dtype=jnp.int32)[:, None]
-    pick_tokens = jnp.sum(
-        pick_pairs.reshape(slots, tokens, TOPK).astype(jnp.float32), axis=2
-    ).astype(jnp.bfloat16)
-    counts = jnp.sum(
-        (flat_ids[None, :] == jnp.arange(EXPERTS, dtype=jnp.int32)[:, None]).astype(jnp.float32), axis=1
-    ).astype(jnp.bfloat16)
-
-    packed = jnp.dot(pick_tokens, unscaled, preferred_element_type=jnp.float32).astype(jnp.bfloat16)
-    packed = packed.reshape(EXPERTS, 1, CLASSES, PER_CLASS, width)
-    meta = jnp.broadcast_to(counts[:, None, None, None, None], (EXPERTS, 1, CLASSES, PER_CLASS, META))
-    outgoing = jnp.concatenate([packed, meta], axis=-1)
-    outgoing = jnp.broadcast_to(outgoing, (EXPERTS, 2, CLASSES, PER_CLASS, width + META))
-    received = lax.all_to_all(
-        outgoing.reshape(BLOCKS, PER_CLASS, width + META), DP, split_axis=0, concat_axis=0, tiled=True
-    )
-
+    summed, outgoing, mix_rows = tokens_packed(
+        block, lengths, expert_ids, expert_weights, residual, queries, keys, values
+    )
+    received = lax.all_to_all(outgoing, DP, split_axis=0, concat_axis=0, tiled=True)
     class_rows, chosen = compacted(received.reshape(BLOCKS * PER_CLASS, width + META), own_class)
     rows = lax.all_gather(class_rows, "zn", axis=0, tiled=True)
     send, own = hidden_pieces(rows, norm_gain, w_in, lax.axis_index("core"))
@@ -266,11 +335,7 @@
     )
     per_expert = jnp.sum(
         combined.reshape(EXPERTS, 2, SRC_CAP, width).astype(jnp.float32), axis=1
-    ).reshape(slots, width)
-    mix_rows = jnp.sum(
-        (pick_pairs.astype(jnp.float32) * expert_weights.reshape(-1)[None, :]).reshape(slots, tokens, TOPK),
-        axis=2,
-    )
+    ).reshape(EXPERTS * SRC_CAP, width)
     addition = jnp.einsum("st,sd->td", mix_rows, per_expert, precision=lax.Precision.HIGHEST)
     return (summed + addition).astype(jnp.bfloat16)
 

time: 166 us -> 171 us (1.030)
  Pallas kernels: 4.57 us -> 17 us
  local copies, waits for them, and re-layouts: 3.38 us -> 0.27 us
  matrix products: 4.83 us -> 2.14 us
    pallas_call x1 -> x2, Pallas kernels: 3.53 us -> 16 us  [the longest x1 12.8 us: tokens_packed(): pl.pallas_call(tokens_kernel, grid=(TOKENS // STEP,), in_specs=[pl.BlockS...]
    dot_general x3 -> x0, matrix products: 2.7 us -> none  [the longest x1 1.86 us: attend(): jnp.einsum('tjd,tld->tjl', query_rows, keys, preferred_element_type=jnp.f...]
where the time goes in v4:
time: 171 us
  blocking collectives  99.7 us (58%)
  waiting for transfers between devices  30.7 us (18%)
  starting transfers between devices  20.7 us (12%)
  Pallas kernels  17 us (10%)
  matrix products  2.14 us (1%)
    all_to_all x1, blocking collectives, shards(): lax.all_to_all(returned.reshape(BLOCKS, PER_CLASS, width), DP, split_axis...  33.1 us
    all_to_all x1, waiting for transfers between devices, shards(): lax.all_to_all(outgoing, DP, split_axis=0, concat_axis=0, tiled=True)  28.8 us
    all_to_all x1, blocking collectives, summed_at_owner(): lax.all_to_all(pieces, axis, split_axis=0, concat_axis=0, tiled=True)  22.2 us
    all_to_all x1, starting transfers between devices, shards(): lax.all_to_all(outgoing, DP, split_axis=0, concat_axis=0, tiled=True)  18.8 us
    all_gather x1, blocking collectives, shards(): rows = lax.all_gather(class_rows, 'zn', axis=0, tiled=True)  17.4 us
    all_to_all x1, blocking collectives, shards(): lax.all_to_all(core_summed(own, other), 'y', split_axis=0, concat_axis=0,...  13.9 us
    pallas_call x1, Pallas kernels, tokens_packed(): pl.pallas_call(tokens_kernel, grid=(TOKENS // STEP,), in_specs=[pl.BlockS...  12.8 us
    all_to_all x1, blocking collectives, shards(): lax.all_to_all(silu_copies(pieces), 'y', split_axis=0, concat_axis=0, til...  10.7 us
  transfers between devices with their start and end apart: 2, of which 2 were waited for; matrix products, arithmetic and copies ran while one was open for 0% of the time, Pallas kernels for 0%

profile of v4, /device:TPU:6, one launch (start us, length us, event | category | flops | bytes accessed | tf_op | source)
XLA Modules:
  0.0 170.8 jit_solution(8990302535097134637)
XLA Ops:
  0.0 0.0 copy-start
  0.0 0.0 copy-start.1
  0.0 12.8 %tokens_packed.1 = (f32[32,768]{1,0:T(8,128)S(1)}, bf16[64,4,896]{2,1,0:T(4,128)(2,1)}, f32[128,32]{1,0:T(8,128)S(1)}) custom-call(s32[1]{0:T(128)} %bitcast.block_ref, s32[32]{0:T(128)} %lengths_ref.1, s32[2,32]{1,0:T(2,128)} %bitcast.21, f32[2,32]{1,0:T(2,128)} %bitcast.22, bf16[32,768]{1,0:T(8,128)(2,1)} %residual_ref.1, bf16[32,768]{1,0:T(8,128)(2,1)} %queries_ref.1, ...), custom_call_target="tpu_custom_call" | custom-call | tf_op jit(solution)/shard_map/tokens_packed/pallas_call | solution.py:110
  12.8 18.8 %all-to-all-start = ((bf16[64,4,896]{2,1,0:T(4,128)(2,1)}), bf16[64,4,896]{2,1,0:T(4,128)(2,1)S(1)}, u32[]{:S(2)}, u32[]{:S(2)}) async-start(bf16[64,4,896]{2,1,0:T(4,128)(2,1)} %get-tuple-element.14), calls=%async_computation | async-start | bytes 917504 | tf_op jit(solution)/shard_map/all_to_all | solution.py:318
  31.6 0.0 copy-done.1
  31.6 28.8 %all-to-all-done = bf16[64,4,896]{2,1,0:T(4,128)(2,1)S(1)} async-done(((bf16[64,4,896]{2,1,0:T(4,128)(2,1)}), bf16[64,4,896]{2,1,0:T(4,128)(2,1)S(1)}, u32[]{:S(2)}, u32[]{:S(2)}) %all-to-all-start) | async-done | bytes 458784 | tf_op jit(solution)/shard_map/all_to_all | solution.py:318
  60.5 0.1 reshape.32.received_ref
  60.6 0.7 compacted.1
  61.3 17.4 %all_gather.6.rows_ref = bf16[480,768]{1,0:T(8,128)(2,1)S(1)} all-gather(bf16[120,768]{1,0:T(8,128)(2,1)S(1)} %get-tuple-element.16), channel_id=1, replica_groups=mesh['x'=4,'zh'=2,'zq'=2,'zn'=4,'y'=4,'core'=2] {'zn'}, dimensions={0}, use_global_device_ids=true | all-gather | bytes 921600 | tf_op jit(solution)/shard_map/all_gather | solution.py:320
  78.7 3.2 %hidden_pieces.1 = (bf16[4,496,128]{2,1,0:T(8,128)(2,1)S(1)}, bf16[4,496,128]{2,1,0:T(8,128)(2,1)S(1)}) custom-call(s32[1]{0:T(128)} %bitcast.4.core_ref, bf16[480,768]{1,0:T(8,128)(2,1)S(1)} %all_gather.6.rows_ref, bf16[1,768]{1,0:T(2,128)(2,1)S(1)} %reshape.34.gain_ref, bf16[768,1024]{1,0:T(8,128)(2,1)} %w_ref.1), custom_call_target="tpu_custom_call" | custom-call | tf_op jit(solution)/shard_map/hidden_pieces/pallas_call | solution.py:202
  81.9 1.9 %collective-permute-start = (bf16[4,496,128]{2,1,0:T(8,128)(2,1)S(1)}, bf16[4,496,128]{2,1,0:T(8,128)(2,1)S(1)}, u32[]{:S(2)}, u32[]{:S(2)}) collective-permute-start(bf16[4,496,128]{2,1,0:T(8,128)(2,1)S(1)} %get-tuple-element.18), channel_id=1, source_target_pairs={{0,1},{1,0},{2,3},{3,2},{4,5},{5,4},{6,7},{7,6},{8,9},{9,8},{10,11... | collective-permute-start | bytes 1523720 | tf_op jit(solution)/shard_map/ppermute | solution.py:322
  83.8 1.9 %collective-permute-done.other_ref = bf16[4,496,128]{2,1,0:T(8,128)(2,1)S(1)} collective-permute-done((bf16[4,496,128]{2,1,0:T(8,128)(2,1)S(1)}, bf16[4,496,128]{2,1,0:T(8,128)(2,1)S(1)}, u32[]{:S(2)}, u32[]{:S(2)}) %collective-permute-start) | collective-permute-done | bytes 507936 | tf_op jit(solution)/shard_map/ppermute | solution.py:322
  85.6 0.1 core_summed.1
  85.8 13.9 %all_to_all.25.in_ref = bf16[4,496,128]{2,1,0:T(8,128)(2,1)S(1)} all-to-all(bf16[4,496,128]{2,1,0:T(8,128)(2,1)S(1)} %core_summed.1), channel_id=1, replica_groups=mesh['x'=4,'zh'=2,'zq'=2,'zn'=4,'y'=4,'core'=2] {'y'}, dimensions={0} | all-to-all | bytes 1015808 | tf_op jit(solution)/shard_map/all_to_all | solution.py:323
  99.6 0.2 silu_copies.1
  99.8 10.7 %all_to_all.26 = bf16[4,480,128]{2,1,0:T(8,128)(2,1)S(1)} all-to-all(bf16[4,480,128]{2,1,0:T(8,128)(2,1)S(1)} %silu_copies.1), channel_id=1, replica_groups=mesh['x'=4,'zh'=2,'zq'=2,'zn'=4,'y'=4,'core'=2] {'y'}, dimensions={0} | all-to-all | bytes 983040 | tf_op jit(solution)/shard_map/all_to_all | solution.py:324
  110.5 2.5 %all_gather.7 = bf16[8,480,128]{2,1,0:T(8,128)(2,1)S(1)} all-gather(bf16[4,480,128]{2,1,0:T(8,128)(2,1)S(1)} %all_to_all.26), channel_id=1, replica_groups=mesh['x'=4,'zh'=2,'zq'=2,'zn'=4,'y'=4,'core'=2] {'core'}, dimensions={0}, use_global_device_ids=true | all-gather | bytes 1474560 | tf_op jit(solution)/shard_map/all_gather | solution.py:325
  113.0 0.0 copy-done
  113.0 0.9 convolution_convert_fusion
  113.9 22.2 %all_to_all.27 = bf16[4,120,768]{2,1,0:T(8,128)(2,1)S(1)} all-to-all(bf16[4,120,768]{2,1,0:T(8,128)(2,1)S(1)} %bitcast.20), channel_id=1, replica_groups=mesh['x'=4,'zh'=2,'zq'=2,'zn'=4,'y'=4,'core'=2] {'zn'}, dimensions={0} | all-to-all | bytes 1474560 | tf_op jit(solution)/shard_map/all_to_all | solution.py:151
  136.1 0.1 reduce_sum.21
  136.2 0.2 convolution_convert_fusion.1
  136.4 0.1 reshape.37
  136.6 33.1 %all_to_all.28 = bf16[64,4,768]{2,1,0:T(4,128)(2,1)S(1)} all-to-all(bf16[64,4,768]{2,1,0:T(4,128)(2,1)S(1)} %reshape.37), channel_id=1, replica_groups=mesh['x'=4,'zh'=2,'zq'=2,'zn'=4,'y'=4,'core'=2] {'x','zh','zq','zn'}, dimensions={0} | all-to-all | bytes 786432 | tf_op jit(solution)/shard_map/all_to_all | solution.py:333
  169.7 0.1 reshape.39
  169.7 0.1 reduce_sum.22
  169.8 1.0 fusion
  (1 shorter events, 0.0 us)
Async XLA Ops:
  0.0 113.0 %copy-start = (bf16[1024,768]{1,0:T(8,128)(2,1)S(1)}, bf16[1024,768]{1,0:T(8,128)(2,1)}, u32[]{:S(2)}) copy-start(bf16[1024,768]{1,0:T(8,128)(2,1)} %param.19) | copy-start | bytes 4718596
  0.0 31.6 %copy-start.1 = (bf16[768]{0:T(1024)(128)(2,1)S(1)}, bf16[768]{0:T(1024)(128)(2,1)}, u32[]{:S(2)}) copy-start(bf16[768]{0:T(1024)(128)(2,1)} %param.15) | copy-start | bytes 4612
  12.8 47.7 %all-to-all-start = ((bf16[64,4,896]{2,1,0:T(4,128)(2,1)}), bf16[64,4,896]{2,1,0:T(4,128)(2,1)S(1)}, u32[]{:S(2)}, u32[]{:S(2)}) async-start(bf16[64,4,896]{2,1,0:T(4,128)(2,1)} %get-tuple-element.14), calls=%async_computation | async-start | bytes 917504 | tf_op jit(solution)/shard_map/all_to_all | solution.py:318
  81.9 3.8 %collective-permute-start = (bf16[4,496,128]{2,1,0:T(8,128)(2,1)S(1)}, bf16[4,496,128]{2,1,0:T(8,128)(2,1)S(1)}, u32[]{:S(2)}, u32[]{:S(2)}) collective-permute-start(bf16[4,496,128]{2,1,0:T(8,128)(2,1)S(1)} %get-tuple-element.18), channel_id=1, source_target_pairs={{0,1},{1,0},{2,3},{3,2},{4,5},{5,4},{6,7},{7,6},{8,9},{9,8},{10,11... | collective-permute-start | bytes 1523720 | tf_op jit(solution)/shard_map/ppermute | solution.py:322

commit v5 on v4

--- a/solution.py
+++ b/solution.py
@@ -30,7 +30,7 @@
 
 
 TOKENS = 32
-STEP = 16
+STEP = 32
 GROUP = HEADS // KV
 
 
@@ -68,17 +68,22 @@
     for h in range(GROUP):
         query_ref[:, h, :] = queries_ref[:, h * HEAD : (h + 1) * HEAD].astype(jnp.float32)
     position = lax.broadcasted_iota(jnp.int32, (8, CACHE), 1)
+    scores = []
     for t in range(STEP):
-        scores = lax.dot_general(
+        products = lax.dot_general(
             query_ref[t].astype(jnp.bfloat16),
             keys_ref[t],
             (((1,), (1,)), ((), ())),
             preferred_element_type=jnp.float32,
         ) * HEAD ** (-0.5)
-        scores = jnp.where(position < lengths_ref[step * STEP + t], scores, -1e30)
-        powered = jnp.exp(scores - jnp.max(scores, axis=1, keepdims=True))
-        probs = (powered / jnp.sum(powered, axis=1, keepdims=True)).astype(jnp.bfloat16)
-        attended_ref[t] = jnp.dot(probs, values_ref[t], preferred_element_type=jnp.float32)
+        scores.append(jnp.where(position < lengths_ref[step * STEP + t], products, -1e30))
+    scores = jnp.concatenate(scores, axis=0)
+    powered = jnp.exp(scores - jnp.max(scores, axis=1, keepdims=True))
+    probs = powered / jnp.sum(powered, axis=1, keepdims=True)
+    for t in range(STEP):
+        attended_ref[t] = jnp.dot(
+            probs[t * 8 : (t + 1) * 8].astype(jnp.bfloat16), values_ref[t], preferred_element_type=jnp.float32
+        )
     for h in range(GROUP):
         lanes = slice(h * HEAD, (h + 1) * HEAD)
         total = residual_ref[:, lanes].astype(jnp.float32) + attended_ref[:, h, :]
@@ -135,7 +140,7 @@
             pltpu.VMEM((STEP, 8, HEAD), jnp.float32),
             pltpu.VMEM((TOKENS, width), jnp.float32),
         ],
-        compiler_params=pltpu.CompilerParams(vmem_limit_bytes=32 << 20),
+        compiler_params=pltpu.CompilerParams(vmem_limit_bytes=10 << 20),
         name="tokens_packed",
     )(
         block.reshape(1),
@@ -162,20 +167,9 @@
     return jnp.concatenate([leading, (sums - leading.astype(jnp.float32)).astype(jnp.bfloat16)], axis=0)
 
 
-def hidden_kernel(core_ref, rows_ref, gain_ref, w_ref, send_ref, keep_ref, held_ref, sems):
-    columns = 2 * UNIT
-    copies = []
-    for k in range(4):
-        source = (k + 2 - 2 * core_ref[0]) % 4 * columns
-        copies.append(
-            pltpu.make_async_copy(
-                w_ref.at[:, pl.ds(pl.multiple_of(source, columns), columns)], held_ref.at[k], sems.at[k]
-            )
-        )
-        copies[k].start()
-
-    wide = rows_ref[...].astype(jnp.float32)
-    scaled = (wide * gain_ref[...].astype(jnp.float32)).astype(jnp.bfloat16)
+def hidden_kernel(core_ref, rows_ref, w_ref, send_ref, keep_ref):
+    rows = rows_ref[...]
+    wide = rows.astype(jnp.float32)
     sums = jnp.sum(wide * wide, axis=1, keepdims=True)
     lines = [
         jnp.sum(
@@ -186,18 +180,23 @@
     lines.append(jnp.zeros((SQUARES // 2 - CLASSES, UNIT), jnp.float32))
     squares = leading_and_rest(jnp.concatenate(lines, axis=0))
 
+    columns = 2 * UNIT
     for k in range(4):
         out_ref = send_ref if k < 2 else keep_ref
-        copies[k].wait()
-        parts = jnp.dot(scaled, held_ref[k], preferred_element_type=jnp.float32)
+        source = (k + 2 - 2 * core_ref[0]) % 4 * columns
+        parts = jnp.dot(
+            rows,
+            w_ref[:, pl.ds(pl.multiple_of(source, columns), columns)],
+            preferred_element_type=jnp.float32,
+        )
         for half in range(2):
             piece = k % 2 * 2 + half
             out_ref[piece, :ROWS] = parts[:, half * UNIT : (half + 1) * UNIT].astype(jnp.bfloat16)
             out_ref[piece, ROWS:] = squares
 
 
-def hidden_pieces(rows, norm_gain, w_in, core):
-    width, units = w_in.shape
+def hidden_pieces(rows, w_in, core):
+    units = w_in.shape[1]
     half = jax.ShapeDtypeStruct((units // (2 * UNIT), ROWS + SQUARES, UNIT), jnp.bfloat16)
     return pl.pallas_call(
         hidden_kernel,
@@ -205,16 +204,11 @@
             pl.BlockSpec(memory_space=pltpu.SMEM),
             pl.BlockSpec(memory_space=pltpu.VMEM),
             pl.BlockSpec(memory_space=pltpu.VMEM),
-            pl.BlockSpec(memory_space=pl.ANY),
         ],
         out_shape=[half, half],
-        scratch_shapes=[
-            pltpu.VMEM((4, width, 2 * UNIT), jnp.bfloat16),
-            pltpu.SemaphoreType.DMA((4,)),
-        ],
-        compiler_params=pltpu.CompilerParams(vmem_limit_bytes=32 << 20),
+        compiler_params=pltpu.CompilerParams(vmem_limit_bytes=10 << 20),
         name="hidden_pieces",
-    )(core.reshape(1), rows, norm_gain.reshape(1, width), pltpu.with_memory_space_constraint(w_in, pltpu.HBM))
+    )(core.reshape(1), rows, w_in)
 
 
 def core_kernel(own_ref, other_ref, out_ref):
@@ -231,7 +225,7 @@
     return pl.pallas_call(
         core_kernel,
         out_shape=jax.ShapeDtypeStruct(own.shape, jnp.bfloat16),
-        compiler_params=pltpu.CompilerParams(vmem_limit_bytes=32 << 20),
+        compiler_params=pltpu.CompilerParams(vmem_limit_bytes=10 << 20),
         name="core_summed",
     )(own, other)
 
@@ -253,15 +247,16 @@
     return pl.pallas_call(
         silu_kernel,
         out_shape=jax.ShapeDtypeStruct((pieces.shape[0], ROWS, UNIT), jnp.bfloat16),
-        compiler_params=pltpu.CompilerParams(vmem_limit_bytes=32 << 20),
+        compiler_params=pltpu.CompilerParams(vmem_limit_bytes=10 << 20),
         name="silu_copies",
     )(pieces)
 
 
 def compact_kernel(class_ref, received_ref, rows_ref, place_ref):
-    slots = received_ref.shape[0]
     width = rows_ref.shape[1]
     own_class = class_ref[0]
+    received = received_ref[...].reshape(BLOCKS * PER_CLASS, width + META)
+    slots = received.shape[0]
     row = lax.broadcasted_iota(jnp.int32, (slots, slots), 0)
     column = lax.broadcasted_iota(jnp.int32, (slots, slots), 1)
     earlier = (column // PER_CLASS < row // PER_CLASS) & (column % PER_CLASS == 0)
@@ -270,7 +265,7 @@
     def earlier_sum(counts):
         return jnp.dot(earlier, counts, preferred_element_type=jnp.float32).astype(jnp.int32)
 
-    counts = received_ref[:, width:]
+    counts = received[:, width:]
     named = counts.astype(jnp.float32).astype(jnp.int32)
     kept = jnp.clip(CAPACITY - earlier_sum(counts), 0, named)
     line = lax.broadcasted_iota(jnp.int32, named.shape, 0)
@@ -283,13 +278,13 @@
     chosen = chosen.astype(jnp.float32).astype(jnp.bfloat16)
     place_ref[...] = chosen
     rows = lax.dot_general(
-        chosen, received_ref[:, :width], (((0,), (0,)), ((), ())), preferred_element_type=jnp.float32
+        chosen, received[:, :width], (((0,), (0,)), ((), ())), preferred_element_type=jnp.float32
     )
     rows_ref[...] = rows[: rows_ref.shape[0]].astype(jnp.bfloat16)
 
 
 def compacted(received, own_class):
-    slots, wide = received.shape
+    blocks, places, wide = received.shape
     return pl.pallas_call(
         compact_kernel,
         in_specs=[
@@ -298,9 +293,9 @@
         ],
         out_shape=[
             jax.ShapeDtypeStruct((CLASS_ROWS, wide - META), jnp.bfloat16),
-            jax.ShapeDtypeStruct((slots, META), jnp.bfloat16),
-        ],
-        compiler_params=pltpu.CompilerParams(vmem_limit_bytes=32 << 20),
+            jax.ShapeDtypeStruct((blocks * places, META), jnp.bfloat16),
+        ],
+        compiler_params=pltpu.CompilerParams(vmem_limit_bytes=10 << 20),
         name="compacted",
     )(own_class.reshape(1), received)
 
@@ -315,10 +310,11 @@
     summed, outgoing, mix_rows = tokens_packed(
         block, lengths, expert_ids, expert_weights, residual, queries, keys, values
     )
+    gained = (w_in.astype(jnp.float32) * norm_gain.astype(jnp.float32)[:, None]).astype(jnp.bfloat16)
     received = lax.all_to_all(outgoing, DP, split_axis=0, concat_axis=0, tiled=True)
-    class_rows, chosen = compacted(received.reshape(BLOCKS * PER_CLASS, width + META), own_class)
+    class_rows, chosen = compacted(received, own_class)
     rows = lax.all_gather(class_rows, "zn", axis=0, tiled=True)
-    send, own = hidden_pieces(rows, norm_gain, w_in, lax.axis_index("core"))
+    send, own = hidden_pieces(rows, gained, lax.axis_index("core"))
     other = lax.ppermute(send, "core", ((0, 1), (1, 0)))
     pieces = lax.all_to_all(core_summed(own, other), "y", split_axis=0, concat_axis=0, tiled=True)
     gathered = lax.all_to_all(silu_copies(pieces), "y", split_axis=0, concat_axis=0, tiled=True)

time: 171 us -> 161 us (0.942)
  Pallas kernels: 17 us -> 6.87 us
  waiting for transfers between devices: 30.7 us -> 28.9 us
  other arithmetic: 0.17 us -> 1.9 us
    pallas_call x1, Pallas kernels: 12.8 us -> 3.72 us  [tokens_packed(): pl.pallas_call(tokens_kernel, grid=(TOKENS // STEP,), in_specs=[pl.BlockS...]
    pallas_call x1, Pallas kernels: 3.17 us -> 0.95 us  [hidden_pieces(): pl.pallas_call(hidden_kernel, in_specs=[pl.BlockSpec(memory_space=pltpu.S...]
    all_to_all x1, waiting for transfers between devices: 28.8 us -> 27 us  [shards(): lax.all_to_all(outgoing, DP, split_axis=0, concat_axis=0, tiled=True)]
    convert_element_type x0 -> x2, other arithmetic: none -> 1.73 us  [the longest x1 1.73 us: shards(): (w_in.astype(jnp.float32) * norm_gain.astype(jnp.float32)[:, None]).astyp...]
  transfers between devices with their start and end apart: 2 -> 2, of which waited for: 2 -> 2; matrix products, arithmetic and copies ran while one was open for 0% -> 1% of each run, Pallas kernels for 0% -> 0%
where the time goes in v5:
time: 161 us
  blocking collectives  99.7 us (62%)
  waiting for transfers between devices  28.9 us (18%)
  starting transfers between devices  20.9 us (13%)
  Pallas kernels  6.87 us (4%)
  matrix products  2.14 us (1%)
  other arithmetic  1.9 us (1%)
    all_to_all x1, blocking collectives, shards(): lax.all_to_all(returned.reshape(BLOCKS, PER_CLASS, width), DP, split_axis...  33.2 us
    all_to_all x1, waiting for transfers between devices, shards(): lax.all_to_all(outgoing, DP, split_axis=0, concat_axis=0, tiled=True)  27 us
    all_to_all x1, blocking collectives, summed_at_owner(): lax.all_to_all(pieces, axis, split_axis=0, concat_axis=0, tiled=True)  22.2 us
    all_to_all x1, starting transfers between devices, shards(): lax.all_to_all(outgoing, DP, split_axis=0, concat_axis=0, tiled=True)  19 us
    all_gather x1, blocking collectives, shards(): rows = lax.all_gather(class_rows, 'zn', axis=0, tiled=True)  17.4 us
    all_to_all x1, blocking collectives, shards(): lax.all_to_all(core_summed(own, other), 'y', split_axis=0, concat_axis=0,...  13.9 us
    all_to_all x1, blocking collectives, shards(): lax.all_to_all(silu_copies(pieces), 'y', split_axis=0, concat_axis=0, til...  10.7 us
    pallas_call x1, Pallas kernels, tokens_packed(): pl.pallas_call(tokens_kernel, grid=(TOKENS // STEP,), in_specs=[pl.BlockS...  3.72 us
  transfers between devices with their start and end apart: 2, of which 2 were waited for; matrix products, arithmetic and copies ran while one was open for 1% of the time, Pallas kernels for 0%

profile of v5, /device:TPU:6, one launch (start us, length us, event | category | flops | bytes accessed | tf_op | source)
XLA Modules:
  0.0 160.6 jit_solution(10524160166735841653)
XLA Ops:
  0.0 0.0 copy-start
  0.0 0.0 copy-start.1
  0.0 3.7 %tokens_packed.1 = (f32[32,768]{1,0:T(8,128)S(1)}, bf16[64,4,896]{2,1,0:T(4,128)(2,1)}, f32[128,32]{1,0:T(8,128)S(1)}) custom-call(s32[1]{0:T(128)} %bitcast.block_ref, s32[32]{0:T(128)} %lengths_ref.1, s32[2,32]{1,0:T(2,128)} %bitcast.21, f32[2,32]{1,0:T(2,128)} %bitcast.22, bf16[32,768]{1,0:T(8,128)(2,1)} %residual_ref.1, bf16[32,768]{1,0:T(8,128)(2,1)} %queries_ref.1, ...), custom_call_target="tpu_custom_call" | custom-call | tf_op jit(solution)/shard_map/tokens_packed/pallas_call | solution.py:115
  3.7 19.0 %all-to-all-start = ((bf16[64,4,896]{2,1,0:T(4,128)(2,1)}), bf16[64,4,896]{2,1,0:T(4,128)(2,1)}, u32[]{:S(2)}, u32[]{:S(2)}) async-start(bf16[64,4,896]{2,1,0:T(4,128)(2,1)} %get-tuple-element.14), calls=%async_computation | async-start | bytes 917504 | tf_op jit(solution)/shard_map/all_to_all | solution.py:314
  22.7 0.0 copy-done.1
  22.7 1.7 %multiply_convert_fusion.w_ref = bf16[768,1024]{1,0:T(8,128)(2,1)S(1)} fusion(bf16[768,1024]{1,0:T(8,128)(2,1)} %param.18, f32[768]{0:T(1024)S(1)} %convert_element_type.27), kind=kLoop, calls=%fused_computation | loop fusion | flops 2359296 | bytes 3148800 | tf_op jit(solution)/shard_map/convert_element_type | solution.py:313
  24.5 27.0 %all-to-all-done.received_ref = bf16[64,4,896]{2,1,0:T(4,128)(2,1)} async-done(((bf16[64,4,896]{2,1,0:T(4,128)(2,1)}), bf16[64,4,896]{2,1,0:T(4,128)(2,1)}, u32[]{:S(2)}, u32[]{:S(2)}) %all-to-all-start) | async-done | bytes 458784 | tf_op jit(solution)/shard_map/all_to_all | solution.py:314
  51.5 1.9 %compacted.1 = (bf16[120,768]{1,0:T(8,128)(2,1)S(1)}, bf16[256,128]{1,0:T(8,128)(2,1)S(1)}) custom-call(s32[1]{0:T(128)} %bitcast.3.class_ref, bf16[64,4,896]{2,1,0:T(4,128)(2,1)} %all-to-all-done.received_ref), custom_call_target="tpu_custom_call" | custom-call | tf_op jit(solution)/shard_map/compacted/pallas_call | solution.py:288
  53.4 17.4 %all_gather.6.rows_ref = bf16[480,768]{1,0:T(8,128)(2,1)S(1)} all-gather(bf16[120,768]{1,0:T(8,128)(2,1)S(1)} %get-tuple-element.16), channel_id=1, replica_groups=mesh['x'=4,'zh'=2,'zq'=2,'zn'=4,'y'=4,'core'=2] {'zn'}, dimensions={0}, use_global_device_ids=true | all-gather | bytes 921600 | tf_op jit(solution)/shard_map/all_gather | solution.py:316
  70.8 1.0 hidden_pieces.1
  71.7 1.9 %collective-permute-start = (bf16[4,496,128]{2,1,0:T(8,128)(2,1)S(1)}, bf16[4,496,128]{2,1,0:T(8,128)(2,1)S(1)}, u32[]{:S(2)}, u32[]{:S(2)}) collective-permute-start(bf16[4,496,128]{2,1,0:T(8,128)(2,1)S(1)} %get-tuple-element.18), channel_id=1, source_target_pairs={{0,1},{1,0},{2,3},{3,2},{4,5},{5,4},{6,7},{7,6},{8,9},{9,8},{10,11... | collective-permute-start | bytes 1523720 | tf_op jit(solution)/shard_map/ppermute | solution.py:318
  73.6 1.9 %collective-permute-done.other_ref = bf16[4,496,128]{2,1,0:T(8,128)(2,1)S(1)} collective-permute-done((bf16[4,496,128]{2,1,0:T(8,128)(2,1)S(1)}, bf16[4,496,128]{2,1,0:T(8,128)(2,1)S(1)}, u32[]{:S(2)}, u32[]{:S(2)}) %collective-permute-start) | collective-permute-done | bytes 507936 | tf_op jit(solution)/shard_map/ppermute | solution.py:318
  75.5 0.1 core_summed.1
  75.6 13.9 %all_to_all.25.in_ref = bf16[4,496,128]{2,1,0:T(8,128)(2,1)S(1)} all-to-all(bf16[4,496,128]{2,1,0:T(8,128)(2,1)S(1)} %core_summed.1), channel_id=1, replica_groups=mesh['x'=4,'zh'=2,'zq'=2,'zn'=4,'y'=4,'core'=2] {'y'}, dimensions={0} | all-to-all | bytes 1015808 | tf_op jit(solution)/shard_map/all_to_all | solution.py:319
  89.5 0.2 silu_copies.1
  89.7 10.7 %all_to_all.26 = bf16[4,480,128]{2,1,0:T(8,128)(2,1)S(1)} all-to-all(bf16[4,480,128]{2,1,0:T(8,128)(2,1)S(1)} %silu_copies.1), channel_id=1, replica_groups=mesh['x'=4,'zh'=2,'zq'=2,'zn'=4,'y'=4,'core'=2] {'y'}, dimensions={0} | all-to-all | bytes 983040 | tf_op jit(solution)/shard_map/all_to_all | solution.py:320
  100.3 2.5 %all_gather.7 = bf16[8,480,128]{2,1,0:T(8,128)(2,1)S(1)} all-gather(bf16[4,480,128]{2,1,0:T(8,128)(2,1)S(1)} %all_to_all.26), channel_id=1, replica_groups=mesh['x'=4,'zh'=2,'zq'=2,'zn'=4,'y'=4,'core'=2] {'core'}, dimensions={0}, use_global_device_ids=true | all-gather | bytes 1474560 | tf_op jit(solution)/shard_map/all_gather | solution.py:321
  102.8 0.0 copy-done
  102.8 0.9 convolution_convert_fusion
  103.8 22.2 %all_to_all.27 = bf16[4,120,768]{2,1,0:T(8,128)(2,1)S(1)} all-to-all(bf16[4,120,768]{2,1,0:T(8,128)(2,1)S(1)} %bitcast.20), channel_id=1, replica_groups=mesh['x'=4,'zh'=2,'zq'=2,'zn'=4,'y'=4,'core'=2] {'zn'}, dimensions={0} | all-to-all | bytes 1474560 | tf_op jit(solution)/shard_map/all_to_all | solution.py:156
  125.9 0.1 reduce_sum.21
  126.0 0.2 convolution_convert_fusion.1
  126.3 0.1 reshape.30
  126.4 33.2 %all_to_all.28 = bf16[64,4,768]{2,1,0:T(4,128)(2,1)S(1)} all-to-all(bf16[64,4,768]{2,1,0:T(4,128)(2,1)S(1)} %reshape.30), channel_id=1, replica_groups=mesh['x'=4,'zh'=2,'zq'=2,'zn'=4,'y'=4,'core'=2] {'x','zh','zq','zn'}, dimensions={0} | all-to-all | bytes 786432 | tf_op jit(solution)/shard_map/all_to_all | solution.py:329
  159.5 0.1 reshape.32
  159.6 0.1 reduce_sum.22
  159.7 1.0 fusion
  (1 shorter events, 0.0 us)
Async XLA Ops:
  0.0 102.8 %copy-start = (bf16[1024,768]{1,0:T(8,128)(2,1)S(1)}, bf16[1024,768]{1,0:T(8,128)(2,1)}, u32[]{:S(2)}) copy-start(bf16[1024,768]{1,0:T(8,128)(2,1)} %param.19) | copy-start | bytes 4718596
  0.0 22.7 %copy-start.1 = (bf16[768]{0:T(1024)(128)(2,1)S(1)}, bf16[768]{0:T(1024)(128)(2,1)}, u32[]{:S(2)}) copy-start(bf16[768]{0:T(1024)(128)(2,1)} %param.15) | copy-start | bytes 4612
  3.7 47.8 %all-to-all-start = ((bf16[64,4,896]{2,1,0:T(4,128)(2,1)}), bf16[64,4,896]{2,1,0:T(4,128)(2,1)}, u32[]{:S(2)}, u32[]{:S(2)}) async-start(bf16[64,4,896]{2,1,0:T(4,128)(2,1)} %get-tuple-element.14), calls=%async_computation | async-start | bytes 917504 | tf_op jit(solution)/shard_map/all_to_all | solution.py:314
  71.7 3.8 %collective-permute-start = (bf16[4,496,128]{2,1,0:T(8,128)(2,1)S(1)}, bf16[4,496,128]{2,1,0:T(8,128)(2,1)S(1)}, u32[]{:S(2)}, u32[]{:S(2)}) collective-permute-start(bf16[4,496,128]{2,1,0:T(8,128)(2,1)S(1)} %get-tuple-element.18), channel_id=1, source_target_pairs={{0,1},{1,0},{2,3},{3,2},{4,5},{5,4},{6,7},{7,6},{8,9},{9,8},{10,11... | collective-permute-start | bytes 1523720 | tf_op jit(solution)/shard_map/ppermute | solution.py:318

commit v6 on v5

--- a/solution.py
+++ b/solution.py
@@ -19,9 +19,11 @@
 CAPACITY = 384
 CLASS_ROWS = CAPACITY // CLASSES + BLOCKS * 6 // (4 * CLASSES)
 META = 128
-ROWS = CLASSES * CLASS_ROWS
+ROWS = CAPACITY
+SLOT_ROWS = CAPACITY // CLASSES
 SQUARES = 16
 UNIT = 128
+LINES = ROWS // UNIT
 
 NORM_EPSILON = 1e-05
 
@@ -34,8 +36,7 @@
 GROUP = HEADS // KV
 
 
-def route(block, ids_ref, weights_ref):
-    ids = ids_ref[...]
+def ranks(ids):
     experts = lax.broadcasted_iota(jnp.int32, (EXPERTS, TOKENS), 0)
     names = [(ids[k : k + 1] == experts).astype(jnp.float32) for k in range(TOPK)]
     named = names[0] + names[1]
@@ -43,21 +44,21 @@
         jnp.int32, (TOKENS, TOKENS), 1
     )
     earlier = jnp.dot(named, before.astype(jnp.float32), preferred_element_type=jnp.float32)
-    slot = lax.broadcasted_iota(jnp.int32, (EXPERTS * SRC_CAP, TOKENS), 0)
-    pick = jnp.zeros(slot.shape, jnp.float32)
-    mix = jnp.zeros(slot.shape, jnp.float32)
-    for k in range(TOPK):
-        rank = jnp.sum(earlier * names[k], axis=0, keepdims=True).astype(jnp.int32)
-        target = ids[k : k + 1] * SRC_CAP + (rank + block) % CLASSES * PER_CLASS + rank // CLASSES
-        here = slot == target
-        pick = jnp.where(here, 1.0, pick)
-        mix = jnp.where(here, weights_ref[k : k + 1], mix)
-    return pick, mix, jnp.sum(named, axis=1, keepdims=True)
+    rank = [jnp.sum(earlier * name, axis=0, keepdims=True).astype(jnp.int32) for name in names]
+    return names, rank, named
+
+
+def slot_iota():
+    return lax.broadcasted_iota(jnp.int32, (EXPERTS * SRC_CAP, TOKENS), 0)
+
+
+def packet_place(ids, rank, turn):
+    return ids * SRC_CAP + (rank + turn) % CLASSES * PER_CLASS + rank // CLASSES
 
 
 def tokens_kernel(
-    block_ref, lengths_ref, ids_ref, weights_ref, residual_ref, queries_ref, keys_ref, values_ref,
-    summed_ref, out_ref, mix_ref, query_ref, attended_ref, all_ref,
+    block_ref, lengths_ref, ids_ref, residual_ref, queries_ref, keys_ref, values_ref,
+    summed_ref, out_ref, query_ref, attended_ref, all_ref,
 ):
     step = pl.program_id(0)
 
@@ -92,14 +93,22 @@
 
     @pl.when(step == TOKENS // STEP - 1)
     def _():
-        pick, mix, counts = route(block_ref[0], ids_ref, weights_ref)
-        mix_ref[...] = mix
+        ids = ids_ref[...]
+        _, rank, named = ranks(ids)
+        pick = jnp.zeros((EXPERTS * SRC_CAP, TOKENS), jnp.float32)
+        for k in range(TOPK):
+            pick = jnp.where(slot_iota() == packet_place(ids[k : k + 1], rank[k], block_ref[0]), 1.0, pick)
         packed = jnp.dot(
             pick.astype(jnp.bfloat16), all_ref[...].astype(jnp.bfloat16), preferred_element_type=jnp.float32
         )
         width = packed.shape[1]
+        own_lane = lax.broadcasted_iota(jnp.int32, (EXPERTS, META), 0) == lax.broadcasted_iota(
+            jnp.int32, (EXPERTS, META), 1
+        )
+        counts = jnp.sum(named, axis=1, keepdims=True)
+        counts = jnp.sum(jnp.where(own_lane, counts, 0.0), axis=0, keepdims=True)
+        meta = jnp.broadcast_to(counts, (PER_CLASS, META)).astype(jnp.bfloat16)
         for e in range(EXPERTS):
-            meta = jnp.broadcast_to(counts[e : e + 1], (PER_CLASS, META)).astype(jnp.bfloat16)
             for c in range(CLASSES):
                 first = e * SRC_CAP + c * PER_CLASS
                 rows = packed[first : first + PER_CLASS].astype(jnp.bfloat16)
@@ -109,7 +118,7 @@
                     out_ref[peer, :, width:] = meta
 
 
-def tokens_packed(block, lengths, expert_ids, expert_weights, residual, queries, keys, values):
+def tokens_packed(block, lengths, expert_ids, residual, queries, keys, values):
     tokens, width = residual.shape
     whole = lambda *shape: pl.BlockSpec(shape, lambda i: (0,) * len(shape))
     return pl.pallas_call(
@@ -119,7 +128,6 @@
             pl.BlockSpec(memory_space=pltpu.SMEM),
             pl.BlockSpec(memory_space=pltpu.SMEM),
             whole(TOPK, TOKENS),
-            whole(TOPK, TOKENS),
             pl.BlockSpec((STEP, width), lambda i: (i, 0)),
             pl.BlockSpec((STEP, width), lambda i: (i, 0)),
             pl.BlockSpec((STEP, CACHE, HEAD), lambda i: (i, 0, 0)),
@@ -128,12 +136,10 @@
         out_specs=[
             pl.BlockSpec((STEP, width), lambda i: (i, 0)),
             whole(BLOCKS, PER_CLASS, width + META),
-            whole(EXPERTS * SRC_CAP, TOKENS),
         ],
         out_shape=[
             jax.ShapeDtypeStruct((tokens, width), jnp.float32),
             jax.ShapeDtypeStruct((BLOCKS, PER_CLASS, width + META), jnp.bfloat16),
-            jax.ShapeDtypeStruct((EXPERTS * SRC_CAP, TOKENS), jnp.float32),
         ],
         scratch_shapes=[
             pltpu.VMEM((STEP, 8, HEAD), jnp.float32),
@@ -146,7 +152,7 @@
         block.reshape(1),
         *(
             pltpu.with_memory_space_constraint(operand, pltpu.HBM)
-            for operand in (lengths, expert_ids.T, expert_weights.T, residual, queries, keys, values)
+            for operand in (lengths, expert_ids.T, residual, queries, keys, values)
         ),
     )
 
@@ -158,8 +164,8 @@
 
 
 def diagonal():
-    row = lax.broadcasted_iota(jnp.int32, (CLASS_ROWS, UNIT), 0)
-    return row == lax.broadcasted_iota(jnp.int32, (CLASS_ROWS, UNIT), 1)
+    row = lax.broadcasted_iota(jnp.int32, (UNIT, UNIT), 0)
+    return row == lax.broadcasted_iota(jnp.int32, (UNIT, UNIT), 1)
 
 
 def leading_and_rest(sums):
@@ -167,17 +173,17 @@
     return jnp.concatenate([leading, (sums - leading.astype(jnp.float32)).astype(jnp.bfloat16)], axis=0)
 
 
-def hidden_kernel(core_ref, rows_ref, w_ref, send_ref, keep_ref):
-    rows = rows_ref[...]
-    wide = rows.astype(jnp.float32)
+def hidden_kernel(core_ref, place_ref, gathered_ref, w_ref, send_ref, keep_ref):
+    wide = lax.dot_general(
+        place_ref[...], gathered_ref[...], (((0,), (0,)), ((), ())), preferred_element_type=jnp.float32
+    )
+    rows = wide.astype(jnp.bfloat16)
     sums = jnp.sum(wide * wide, axis=1, keepdims=True)
     lines = [
-        jnp.sum(
-            jnp.where(diagonal(), sums[c * CLASS_ROWS : (c + 1) * CLASS_ROWS], 0.0), axis=0, keepdims=True
-        )
-        for c in range(CLASSES)
+        jnp.sum(jnp.where(diagonal(), sums[g * UNIT : (g + 1) * UNIT], 0.0), axis=0, keepdims=True)
+        for g in range(LINES)
     ]
-    lines.append(jnp.zeros((SQUARES // 2 - CLASSES, UNIT), jnp.float32))
+    lines.append(jnp.zeros((SQUARES // 2 - LINES, UNIT), jnp.float32))
     squares = leading_and_rest(jnp.concatenate(lines, axis=0))
 
     columns = 2 * UNIT
@@ -195,7 +201,7 @@
             out_ref[piece, ROWS:] = squares
 
 
-def hidden_pieces(rows, w_in, core):
+def hidden_pieces(place, gathered, w_in, core):
     units = w_in.shape[1]
     half = jax.ShapeDtypeStruct((units // (2 * UNIT), ROWS + SQUARES, UNIT), jnp.bfloat16)
     return pl.pallas_call(
@@ -204,11 +210,12 @@
             pl.BlockSpec(memory_space=pltpu.SMEM),
             pl.BlockSpec(memory_space=pltpu.VMEM),
             pl.BlockSpec(memory_space=pltpu.VMEM),
+            pl.BlockSpec(memory_space=pltpu.VMEM),
         ],
         out_shape=[half, half],
         compiler_params=pltpu.CompilerParams(vmem_limit_bytes=10 << 20),
         name="hidden_pieces",
-    )(core.reshape(1), rows, w_in)
+    )(core.reshape(1), place, gathered, w_in)
 
 
 def core_kernel(own_ref, other_ref, out_ref):
@@ -235,12 +242,12 @@
     for piece in range(1, in_ref.shape[0]):
         total = total + in_ref[piece].astype(jnp.float32)
     squares = total[ROWS : ROWS + SQUARES // 2] + total[ROWS + SQUARES // 2 :]
-    for c in range(CLASSES):
-        own = jnp.sum(jnp.where(diagonal(), squares[c : c + 1], 0.0), axis=1, keepdims=True)
-        scaled = total[c * CLASS_ROWS : (c + 1) * CLASS_ROWS] * lax.rsqrt(own / D + NORM_EPSILON)
+    for g in range(LINES):
+        own = jnp.sum(jnp.where(diagonal(), squares[g : g + 1], 0.0), axis=1, keepdims=True)
+        scaled = total[g * UNIT : (g + 1) * UNIT] * lax.rsqrt(own / D + NORM_EPSILON)
         hidden = (scaled / (1.0 + jnp.exp(-scaled))).astype(jnp.bfloat16)
         for piece in range(out_ref.shape[0]):
-            out_ref[piece, c * CLASS_ROWS : (c + 1) * CLASS_ROWS] = hidden
+            out_ref[piece, g * UNIT : (g + 1) * UNIT] = hidden
 
 
 def silu_copies(pieces):
@@ -252,52 +259,115 @@
     )(pieces)
 
 
-def compact_kernel(class_ref, received_ref, rows_ref, place_ref):
+def output_kernel(hidden_ref, w_ref, out_ref):
+    hidden = jnp.concatenate([hidden_ref[piece] for piece in range(hidden_ref.shape[0])], axis=1)
+    out_ref[...] = jnp.dot(hidden, w_ref[...], preferred_element_type=jnp.float32).astype(jnp.bfloat16)
+
+
+def output_parts(hidden, w_out):
+    return pl.pallas_call(
+        output_kernel,
+        in_specs=[pl.BlockSpec(memory_space=pltpu.VMEM)] * 2,
+        out_shape=jax.ShapeDtypeStruct((ROWS, w_out.shape[1]), jnp.bfloat16),
+        compiler_params=pltpu.CompilerParams(vmem_limit_bytes=10 << 20),
+        name="output_parts",
+    )(hidden, w_out)
+
+
+def flags(condition):
+    return condition.astype(jnp.float32).astype(jnp.bfloat16)
+
+
+def compact_kernel(here_ref, ids_ref, weights_ref, received_ref, rows_ref, place_ref, back_ref, mix_ref):
     width = rows_ref.shape[1]
-    own_class = class_ref[0]
+    own_block, own_class = here_ref[0], here_ref[1]
     received = received_ref[...].reshape(BLOCKS * PER_CLASS, width + META)
     slots = received.shape[0]
     row = lax.broadcasted_iota(jnp.int32, (slots, slots), 0)
     column = lax.broadcasted_iota(jnp.int32, (slots, slots), 1)
-    earlier = (column // PER_CLASS < row // PER_CLASS) & (column % PER_CLASS == 0)
-    earlier = earlier.astype(jnp.float32).astype(jnp.bfloat16)
+    earlier = flags((column // PER_CLASS < row // PER_CLASS) & (column % PER_CLASS == 0))
 
     def earlier_sum(counts):
         return jnp.dot(earlier, counts, preferred_element_type=jnp.float32).astype(jnp.int32)
 
-    counts = received[:, width:]
-    named = counts.astype(jnp.float32).astype(jnp.int32)
-    kept = jnp.clip(CAPACITY - earlier_sum(counts), 0, named)
+    all_counts = received[:, width:]
+    own_expert = own_block // (BLOCKS // EXPERTS)
+    counts = jnp.dot(
+        all_counts,
+        flags(lax.broadcasted_iota(jnp.int32, (META, META), 0) == own_expert),
+        preferred_element_type=jnp.float32,
+    )
+    named = counts.astype(jnp.int32)
+    offset = earlier_sum(counts.astype(jnp.bfloat16))
+    kept = jnp.clip(CAPACITY - offset, 0, named)
     line = lax.broadcasted_iota(jnp.int32, named.shape, 0)
+    lane = lax.broadcasted_iota(jnp.int32, named.shape, 1)
     block, place = line // PER_CLASS, line % PER_CLASS
-    shift = (own_class + BLOCKS - block) % CLASSES
-    in_class = (kept - shift + CLASSES - 1) // CLASSES
-    first = earlier_sum(in_class.astype(jnp.float32).astype(jnp.bfloat16))
-    spot = jnp.where(place < in_class, first + place, -1)
-    chosen = spot == lax.broadcasted_iota(jnp.int32, named.shape, 1)
-    chosen = chosen.astype(jnp.float32).astype(jnp.bfloat16)
-    place_ref[...] = chosen
+
+    def class_order(of_class):
+        shift = (of_class + BLOCKS - block) % CLASSES
+        in_class = (kept - shift + CLASSES - 1) // CLASSES
+        first = earlier_sum(in_class.astype(jnp.float32).astype(jnp.bfloat16))
+        live = place < in_class
+        slot = jnp.where(live, offset + place * CLASSES + shift + 1, 0)
+        return flags((first + place == lane) & live), slot
+
+    chosen, _ = class_order(own_class)
     rows = lax.dot_general(
         chosen, received[:, :width], (((0,), (0,)), ((), ())), preferred_element_type=jnp.float32
     )
-    rows_ref[...] = rows[: rows_ref.shape[0]].astype(jnp.bfloat16)
-
-
-def compacted(received, own_class):
+    rows_ref[...] = rows[:CLASS_ROWS].astype(jnp.bfloat16)
+
+    for c in range(CLASSES):
+        chosen, slot = class_order(c)
+        digits = jnp.where(lane < META // 2, slot // 16, slot % 16).astype(jnp.float32).astype(jnp.bfloat16)
+        found = lax.dot_general(chosen, digits, (((0,), (0,)), ((), ())), preferred_element_type=jnp.float32)
+        found = found[:CLASS_ROWS, :1] * 16.0 + found[:CLASS_ROWS, META // 2 : META // 2 + 1]
+        found = found.astype(jnp.int32) - 1
+        target = jnp.where(found < 0, -1, found % CLASSES * SLOT_ROWS + found // CLASSES)
+        place_ref[c * CLASS_ROWS : (c + 1) * CLASS_ROWS] = flags(
+            target == lax.broadcasted_iota(jnp.int32, (CLASS_ROWS, ROWS), 1)
+        )
+
+    rank = place * CLASSES + (own_class + CLASSES * BLOCKS * SRC_CAP - offset) % CLASSES
+    back_ref[...] = flags(((offset + rank - own_class) // CLASSES == lane) & (rank < kept))
+
+    ids = ids_ref[...]
+    names, rank, _ = ranks(ids)
+    offsets = lax.dot_general(
+        all_counts,
+        flags((block < own_block) & (place == 0)),
+        (((0,), (0,)), ((), ())),
+        preferred_element_type=jnp.float32,
+    )[:EXPERTS, :TOKENS]
+    mix = jnp.zeros(mix_ref.shape, jnp.float32)
+    for k in range(TOPK):
+        turn = jnp.sum(offsets * names[k], axis=0, keepdims=True).astype(jnp.int32)
+        mix = jnp.where(
+            slot_iota() == packet_place(ids[k : k + 1], rank[k], turn), weights_ref[k : k + 1], mix
+        )
+    mix_ref[...] = mix
+
+
+def compacted(received, own_block, own_class, expert_ids, expert_weights):
     blocks, places, wide = received.shape
     return pl.pallas_call(
         compact_kernel,
         in_specs=[
             pl.BlockSpec(memory_space=pltpu.SMEM),
             pl.BlockSpec(memory_space=pltpu.VMEM),
+            pl.BlockSpec(memory_space=pltpu.VMEM),
+            pl.BlockSpec(memory_space=pltpu.VMEM),
         ],
         out_shape=[
             jax.ShapeDtypeStruct((CLASS_ROWS, wide - META), jnp.bfloat16),
+            jax.ShapeDtypeStruct((CLASSES * CLASS_ROWS, ROWS), jnp.bfloat16),
             jax.ShapeDtypeStruct((blocks * places, META), jnp.bfloat16),
+            jax.ShapeDtypeStruct((EXPERTS * SRC_CAP, TOKENS), jnp.float32),
         ],
         compiler_params=pltpu.CompilerParams(vmem_limit_bytes=10 << 20),
         name="compacted",
-    )(own_class.reshape(1), received)
+    )(jnp.stack([own_block, own_class]), expert_ids.T, expert_weights.T, received)
 
 
 def shards(
@@ -307,24 +377,21 @@
     block = ((lax.axis_index("x") * 2 + lax.axis_index("zh")) * 2 + lax.axis_index("zq")) * 4 + lax.axis_index("zn")
     own_class = lax.axis_index("zn")
 
-    summed, outgoing, mix_rows = tokens_packed(
-        block, lengths, expert_ids, expert_weights, residual, queries, keys, values
-    )
+    summed, outgoing = tokens_packed(block, lengths, expert_ids, residual, queries, keys, values)
     gained = (w_in.astype(jnp.float32) * norm_gain.astype(jnp.float32)[:, None]).astype(jnp.bfloat16)
     received = lax.all_to_all(outgoing, DP, split_axis=0, concat_axis=0, tiled=True)
-    class_rows, chosen = compacted(received, own_class)
+    class_rows, place, back, mix_rows = compacted(received, block, own_class, expert_ids, expert_weights)
     rows = lax.all_gather(class_rows, "zn", axis=0, tiled=True)
-    send, own = hidden_pieces(rows, gained, lax.axis_index("core"))
+    send, own = hidden_pieces(place, rows, gained, lax.axis_index("core"))
     other = lax.ppermute(send, "core", ((0, 1), (1, 0)))
     pieces = lax.all_to_all(core_summed(own, other), "y", split_axis=0, concat_axis=0, tiled=True)
     gathered = lax.all_to_all(silu_copies(pieces), "y", split_axis=0, concat_axis=0, tiled=True)
     gathered = lax.all_gather(gathered, "core", axis=0, tiled=True)
-    hidden = jnp.moveaxis(gathered, 0, 1).reshape(ROWS, 8 * UNIT)
-    results = jnp.dot(hidden, w_out, preferred_element_type=jnp.float32).astype(jnp.bfloat16)
-
-    class_out = summed_at_owner(results.reshape(CLASSES, CLASS_ROWS, width), "zn").astype(jnp.bfloat16)
+    results = output_parts(gathered, w_out)
+
+    class_out = summed_at_owner(results.reshape(CLASSES, SLOT_ROWS, width), "zn").astype(jnp.bfloat16)
     returned = jnp.dot(
-        chosen[:, :CLASS_ROWS], class_out, preferred_element_type=jnp.float32
+        back[:, :SLOT_ROWS], class_out, preferred_element_type=jnp.float32
     ).astype(jnp.bfloat16)
     combined = lax.all_to_all(
         returned.reshape(BLOCKS, PER_CLASS, width), DP, split_axis=0, concat_axis=0, tiled=True

time: 161 us -> 157 us (0.975)
  blocking collectives: 99.7 us -> 94.9 us
  Pallas kernels: 6.87 us -> 9.05 us
    all_to_all x1, blocking collectives: 22.2 us -> 19 us  [summed_at_owner(): lax.all_to_all(pieces, axis, split_axis=0, concat_axis=0, tiled=True)]
where the time goes in v6:
time: 157 us
  blocking collectives  94.9 us (60%)
  waiting for transfers between devices  28.7 us (18%)
  starting transfers between devices  20.7 us (13%)
  Pallas kernels  9.05 us (6%)
  other arithmetic  1.98 us (1%)
    all_to_all x1, blocking collectives, shards(): lax.all_to_all(returned.reshape(BLOCKS, PER_CLASS, width), DP, split_axis...  33.3 us
    all_to_all x1, waiting for transfers between devices, shards(): lax.all_to_all(outgoing, DP, split_axis=0, concat_axis=0, tiled=True)  27 us
    all_to_all x1, blocking collectives, summed_at_owner(): lax.all_to_all(pieces, axis, split_axis=0, concat_axis=0, tiled=True)  19 us
    all_to_all x1, starting transfers between devices, shards(): lax.all_to_all(outgoing, DP, split_axis=0, concat_axis=0, tiled=True)  18.8 us
    all_gather x1, blocking collectives, shards(): rows = lax.all_gather(class_rows, 'zn', axis=0, tiled=True)  17.4 us
    all_to_all x1, blocking collectives, shards(): lax.all_to_all(core_summed(own, other), 'y', split_axis=0, concat_axis=0,...  12.8 us
    all_to_all x1, blocking collectives, shards(): lax.all_to_all(silu_copies(pieces), 'y', split_axis=0, concat_axis=0, til...  10 us
    pallas_call x1, Pallas kernels, tokens_packed(): pl.pallas_call(tokens_kernel, grid=(TOKENS // STEP,), in_specs=[pl.BlockS...  3.57 us
  transfers between devices with their start and end apart: 2, of which 2 were waited for; matrix products, arithmetic and copies ran while one was open for 1% of the time, Pallas kernels for 0%

profile of v6, /device:TPU:6, one launch (start us, length us, event | category | flops | bytes accessed | tf_op | source)
XLA Modules:
  0.0 156.8 jit_solution(6902495419127264059)
XLA Ops:
  0.0 0.0 copy-start.3
  0.0 3.6 %tokens_packed.1 = (f32[32,768]{1,0:T(8,128)S(1)}, bf16[64,4,896]{2,1,0:T(4,128)(2,1)}) custom-call(s32[1]{0:T(128)} %bitcast.block_ref, s32[32]{0:T(128)} %lengths_ref.1, s32[2,32]{1,0:T(2,128)} %bitcast.11, bf16[32,768]{1,0:T(8,128)(2,1)} %residual_ref.1, bf16[32,768]{1,0:T(8,128)(2,1)} %queries_ref.1, bf16[32,128,128]{2,1,0:T(8,128)(2,1)} %keys_ref.1, ...), custom_call_target="tpu_custom_call" | custom-call | tf_op jit(solution)/shard_map/tokens_packed/pallas_call | solution.py:124
  3.6 18.8 %all-to-all-start = ((bf16[64,4,896]{2,1,0:T(4,128)(2,1)}), bf16[64,4,896]{2,1,0:T(4,128)(2,1)S(1)}, u32[]{:S(2)}, u32[]{:S(2)}) async-start(bf16[64,4,896]{2,1,0:T(4,128)(2,1)} %get-tuple-element.14), calls=%async_computation | async-start | bytes 917504 | tf_op jit(solution)/shard_map/all_to_all | solution.py:382
  22.4 0.0 copy-done.3
  22.4 0.1 pad_add_fusion.here_ref
  22.5 0.0 copy-start.1
  22.5 0.0 copy-start.2
  22.5 1.8 %multiply_convert_fusion.w_ref = bf16[768,1024]{1,0:T(8,128)(2,1)S(1)} fusion(bf16[768,1024]{1,0:T(8,128)(2,1)} %param.18, f32[768]{0:T(1024)S(1)} %convert_element_type.24), kind=kLoop, calls=%fused_computation | loop fusion | flops 2359296 | bytes 3148800 | tf_op jit(solution)/shard_map/convert_element_type | solution.py:381
  24.2 27.0 %all-to-all-done.received_ref = bf16[64,4,896]{2,1,0:T(4,128)(2,1)S(1)} async-done(((bf16[64,4,896]{2,1,0:T(4,128)(2,1)}), bf16[64,4,896]{2,1,0:T(4,128)(2,1)S(1)}, u32[]{:S(2)}, u32[]{:S(2)}) %all-to-all-start) | async-done | bytes 458784 | tf_op jit(solution)/shard_map/all_to_all | solution.py:382
  51.2 0.0 copy-done.1
  51.2 0.0 copy-done.2
  51.2 3.3 %compacted.1 = (bf16[120,768]{1,0:T(8,128)(2,1)S(1)}, bf16[480,384]{1,0:T(8,128)(2,1)S(1)}, bf16[256,128]{1,0:T(8,128)(2,1)S(1)}, f32[128,32]{1,0:T(8,128)S(1)}) custom-call(s32[2]{0:T(128)S(1)} %pad_add_fusion.here_ref, s32[2,32]{1,0:T(2,128)S(1)} %bitcast.12, f32[2,32]{1,0:T(2,128)S(1)} %bitcast.13, bf16[64,4,896]{2,1,0:T(4,128)(2,1)S(1)} %all-to-all-done.received_ref), custom_call_target="tpu_custom_call" | custom-call | tf_op jit(solution)/shard_map/compacted/pallas_call | solution.py:354
  54.5 17.4 %all_gather.6.gathered_ref = bf16[480,768]{1,0:T(8,128)(2,1)S(1)} all-gather(bf16[120,768]{1,0:T(8,128)(2,1)S(1)} %get-tuple-element.18), channel_id=1, replica_groups=mesh['x'=4,'zh'=2,'zq'=2,'zn'=4,'y'=4,'core'=2] {'zn'}, dimensions={0}, use_global_device_ids=true | all-gather | bytes 921600 | tf_op jit(solution)/shard_map/all_gather | solution.py:384
  71.9 1.1 hidden_pieces.1
  73.1 1.9 %collective-permute-start = (bf16[4,400,128]{2,1,0:T(8,128)(2,1)S(1)}, bf16[4,400,128]{2,1,0:T(8,128)(2,1)S(1)}, u32[]{:S(2)}, u32[]{:S(2)}) collective-permute-start(bf16[4,400,128]{2,1,0:T(8,128)(2,1)S(1)} %get-tuple-element.20), channel_id=1, source_target_pairs={{0,1},{1,0},{2,3},{3,2},{4,5},{5,4},{6,7},{7,6},{8,9},{9,8},{10,11... | collective-permute-start | bytes 1228808 | tf_op jit(solution)/shard_map/ppermute | solution.py:386
  75.0 1.7 %collective-permute-done.other_ref = bf16[4,400,128]{2,1,0:T(8,128)(2,1)S(1)} collective-permute-done((bf16[4,400,128]{2,1,0:T(8,128)(2,1)S(1)}, bf16[4,400,128]{2,1,0:T(8,128)(2,1)S(1)}, u32[]{:S(2)}, u32[]{:S(2)}) %collective-permute-start) | collective-permute-done | bytes 409632 | tf_op jit(solution)/shard_map/ppermute | solution.py:386
  76.7 0.1 core_summed.1
  76.8 12.8 %all_to_all.25.in_ref = bf16[4,400,128]{2,1,0:T(8,128)(2,1)S(1)} all-to-all(bf16[4,400,128]{2,1,0:T(8,128)(2,1)S(1)} %core_summed.1), channel_id=1, replica_groups=mesh['x'=4,'zh'=2,'zq'=2,'zn'=4,'y'=4,'core'=2] {'y'}, dimensions={0} | all-to-all | bytes 819200 | tf_op jit(solution)/shard_map/all_to_all | solution.py:387
  89.6 0.0 copy-start
  89.6 0.2 silu_copies.1
  89.8 10.0 %all_to_all.26 = bf16[4,384,128]{2,1,0:T(8,128)(2,1)S(1)} all-to-all(bf16[4,384,128]{2,1,0:T(8,128)(2,1)S(1)} %silu_copies.1), channel_id=1, replica_groups=mesh['x'=4,'zh'=2,'zq'=2,'zn'=4,'y'=4,'core'=2] {'y'}, dimensions={0} | all-to-all | bytes 786432 | tf_op jit(solution)/shard_map/all_to_all | solution.py:388
  99.8 2.4 %all_gather.7.hidden_ref = bf16[8,384,128]{2,1,0:T(8,128)(2,1)S(1)} all-gather(bf16[4,384,128]{2,1,0:T(8,128)(2,1)S(1)} %all_to_all.26), channel_id=1, replica_groups=mesh['x'=4,'zh'=2,'zq'=2,'zn'=4,'y'=4,'core'=2] {'core'}, dimensions={0}, use_global_device_ids=true | all-gather | bytes 1179648 | tf_op jit(solution)/shard_map/all_gather | solution.py:389
  102.2 0.0 copy-done
  102.2 0.8 output_parts.1
  103.0 19.0 %all_to_all.27 = bf16[4,96,768]{2,1,0:T(8,128)(2,1)S(1)} all-to-all(bf16[4,96,768]{2,1,0:T(8,128)(2,1)S(1)} %bitcast.10), channel_id=1, replica_groups=mesh['x'=4,'zh'=2,'zq'=2,'zn'=4,'y'=4,'core'=2] {'zn'}, dimensions={0} | all-to-all | bytes 1179648 | tf_op jit(solution)/shard_map/all_to_all | solution.py:162
  122.0 0.1 reduce_sum.21
  122.1 0.2 convolution_convert_fusion
  122.3 0.1 reshape.22
  122.4 33.3 %all_to_all.28 = bf16[64,4,768]{2,1,0:T(4,128)(2,1)S(1)} all-to-all(bf16[64,4,768]{2,1,0:T(4,128)(2,1)S(1)} %reshape.22), channel_id=1, replica_groups=mesh['x'=4,'zh'=2,'zq'=2,'zn'=4,'y'=4,'core'=2] {'x','zh','zq','zn'}, dimensions={0} | all-to-all | bytes 786432 | tf_op jit(solution)/shard_map/all_to_all | solution.py:396
  155.7 0.1 reshape.24
  155.8 0.1 reduce_sum.22
  155.8 1.0 fusion
  (1 shorter events, 0.0 us)
Async XLA Ops:
  0.0 22.4 %copy-start.3 = (bf16[768]{0:T(1024)(128)(2,1)S(1)}, bf16[768]{0:T(1024)(128)(2,1)}, u32[]{:S(2)}) copy-start(bf16[768]{0:T(1024)(128)(2,1)} %param.15) | copy-start | bytes 4612
  3.6 47.7 %all-to-all-start = ((bf16[64,4,896]{2,1,0:T(4,128)(2,1)}), bf16[64,4,896]{2,1,0:T(4,128)(2,1)S(1)}, u32[]{:S(2)}, u32[]{:S(2)}) async-start(bf16[64,4,896]{2,1,0:T(4,128)(2,1)} %get-tuple-element.14), calls=%async_computation | async-start | bytes 917504 | tf_op jit(solution)/shard_map/all_to_all | solution.py:382
  22.5 28.8 %copy-start.1 = (s32[32,2]{0,1:T(2,128)S(1)}, s32[32,2]{0,1:T(2,128)}, u32[]{:S(2)}) copy-start(s32[32,2]{0,1:T(2,128)} %param.16) | copy-start | bytes 772
  22.5 28.8 %copy-start.2 = (f32[32,2]{0,1:T(2,128)S(1)}, f32[32,2]{0,1:T(2,128)}, u32[]{:S(2)}) copy-start(f32[32,2]{0,1:T(2,128)} %param.17) | copy-start | bytes 772
  73.1 3.6 %collective-permute-start = (bf16[4,400,128]{2,1,0:T(8,128)(2,1)S(1)}, bf16[4,400,128]{2,1,0:T(8,128)(2,1)S(1)}, u32[]{:S(2)}, u32[]{:S(2)}) collective-permute-start(bf16[4,400,128]{2,1,0:T(8,128)(2,1)S(1)} %get-tuple-element.20), channel_id=1, source_target_pairs={{0,1},{1,0},{2,3},{3,2},{4,5},{5,4},{6,7},{7,6},{8,9},{9,8},{10,11... | collective-permute-start | bytes 1228808 | tf_op jit(solution)/shard_map/ppermute | solution.py:386
  89.6 12.6 %copy-start = (bf16[1024,768]{1,0:T(8,128)(2,1)S(1)}, bf16[1024,768]{1,0:T(8,128)(2,1)}, u32[]{:S(2)}) copy-start(bf16[1024,768]{1,0:T(8,128)(2,1)} %w_ref.1) | copy-start | bytes 4718596

commit v7 on v6

--- a/solution.py
+++ b/solution.py
@@ -173,11 +173,27 @@
     return jnp.concatenate([leading, (sums - leading.astype(jnp.float32)).astype(jnp.bfloat16)], axis=0)
 
 
-def hidden_kernel(core_ref, place_ref, gathered_ref, w_ref, send_ref, keep_ref):
+def write_pieces(rows, squares, w_ref, half, out_ref):
+    columns = 2 * UNIT
+    for k in range(2):
+        source = (half * 2 + k) * columns
+        parts = jnp.dot(
+            rows,
+            w_ref[:, pl.ds(pl.multiple_of(source, columns), columns)],
+            preferred_element_type=jnp.float32,
+        )
+        for side in range(2):
+            piece = k * 2 + side
+            out_ref[piece, :ROWS] = parts[:, side * UNIT : (side + 1) * UNIT].astype(jnp.bfloat16)
+            out_ref[piece, ROWS:] = squares
+
+
+def sent_kernel(core_ref, place_ref, gathered_ref, w_ref, send_ref, rows_ref, squares_ref):
     wide = lax.dot_general(
         place_ref[...], gathered_ref[...], (((0,), (0,)), ((), ())), preferred_element_type=jnp.float32
     )
     rows = wide.astype(jnp.bfloat16)
+    rows_ref[...] = rows
     sums = jnp.sum(wide * wide, axis=1, keepdims=True)
     lines = [
         jnp.sum(jnp.where(diagonal(), sums[g * UNIT : (g + 1) * UNIT], 0.0), axis=0, keepdims=True)
@@ -185,37 +201,42 @@
     ]
     lines.append(jnp.zeros((SQUARES // 2 - LINES, UNIT), jnp.float32))
     squares = leading_and_rest(jnp.concatenate(lines, axis=0))
-
-    columns = 2 * UNIT
-    for k in range(4):
-        out_ref = send_ref if k < 2 else keep_ref
-        source = (k + 2 - 2 * core_ref[0]) % 4 * columns
-        parts = jnp.dot(
-            rows,
-            w_ref[:, pl.ds(pl.multiple_of(source, columns), columns)],
-            preferred_element_type=jnp.float32,
-        )
-        for half in range(2):
-            piece = k % 2 * 2 + half
-            out_ref[piece, :ROWS] = parts[:, half * UNIT : (half + 1) * UNIT].astype(jnp.bfloat16)
-            out_ref[piece, ROWS:] = squares
-
-
-def hidden_pieces(place, gathered, w_in, core):
-    units = w_in.shape[1]
-    half = jax.ShapeDtypeStruct((units // (2 * UNIT), ROWS + SQUARES, UNIT), jnp.bfloat16)
-    return pl.pallas_call(
-        hidden_kernel,
+    squares_ref[...] = squares
+    write_pieces(rows, squares, w_ref, 1 - core_ref[0], send_ref)
+
+
+def kept_kernel(core_ref, rows_ref, squares_ref, w_ref, keep_ref):
+    write_pieces(rows_ref[...], squares_ref[...], w_ref, core_ref[0], keep_ref)
+
+
+def first_product(kernel, name, out_shape, core, *operands):
+    return pl.pallas_call(
+        kernel,
         in_specs=[
             pl.BlockSpec(memory_space=pltpu.SMEM),
-            pl.BlockSpec(memory_space=pltpu.VMEM),
-            pl.BlockSpec(memory_space=pltpu.VMEM),
-            pl.BlockSpec(memory_space=pltpu.VMEM),
-        ],
-        out_shape=[half, half],
-        compiler_params=pltpu.CompilerParams(vmem_limit_bytes=10 << 20),
-        name="hidden_pieces",
-    )(core.reshape(1), place, gathered, w_in)
+            *[pl.BlockSpec(memory_space=pltpu.VMEM)] * len(operands),
+        ],
+        out_shape=out_shape,
+        compiler_params=pltpu.CompilerParams(vmem_limit_bytes=10 << 20),
+        name=name,
+    )(core.reshape(1), *operands)
+
+
+def half_of_units(w_in):
+    return jax.ShapeDtypeStruct((w_in.shape[1] // (2 * UNIT), ROWS + SQUARES, UNIT), jnp.bfloat16)
+
+
+def sent_pieces(place, gathered, w_in, core):
+    out_shape = [
+        half_of_units(w_in),
+        jax.ShapeDtypeStruct((ROWS, gathered.shape[1]), jnp.bfloat16),
+        jax.ShapeDtypeStruct((SQUARES, UNIT), jnp.bfloat16),
+    ]
+    return first_product(sent_kernel, "sent_pieces", out_shape, core, place, gathered, w_in)
+
+
+def kept_pieces(rows, squares, w_in, core):
+    return first_product(kept_kernel, "kept_pieces", half_of_units(w_in), core, rows, squares, w_in)
 
 
 def core_kernel(own_ref, other_ref, out_ref):
@@ -278,11 +299,8 @@
     return condition.astype(jnp.float32).astype(jnp.bfloat16)
 
 
-def compact_kernel(here_ref, ids_ref, weights_ref, received_ref, rows_ref, place_ref, back_ref, mix_ref):
-    width = rows_ref.shape[1]
-    own_block, own_class = here_ref[0], here_ref[1]
-    received = received_ref[...].reshape(BLOCKS * PER_CLASS, width + META)
-    slots = received.shape[0]
+def kept_of_blocks(all_counts, own_block):
+    slots = all_counts.shape[0]
     row = lax.broadcasted_iota(jnp.int32, (slots, slots), 0)
     column = lax.broadcasted_iota(jnp.int32, (slots, slots), 1)
     earlier = flags((column // PER_CLASS < row // PER_CLASS) & (column % PER_CLASS == 0))
@@ -290,18 +308,24 @@
     def earlier_sum(counts):
         return jnp.dot(earlier, counts, preferred_element_type=jnp.float32).astype(jnp.int32)
 
-    all_counts = received[:, width:]
     own_expert = own_block // (BLOCKS // EXPERTS)
     counts = jnp.dot(
         all_counts,
         flags(lax.broadcasted_iota(jnp.int32, (META, META), 0) == own_expert),
         preferred_element_type=jnp.float32,
     )
-    named = counts.astype(jnp.int32)
     offset = earlier_sum(counts.astype(jnp.bfloat16))
-    kept = jnp.clip(CAPACITY - offset, 0, named)
-    line = lax.broadcasted_iota(jnp.int32, named.shape, 0)
-    lane = lax.broadcasted_iota(jnp.int32, named.shape, 1)
+    return offset, jnp.clip(CAPACITY - offset, 0, counts.astype(jnp.int32)), earlier_sum
+
+
+def compact_kernel(here_ref, received_ref, rows_ref, place_ref, counts_ref):
+    width = rows_ref.shape[1]
+    received = received_ref[...].reshape(BLOCKS * PER_CLASS, width + META)
+    all_counts = received[:, width:]
+    counts_ref[...] = all_counts
+    offset, kept, earlier_sum = kept_of_blocks(all_counts, here_ref[0])
+    line = lax.broadcasted_iota(jnp.int32, kept.shape, 0)
+    lane = lax.broadcasted_iota(jnp.int32, kept.shape, 1)
     block, place = line // PER_CLASS, line % PER_CLASS
 
     def class_order(of_class):
@@ -312,7 +336,7 @@
         slot = jnp.where(live, offset + place * CLASSES + shift + 1, 0)
         return flags((first + place == lane) & live), slot
 
-    chosen, _ = class_order(own_class)
+    chosen, _ = class_order(here_ref[1])
     rows = lax.dot_general(
         chosen, received[:, :width], (((0,), (0,)), ((), ())), preferred_element_type=jnp.float32
     )
@@ -329,6 +353,32 @@
             target == lax.broadcasted_iota(jnp.int32, (CLASS_ROWS, ROWS), 1)
         )
 
+
+def compacted(received, own_block, own_class):
+    blocks, places, wide = received.shape
+    return pl.pallas_call(
+        compact_kernel,
+        in_specs=[
+            pl.BlockSpec(memory_space=pltpu.SMEM),
+            pl.BlockSpec(memory_space=pltpu.VMEM),
+        ],
+        out_shape=[
+            jax.ShapeDtypeStruct((CLASS_ROWS, wide - META), jnp.bfloat16),
+            jax.ShapeDtypeStruct((CLASSES * CLASS_ROWS, ROWS), jnp.bfloat16),
+            jax.ShapeDtypeStruct((blocks * places, META), jnp.bfloat16),
+        ],
+        compiler_params=pltpu.CompilerParams(vmem_limit_bytes=10 << 20),
+        name="compacted",
+    )(jnp.stack([own_block, own_class]), received)
+
+
+def back_kernel(here_ref, ids_ref, weights_ref, counts_ref, back_ref, mix_ref):
+    own_block, own_class = here_ref[0], here_ref[1]
+    all_counts = counts_ref[...]
+    offset, kept, _ = kept_of_blocks(all_counts, own_block)
+    line = lax.broadcasted_iota(jnp.int32, kept.shape, 0)
+    lane = lax.broadcasted_iota(jnp.int32, kept.shape, 1)
+    block, place = line // PER_CLASS, line % PER_CLASS
     rank = place * CLASSES + (own_class + CLASSES * BLOCKS * SRC_CAP - offset) % CLASSES
     back_ref[...] = flags(((offset + rank - own_class) // CLASSES == lane) & (rank < kept))
 
@@ -340,19 +390,24 @@
         (((0,), (0,)), ((), ())),
         preferred_element_type=jnp.float32,
     )[:EXPERTS, :TOKENS]
-    mix = jnp.zeros(mix_ref.shape, jnp.float32)
+    mix = jnp.zeros((EXPERTS * SRC_CAP, TOKENS), jnp.float32)
     for k in range(TOPK):
         turn = jnp.sum(offsets * names[k], axis=0, keepdims=True).astype(jnp.int32)
         mix = jnp.where(
             slot_iota() == packet_place(ids[k : k + 1], rank[k], turn), weights_ref[k : k + 1], mix
         )
-    mix_ref[...] = mix
-
-
-def compacted(received, own_block, own_class, expert_ids, expert_weights):
-    blocks, places, wide = received.shape
-    return pl.pallas_call(
-        compact_kernel,
+    for part in range(3):
+        rounded = mix.astype(jnp.bfloat16)
+        for e in range(EXPERTS):
+            for group in range(2):
+                first = (e * 2 + group) * SRC_CAP
+                mix_ref[part, first : first + SRC_CAP] = rounded[e * SRC_CAP : (e + 1) * SRC_CAP]
+        mix = mix - rounded.astype(jnp.float32)
+
+
+def way_back(counts, own_block, own_class, expert_ids, expert_weights):
+    return pl.pallas_call(
+        back_kernel,
         in_specs=[
             pl.BlockSpec(memory_space=pltpu.SMEM),
             pl.BlockSpec(memory_space=pltpu.VMEM),
@@ -360,14 +415,32 @@
             pl.BlockSpec(memory_space=pltpu.VMEM),
         ],
         out_shape=[
-            jax.ShapeDtypeStruct((CLASS_ROWS, wide - META), jnp.bfloat16),
-            jax.ShapeDtypeStruct((CLASSES * CLASS_ROWS, ROWS), jnp.bfloat16),
-            jax.ShapeDtypeStruct((blocks * places, META), jnp.bfloat16),
-            jax.ShapeDtypeStruct((EXPERTS * SRC_CAP, TOKENS), jnp.float32),
-        ],
-        compiler_params=pltpu.CompilerParams(vmem_limit_bytes=10 << 20),
-        name="compacted",
-    )(jnp.stack([own_block, own_class]), expert_ids.T, expert_weights.T, received)
+            jax.ShapeDtypeStruct(counts.shape, jnp.bfloat16),
+            jax.ShapeDtypeStruct((3, 2 * EXPERTS * SRC_CAP, TOKENS), jnp.bfloat16),
+        ],
+        compiler_params=pltpu.CompilerParams(vmem_limit_bytes=10 << 20),
+        name="way_back",
+    )(jnp.stack([own_block, own_class]), expert_ids.T, expert_weights.T, counts)
+
+
+def final_kernel(summed_ref, combined_ref, mix_ref, out_ref):
+    total = summed_ref[...]
+    rows = combined_ref[...].reshape(BLOCKS * PER_CLASS, total.shape[1])
+    for part in (2, 1, 0):
+        total = total + lax.dot_general(
+            mix_ref[part], rows, (((0,), (0,)), ((), ())), preferred_element_type=jnp.float32
+        )
+    out_ref[...] = total.astype(jnp.bfloat16)
+
+
+def final_rows(summed, combined, mix):
+    return pl.pallas_call(
+        final_kernel,
+        in_specs=[pl.BlockSpec(memory_space=pltpu.VMEM)] * 3,
+        out_shape=jax.ShapeDtypeStruct(summed.shape, jnp.bfloat16),
+        compiler_params=pltpu.CompilerParams(vmem_limit_bytes=10 << 20),
+        name="final_rows",
+    )(summed, combined, mix)
 
 
 def shards(
@@ -380,10 +453,15 @@
     summed, outgoing = tokens_packed(block, lengths, expert_ids, residual, queries, keys, values)
     gained = (w_in.astype(jnp.float32) * norm_gain.astype(jnp.float32)[:, None]).astype(jnp.bfloat16)
     received = lax.all_to_all(outgoing, DP, split_axis=0, concat_axis=0, tiled=True)
-    class_rows, place, back, mix_rows = compacted(received, block, own_class, expert_ids, expert_weights)
+    class_rows, place, counts = compacted(received, block, own_class)
     rows = lax.all_gather(class_rows, "zn", axis=0, tiled=True)
-    send, own = hidden_pieces(place, rows, gained, lax.axis_index("core"))
+    core = lax.axis_index("core")
+    send, rows, squares = sent_pieces(place, rows, gained, core)
     other = lax.ppermute(send, "core", ((0, 1), (1, 0)))
+    own = kept_pieces(rows, squares, gained, core)
+    counts, squares = lax.optimization_barrier((counts, squares))
+    back, mix = way_back(counts, block, own_class, expert_ids, expert_weights)
+    own, back, mix = lax.optimization_barrier((own, back, mix))
     pieces = lax.all_to_all(core_summed(own, other), "y", split_axis=0, concat_axis=0, tiled=True)
     gathered = lax.all_to_all(silu_copies(pieces), "y", split_axis=0, concat_axis=0, tiled=True)
     gathered = lax.all_gather(gathered, "core", axis=0, tiled=True)
@@ -396,11 +474,7 @@
     combined = lax.all_to_all(
         returned.reshape(BLOCKS, PER_CLASS, width), DP, split_axis=0, concat_axis=0, tiled=True
     )
-    per_expert = jnp.sum(
-        combined.reshape(EXPERTS, 2, SRC_CAP, width).astype(jnp.float32), axis=1
-    ).reshape(EXPERTS * SRC_CAP, width)
-    addition = jnp.einsum("st,sd->td", mix_rows, per_expert, precision=lax.Precision.HIGHEST)
-    return (summed + addition).astype(jnp.bfloat16)
+    return final_rows(summed, combined, mix)
 
 
 def solution(mesh):

time: 157 us -> 157 us (level)
  Pallas kernels: 9.05 us -> 11.3 us
  waiting for transfers between devices: 28.7 us -> 27.1 us
    pallas_call x1 -> x4, Pallas kernels: 1.15 us -> 3.42 us  [the longest x2 1.32 us: first_product(): pl.pallas_call(kernel, in_specs=[pl.BlockSpec(memory_space=pltpu.SMEM), *...]
    ppermute x1, waiting for transfers between devices: 1.71 us -> 0.07 us  [shards(): other = lax.ppermute(send, 'core', ((0, 1), (1, 0)))]
  transfers between devices with their start and end apart: 2 -> 2, of which waited for: 2 -> 2; matrix products, arithmetic and copies ran while one was open for 1% -> 1% of each run, Pallas kernels for 0% -> 1%
where the time goes in v7:
time: 157 us
  blocking collectives  95.5 us (61%)
  waiting for transfers between devices  27.1 us (17%)
  starting transfers between devices  20.7 us (13%)
  Pallas kernels  11.3 us (7%)
  other arithmetic  1.9 us (1%)
    all_to_all x1, blocking collectives, shards(): lax.all_to_all(returned.reshape(BLOCKS, PER_CLASS, width), DP, split_axis...  33.3 us
    all_to_all x1, waiting for transfers between devices, shards(): lax.all_to_all(outgoing, DP, split_axis=0, concat_axis=0, tiled=True)  27 us
    all_to_all x1, blocking collectives, summed_at_owner(): lax.all_to_all(pieces, axis, split_axis=0, concat_axis=0, tiled=True)  19 us
    all_to_all x1, starting transfers between devices, shards(): lax.all_to_all(outgoing, DP, split_axis=0, concat_axis=0, tiled=True)  18.8 us
    all_gather x1, blocking collectives, shards(): rows = lax.all_gather(class_rows, 'zn', axis=0, tiled=True)  17.4 us
    all_to_all x1, blocking collectives, shards(): lax.all_to_all(core_summed(own, other), 'y', split_axis=0, concat_axis=0,...  13.1 us
    all_to_all x1, blocking collectives, shards(): lax.all_to_all(silu_copies(pieces), 'y', split_axis=0, concat_axis=0, til...  10.3 us
    pallas_call x1, Pallas kernels, tokens_packed(): pl.pallas_call(tokens_kernel, grid=(TOKENS // STEP,), in_specs=[pl.BlockS...  3.57 us
  transfers between devices with their start and end apart: 2, of which 2 were waited for; matrix products, arithmetic and copies ran while one was open for 1% of the time, Pallas kernels for 1%

profile of v7, /device:TPU:6, one launch (start us, length us, event | category | flops | bytes accessed | tf_op | source)
XLA Modules:
  0.0 157.0 jit_solution(21988416555599408)
XLA Ops:
  0.0 0.0 copy-start.3
  0.0 3.6 %tokens_packed.1 = (f32[32,768]{1,0:T(8,128)S(1)}, bf16[64,4,896]{2,1,0:T(4,128)(2,1)}) custom-call(s32[1]{0:T(128)} %bitcast.block_ref, s32[32]{0:T(128)} %lengths_ref.1, s32[2,32]{1,0:T(2,128)} %bitcast.8, bf16[32,768]{1,0:T(8,128)(2,1)} %residual_ref.1, bf16[32,768]{1,0:T(8,128)(2,1)} %queries_ref.1, bf16[32,128,128]{2,1,0:T(8,128)(2,1)} %keys_ref.1, ...), custom_call_target="tpu_custom_call" | custom-call | tf_op jit(solution)/shard_map/tokens_packed/pallas_call | solution.py:124
  3.6 18.8 %all-to-all-start = ((bf16[64,4,896]{2,1,0:T(4,128)(2,1)}), bf16[64,4,896]{2,1,0:T(4,128)(2,1)S(1)}, u32[]{:S(2)}, u32[]{:S(2)}) async-start(bf16[64,4,896]{2,1,0:T(4,128)(2,1)} %get-tuple-element.20), calls=%async_computation | async-start | bytes 917504 | tf_op jit(solution)/shard_map/all_to_all | solution.py:455
  22.4 0.0 copy-done.3
  22.4 0.1 pad_add_fusion.here_ref
  22.5 1.7 %multiply_convert_fusion.w_ref = bf16[768,1024]{1,0:T(8,128)(2,1)S(1)} fusion(bf16[768,1024]{1,0:T(8,128)(2,1)} %param.18, f32[768]{0:T(1024)S(1)} %convert_element_type.15), kind=kLoop, calls=%fused_computation | loop fusion | flops 2359296 | bytes 3148800 | tf_op jit(solution)/shard_map/convert_element_type | solution.py:454
  24.2 27.0 %all-to-all-done.received_ref = bf16[64,4,896]{2,1,0:T(4,128)(2,1)S(1)} async-done(((bf16[64,4,896]{2,1,0:T(4,128)(2,1)}), bf16[64,4,896]{2,1,0:T(4,128)(2,1)S(1)}, u32[]{:S(2)}, u32[]{:S(2)}) %all-to-all-start) | async-done | bytes 458784 | tf_op jit(solution)/shard_map/all_to_all | solution.py:455
  51.2 3.3 %compacted.1 = (bf16[120,768]{1,0:T(8,128)(2,1)S(1)}, bf16[480,384]{1,0:T(8,128)(2,1)S(1)}, bf16[256,128]{1,0:T(8,128)(2,1)S(1)}) custom-call(s32[2]{0:T(128)S(1)} %pad_add_fusion.here_ref, bf16[64,4,896]{2,1,0:T(4,128)(2,1)S(1)} %all-to-all-done.received_ref), custom_call_target="tpu_custom_call" | custom-call | tf_op jit(solution)/shard_map/compacted/pallas_call | solution.py:359
  54.5 17.4 %all_gather.6.gathered_ref = bf16[480,768]{1,0:T(8,128)(2,1)S(1)} all-gather(bf16[120,768]{1,0:T(8,128)(2,1)S(1)} %get-tuple-element.22), channel_id=1, replica_groups=mesh['x'=4,'zh'=2,'zq'=2,'zn'=4,'y'=4,'core'=2] {'zn'}, dimensions={0}, use_global_device_ids=true | all-gather | bytes 921600 | tf_op jit(solution)/shard_map/all_gather | solution.py:457
  71.9 0.8 sent_pieces.1
  72.8 0.0 copy-start.1
  72.8 0.0 copy-start.2
  72.8 1.9 %collective-permute-start = (bf16[4,400,128]{2,1,0:T(8,128)(2,1)S(1)}, bf16[4,400,128]{2,1,0:T(8,128)(2,1)S(1)}, u32[]{:S(2)}, u32[]{:S(2)}) collective-permute-start(bf16[4,400,128]{2,1,0:T(8,128)(2,1)S(1)} %get-tuple-element.31), channel_id=1, source_target_pairs={{0,1},{1,0},{2,3},{3,2},{4,5},{5,4},{6,7},{7,6},{8,9},{9,8},{10,11... | collective-permute-start | bytes 1228808 | tf_op jit(solution)/shard_map/ppermute | solution.py:460
  74.7 0.5 kept_pieces.1.own_ref
  75.2 0.0 copy-done.1
  75.2 0.0 copy-done.2
  75.2 1.1 way_back.1
  76.3 0.1 collective-permute-done.other_ref
  76.4 0.1 core_summed.1
  76.5 13.1 %all_to_all.25.in_ref = bf16[4,400,128]{2,1,0:T(8,128)(2,1)S(1)} all-to-all(bf16[4,400,128]{2,1,0:T(8,128)(2,1)S(1)} %core_summed.1), channel_id=1, replica_groups=mesh['x'=4,'zh'=2,'zq'=2,'zn'=4,'y'=4,'core'=2] {'y'}, dimensions={0} | all-to-all | bytes 819200 | tf_op jit(solution)/shard_map/all_to_all | solution.py:465
  89.6 0.0 copy-start
  89.7 0.2 silu_copies.1
  89.8 10.3 %all_to_all.26 = bf16[4,384,128]{2,1,0:T(8,128)(2,1)S(1)} all-to-all(bf16[4,384,128]{2,1,0:T(8,128)(2,1)S(1)} %silu_copies.1), channel_id=1, replica_groups=mesh['x'=4,'zh'=2,'zq'=2,'zn'=4,'y'=4,'core'=2] {'y'}, dimensions={0} | all-to-all | bytes 786432 | tf_op jit(solution)/shard_map/all_to_all | solution.py:466
  100.2 2.4 %all_gather.7.hidden_ref = bf16[8,384,128]{2,1,0:T(8,128)(2,1)S(1)} all-gather(bf16[4,384,128]{2,1,0:T(8,128)(2,1)S(1)} %all_to_all.26), channel_id=1, replica_groups=mesh['x'=4,'zh'=2,'zq'=2,'zn'=4,'y'=4,'core'=2] {'core'}, dimensions={0}, use_global_device_ids=true | all-gather | bytes 1179648 | tf_op jit(solution)/shard_map/all_gather | solution.py:467
  102.5 0.0 copy-done
  102.5 0.8 output_parts.1
  103.3 19.0 %all_to_all.27 = bf16[4,96,768]{2,1,0:T(8,128)(2,1)S(1)} all-to-all(bf16[4,96,768]{2,1,0:T(8,128)(2,1)S(1)} %bitcast.7), channel_id=1, replica_groups=mesh['x'=4,'zh'=2,'zq'=2,'zn'=4,'y'=4,'core'=2] {'zn'}, dimensions={0} | all-to-all | bytes 1179648 | tf_op jit(solution)/shard_map/all_to_all | solution.py:162
  122.3 0.1 reduce_sum.12
  122.4 0.2 convolution_convert_fusion
  122.6 0.1 reshape.17
  122.7 33.3 %all_to_all.28.combined_ref = bf16[64,4,768]{2,1,0:T(4,128)(2,1)S(1)} all-to-all(bf16[64,4,768]{2,1,0:T(4,128)(2,1)S(1)} %reshape.17), channel_id=1, replica_groups=mesh['x'=4,'zh'=2,'zq'=2,'zn'=4,'y'=4,'core'=2] {'x','zh','zq','zn'}, dimensions={0} | all-to-all | bytes 786432 | tf_op jit(solution)/shard_map/all_to_all | solution.py:474
  156.0 1.0 final_rows.1
  (1 shorter events, 0.0 us)
Async XLA Ops:
  0.0 22.4 %copy-start.3 = (bf16[768]{0:T(1024)(128)(2,1)S(1)}, bf16[768]{0:T(1024)(128)(2,1)}, u32[]{:S(2)}) copy-start(bf16[768]{0:T(1024)(128)(2,1)} %param.15) | copy-start | bytes 4612
  3.6 47.7 %all-to-all-start = ((bf16[64,4,896]{2,1,0:T(4,128)(2,1)}), bf16[64,4,896]{2,1,0:T(4,128)(2,1)S(1)}, u32[]{:S(2)}, u32[]{:S(2)}) async-start(bf16[64,4,896]{2,1,0:T(4,128)(2,1)} %get-tuple-element.20), calls=%async_computation | async-start | bytes 917504 | tf_op jit(solution)/shard_map/all_to_all | solution.py:455
  72.8 2.4 %copy-start.1 = (s32[32,2]{0,1:T(2,128)S(1)}, s32[32,2]{0,1:T(2,128)}, u32[]{:S(2)}) copy-start(s32[32,2]{0,1:T(2,128)} %param.16) | copy-start | bytes 772
  72.8 2.4 %copy-start.2 = (f32[32,2]{0,1:T(2,128)S(1)}, f32[32,2]{0,1:T(2,128)}, u32[]{:S(2)}) copy-start(f32[32,2]{0,1:T(2,128)} %param.17) | copy-start | bytes 772
  72.8 3.6 %collective-permute-start = (bf16[4,400,128]{2,1,0:T(8,128)(2,1)S(1)}, bf16[4,400,128]{2,1,0:T(8,128)(2,1)S(1)}, u32[]{:S(2)}, u32[]{:S(2)}) collective-permute-start(bf16[4,400,128]{2,1,0:T(8,128)(2,1)S(1)} %get-tuple-element.31), channel_id=1, source_target_pairs={{0,1},{1,0},{2,3},{3,2},{4,5},{5,4},{6,7},{7,6},{8,9},{9,8},{10,11... | collective-permute-start | bytes 1228808 | tf_op jit(solution)/shard_map/ppermute | solution.py:460
  89.6 12.9 %copy-start = (bf16[1024,768]{1,0:T(8,128)(2,1)S(1)}, bf16[1024,768]{1,0:T(8,128)(2,1)}, u32[]{:S(2)}) copy-start(bf16[1024,768]{1,0:T(8,128)(2,1)} %w_ref.1) | copy-start | bytes 4718596

commit v8 on v7

--- a/solution.py
+++ b/solution.py
@@ -303,12 +303,12 @@
     slots = all_counts.shape[0]
     row = lax.broadcasted_iota(jnp.int32, (slots, slots), 0)
     column = lax.broadcasted_iota(jnp.int32, (slots, slots), 1)
-    earlier = flags((column // PER_CLASS < row // PER_CLASS) & (column % PER_CLASS == 0))
+    earlier = flags(((column & 3) == 0) & (column < (row & -4)))
 
     def earlier_sum(counts):
         return jnp.dot(earlier, counts, preferred_element_type=jnp.float32).astype(jnp.int32)
 
-    own_expert = own_block // (BLOCKS // EXPERTS)
+    own_expert = own_block >> 3
     counts = jnp.dot(
         all_counts,
         flags(lax.broadcasted_iota(jnp.int32, (META, META), 0) == own_expert),
@@ -320,36 +320,37 @@
 
 def compact_kernel(here_ref, received_ref, rows_ref, place_ref, counts_ref):
     width = rows_ref.shape[1]
+    own_class = here_ref[1]
     received = received_ref[...].reshape(BLOCKS * PER_CLASS, width + META)
     all_counts = received[:, width:]
     counts_ref[...] = all_counts
     offset, kept, earlier_sum = kept_of_blocks(all_counts, here_ref[0])
     line = lax.broadcasted_iota(jnp.int32, kept.shape, 0)
     lane = lax.broadcasted_iota(jnp.int32, kept.shape, 1)
-    block, place = line // PER_CLASS, line % PER_CLASS
-
-    def class_order(of_class):
-        shift = (of_class + BLOCKS - block) % CLASSES
-        in_class = (kept - shift + CLASSES - 1) // CLASSES
-        first = earlier_sum(in_class.astype(jnp.float32).astype(jnp.bfloat16))
-        live = place < in_class
-        slot = jnp.where(live, offset + place * CLASSES + shift + 1, 0)
-        return flags((first + place == lane) & live), slot
-
-    chosen, _ = class_order(here_ref[1])
-    rows = lax.dot_general(
-        chosen, received[:, :width], (((0,), (0,)), ((), ())), preferred_element_type=jnp.float32
-    )
-    rows_ref[...] = rows[:CLASS_ROWS].astype(jnp.bfloat16)
-
-    for c in range(CLASSES):
-        chosen, slot = class_order(c)
-        digits = jnp.where(lane < META // 2, slot // 16, slot % 16).astype(jnp.float32).astype(jnp.bfloat16)
+    block, place = line >> 2, line & 3
+
+    shift = (own_class + (lane >> 5) + BLOCKS - block) & 3
+    in_class = (kept - shift + 3) >> 2
+    first = earlier_sum(in_class.astype(jnp.float32).astype(jnp.bfloat16))
+    live = place < in_class
+    spot = jnp.where(live, first + place, -1)
+    slot = jnp.where(live, offset + place * 4 + shift + 1, 0)
+    digits = jnp.where((lane & 16) == 0, slot >> 4, slot & 15).astype(jnp.float32).astype(jnp.bfloat16)
+
+    for turn in range(CLASSES):
+        start = turn * 32
+        chosen = flags(spot[:, start : start + 1] == lane)
+        if turn == 0:
+            rows = lax.dot_general(
+                chosen, received[:, :width], (((0,), (0,)), ((), ())), preferred_element_type=jnp.float32
+            )
+            rows_ref[...] = rows[:CLASS_ROWS].astype(jnp.bfloat16)
         found = lax.dot_general(chosen, digits, (((0,), (0,)), ((), ())), preferred_element_type=jnp.float32)
-        found = found[:CLASS_ROWS, :1] * 16.0 + found[:CLASS_ROWS, META // 2 : META // 2 + 1]
+        found = found[:CLASS_ROWS, start : start + 1] * 16.0 + found[:CLASS_ROWS, start + 16 : start + 17]
         found = found.astype(jnp.int32) - 1
-        target = jnp.where(found < 0, -1, found % CLASSES * SLOT_ROWS + found // CLASSES)
-        place_ref[c * CLASS_ROWS : (c + 1) * CLASS_ROWS] = flags(
+        target = jnp.where(found < 0, -1, (found & 3) * SLOT_ROWS + (found >> 2))
+        of_class = (own_class + turn) & 3
+        place_ref[pl.ds(pl.multiple_of(of_class * CLASS_ROWS, 8), CLASS_ROWS)] = flags(
             target == lax.broadcasted_iota(jnp.int32, (CLASS_ROWS, ROWS), 1)
         )
 
@@ -378,9 +379,9 @@
     offset, kept, _ = kept_of_blocks(all_counts, own_block)
     line = lax.broadcasted_iota(jnp.int32, kept.shape, 0)
     lane = lax.broadcasted_iota(jnp.int32, kept.shape, 1)
-    block, place = line // PER_CLASS, line % PER_CLASS
-    rank = place * CLASSES + (own_class + CLASSES * BLOCKS * SRC_CAP - offset) % CLASSES
-    back_ref[...] = flags(((offset + rank - own_class) // CLASSES == lane) & (rank < kept))
+    block, place = line >> 2, line & 3
+    rank = place * 4 + ((own_class - offset) & 3)
+    back_ref[...] = flags(((offset + rank - own_class) >> 2 == lane) & (rank < kept))
 
     ids = ids_ref[...]
     names, rank, _ = ranks(ids)

time: 157 us -> 156 us (level)
  Pallas kernels: 11.3 us -> 9.71 us
where the time goes in v8:
time: 156 us; the launch traced here: 155 us
  blocking collectives  95.3 us (61%)
  waiting for transfers between devices  27.2 us (17%)
  starting transfers between devices  20.7 us (13%)
  Pallas kernels  9.71 us (6%)
  other arithmetic  1.9 us (1%)
    all_to_all x1, blocking collectives, shards(): lax.all_to_all(returned.reshape(BLOCKS, PER_CLASS, width), DP, split_axis...  33.3 us
    all_to_all x1, waiting for transfers between devices, shards(): lax.all_to_all(outgoing, DP, split_axis=0, concat_axis=0, tiled=True)  27 us
    all_to_all x1, blocking collectives, summed_at_owner(): lax.all_to_all(pieces, axis, split_axis=0, concat_axis=0, tiled=True)  19 us
    all_to_all x1, starting transfers between devices, shards(): lax.all_to_all(outgoing, DP, split_axis=0, concat_axis=0, tiled=True)  18.8 us
    all_gather x1, blocking collectives, shards(): rows = lax.all_gather(class_rows, 'zn', axis=0, tiled=True)  17.4 us
    all_to_all x1, blocking collectives, shards(): lax.all_to_all(core_summed(own, other), 'y', split_axis=0, concat_axis=0,...  13 us
    all_to_all x1, blocking collectives, shards(): lax.all_to_all(silu_copies(pieces), 'y', split_axis=0, concat_axis=0, til...  10.3 us
    pallas_call x1, Pallas kernels, tokens_packed(): pl.pallas_call(tokens_kernel, grid=(TOKENS // STEP,), in_specs=[pl.BlockS...  3.57 us
  transfers between devices with their start and end apart: 2, of which 2 were waited for; matrix products, arithmetic and copies ran while one was open for 1% of the time, Pallas kernels for 1%

profile of v8, /device:TPU:6, one launch (start us, length us, event | category | flops | bytes accessed | tf_op | source)
XLA Modules:
  0.0 155.4 jit_solution(10145781070110121385)
XLA Ops:
  0.0 0.0 copy-start.3
  0.0 3.6 %tokens_packed.1 = (f32[32,768]{1,0:T(8,128)S(1)}, bf16[64,4,896]{2,1,0:T(4,128)(2,1)}) custom-call(s32[1]{0:T(128)} %bitcast.block_ref, s32[32]{0:T(128)} %lengths_ref.1, s32[2,32]{1,0:T(2,128)} %bitcast.8, bf16[32,768]{1,0:T(8,128)(2,1)} %residual_ref.1, bf16[32,768]{1,0:T(8,128)(2,1)} %queries_ref.1, bf16[32,128,128]{2,1,0:T(8,128)(2,1)} %keys_ref.1, ...), custom_call_target="tpu_custom_call" | custom-call | tf_op jit(solution)/shard_map/tokens_packed/pallas_call | solution.py:124
  3.6 18.8 %all-to-all-start = ((bf16[64,4,896]{2,1,0:T(4,128)(2,1)}), bf16[64,4,896]{2,1,0:T(4,128)(2,1)S(1)}, u32[]{:S(2)}, u32[]{:S(2)}) async-start(bf16[64,4,896]{2,1,0:T(4,128)(2,1)} %get-tuple-element.20), calls=%async_computation | async-start | bytes 917504 | tf_op jit(solution)/shard_map/all_to_all | solution.py:456
  22.4 0.0 copy-done.3
  22.4 0.1 pad_add_fusion.here_ref
  22.5 1.7 %multiply_convert_fusion.w_ref = bf16[768,1024]{1,0:T(8,128)(2,1)S(1)} fusion(bf16[768,1024]{1,0:T(8,128)(2,1)} %param.18, f32[768]{0:T(1024)S(1)} %convert_element_type.15), kind=kLoop, calls=%fused_computation | loop fusion | flops 2359296 | bytes 3148800 | tf_op jit(solution)/shard_map/convert_element_type | solution.py:455
  24.2 27.0 %all-to-all-done.received_ref = bf16[64,4,896]{2,1,0:T(4,128)(2,1)S(1)} async-done(((bf16[64,4,896]{2,1,0:T(4,128)(2,1)}), bf16[64,4,896]{2,1,0:T(4,128)(2,1)S(1)}, u32[]{:S(2)}, u32[]{:S(2)}) %all-to-all-start) | async-done | bytes 458784 | tf_op jit(solution)/shard_map/all_to_all | solution.py:456
  51.2 1.8 %compacted.1 = (bf16[120,768]{1,0:T(8,128)(2,1)S(1)}, bf16[480,384]{1,0:T(8,128)(2,1)S(1)}, bf16[256,128]{1,0:T(8,128)(2,1)S(1)}) custom-call(s32[2]{0:T(128)S(1)} %pad_add_fusion.here_ref, bf16[64,4,896]{2,1,0:T(4,128)(2,1)S(1)} %all-to-all-done.received_ref), custom_call_target="tpu_custom_call" | custom-call | tf_op jit(solution)/shard_map/compacted/pallas_call | solution.py:360
  53.0 17.4 %all_gather.6.gathered_ref = bf16[480,768]{1,0:T(8,128)(2,1)S(1)} all-gather(bf16[120,768]{1,0:T(8,128)(2,1)S(1)} %get-tuple-element.22), channel_id=1, replica_groups=mesh['x'=4,'zh'=2,'zq'=2,'zn'=4,'y'=4,'core'=2] {'zn'}, dimensions={0}, use_global_device_ids=true | all-gather | bytes 921600 | tf_op jit(solution)/shard_map/all_gather | solution.py:458
  70.4 0.8 sent_pieces.1
  71.3 0.0 copy-start.1
  71.3 0.0 copy-start.2
  71.3 1.9 %collective-permute-start = (bf16[4,400,128]{2,1,0:T(8,128)(2,1)S(1)}, bf16[4,400,128]{2,1,0:T(8,128)(2,1)S(1)}, u32[]{:S(2)}, u32[]{:S(2)}) collective-permute-start(bf16[4,400,128]{2,1,0:T(8,128)(2,1)S(1)} %get-tuple-element.31), channel_id=1, source_target_pairs={{0,1},{1,0},{2,3},{3,2},{4,5},{5,4},{6,7},{7,6},{8,9},{9,8},{10,11... | collective-permute-start | bytes 1228808 | tf_op jit(solution)/shard_map/ppermute | solution.py:461
  73.2 0.5 kept_pieces.1.own_ref
  73.7 0.0 copy-done.1
  73.7 0.0 copy-done.2
  73.7 1.0 way_back.1
  74.8 0.2 collective-permute-done.other_ref
  74.9 0.1 core_summed.1
  75.0 13.0 %all_to_all.25.in_ref = bf16[4,400,128]{2,1,0:T(8,128)(2,1)S(1)} all-to-all(bf16[4,400,128]{2,1,0:T(8,128)(2,1)S(1)} %core_summed.1), channel_id=1, replica_groups=mesh['x'=4,'zh'=2,'zq'=2,'zn'=4,'y'=4,'core'=2] {'y'}, dimensions={0} | all-to-all | bytes 819200 | tf_op jit(solution)/shard_map/all_to_all | solution.py:466
  88.1 0.0 copy-start
  88.1 0.2 silu_copies.1
  88.2 10.3 %all_to_all.26 = bf16[4,384,128]{2,1,0:T(8,128)(2,1)S(1)} all-to-all(bf16[4,384,128]{2,1,0:T(8,128)(2,1)S(1)} %silu_copies.1), channel_id=1, replica_groups=mesh['x'=4,'zh'=2,'zq'=2,'zn'=4,'y'=4,'core'=2] {'y'}, dimensions={0} | all-to-all | bytes 786432 | tf_op jit(solution)/shard_map/all_to_all | solution.py:467
  98.5 2.4 %all_gather.7.hidden_ref = bf16[8,384,128]{2,1,0:T(8,128)(2,1)S(1)} all-gather(bf16[4,384,128]{2,1,0:T(8,128)(2,1)S(1)} %all_to_all.26), channel_id=1, replica_groups=mesh['x'=4,'zh'=2,'zq'=2,'zn'=4,'y'=4,'core'=2] {'core'}, dimensions={0}, use_global_device_ids=true | all-gather | bytes 1179648 | tf_op jit(solution)/shard_map/all_gather | solution.py:468
  100.9 0.0 copy-done
  100.9 0.8 output_parts.1
  101.7 19.0 %all_to_all.27 = bf16[4,96,768]{2,1,0:T(8,128)(2,1)S(1)} all-to-all(bf16[4,96,768]{2,1,0:T(8,128)(2,1)S(1)} %bitcast.7), channel_id=1, replica_groups=mesh['x'=4,'zh'=2,'zq'=2,'zn'=4,'y'=4,'core'=2] {'zn'}, dimensions={0} | all-to-all | bytes 1179648 | tf_op jit(solution)/shard_map/all_to_all | solution.py:162
  120.6 0.1 reduce_sum.12
  120.7 0.2 convolution_convert_fusion
  121.0 0.1 reshape.17
  121.1 33.3 %all_to_all.28.combined_ref = bf16[64,4,768]{2,1,0:T(4,128)(2,1)S(1)} all-to-all(bf16[64,4,768]{2,1,0:T(4,128)(2,1)S(1)} %reshape.17), channel_id=1, replica_groups=mesh['x'=4,'zh'=2,'zq'=2,'zn'=4,'y'=4,'core'=2] {'x','zh','zq','zn'}, dimensions={0} | all-to-all | bytes 786432 | tf_op jit(solution)/shard_map/all_to_all | solution.py:475
  154.4 1.0 final_rows.1
  (1 shorter events, 0.0 us)
Async XLA Ops:
  0.0 22.4 %copy-start.3 = (bf16[768]{0:T(1024)(128)(2,1)S(1)}, bf16[768]{0:T(1024)(128)(2,1)}, u32[]{:S(2)}) copy-start(bf16[768]{0:T(1024)(128)(2,1)} %param.15) | copy-start | bytes 4612
  3.6 47.7 %all-to-all-start = ((bf16[64,4,896]{2,1,0:T(4,128)(2,1)}), bf16[64,4,896]{2,1,0:T(4,128)(2,1)S(1)}, u32[]{:S(2)}, u32[]{:S(2)}) async-start(bf16[64,4,896]{2,1,0:T(4,128)(2,1)} %get-tuple-element.20), calls=%async_computation | async-start | bytes 917504 | tf_op jit(solution)/shard_map/all_to_all | solution.py:456
  71.3 2.4 %copy-start.1 = (s32[32,2]{0,1:T(2,128)S(1)}, s32[32,2]{0,1:T(2,128)}, u32[]{:S(2)}) copy-start(s32[32,2]{0,1:T(2,128)} %param.16) | copy-start | bytes 772
  71.3 2.4 %copy-start.2 = (f32[32,2]{0,1:T(2,128)S(1)}, f32[32,2]{0,1:T(2,128)}, u32[]{:S(2)}) copy-start(f32[32,2]{0,1:T(2,128)} %param.17) | copy-start | bytes 772
  71.3 3.6 %collective-permute-start = (bf16[4,400,128]{2,1,0:T(8,128)(2,1)S(1)}, bf16[4,400,128]{2,1,0:T(8,128)(2,1)S(1)}, u32[]{:S(2)}, u32[]{:S(2)}) collective-permute-start(bf16[4,400,128]{2,1,0:T(8,128)(2,1)S(1)} %get-tuple-element.31), channel_id=1, source_target_pairs={{0,1},{1,0},{2,3},{3,2},{4,5},{5,4},{6,7},{7,6},{8,9},{9,8},{10,11... | collective-permute-start | bytes 1228808 | tf_op jit(solution)/shard_map/ppermute | solution.py:461
  88.1 12.8 %copy-start = (bf16[1024,768]{1,0:T(8,128)(2,1)S(1)}, bf16[1024,768]{1,0:T(8,128)(2,1)}, u32[]{:S(2)}) copy-start(bf16[1024,768]{1,0:T(8,128)(2,1)} %w_ref.1) | copy-start | bytes 4718596

commit v9 on v8

--- a/solution.py
+++ b/solution.py
@@ -157,12 +157,6 @@
     )
 
 
-def summed_at_owner(pieces, axis):
-    return jnp.sum(
-        lax.all_to_all(pieces, axis, split_axis=0, concat_axis=0, tiled=True).astype(jnp.float32), axis=0
-    )
-
-
 def diagonal():
     row = lax.broadcasted_iota(jnp.int32, (UNIT, UNIT), 0)
     return row == lax.broadcasted_iota(jnp.int32, (UNIT, UNIT), 1)
@@ -280,19 +274,26 @@
     )(pieces)
 
 
-def output_kernel(hidden_ref, w_ref, out_ref):
-    hidden = jnp.concatenate([hidden_ref[piece] for piece in range(hidden_ref.shape[0])], axis=1)
-    out_ref[...] = jnp.dot(hidden, w_ref[...], preferred_element_type=jnp.float32).astype(jnp.bfloat16)
-
-
-def output_parts(hidden, w_out):
+def output_kernel(class_ref, hidden_ref, w_ref, *out_refs):
+    for k, out_ref in enumerate(out_refs):
+        rows = pl.ds(pl.multiple_of((class_ref[0] ^ k) * SLOT_ROWS, SLOT_ROWS), SLOT_ROWS)
+        hidden = jnp.concatenate([hidden_ref[piece, rows] for piece in range(hidden_ref.shape[0])], axis=1)
+        out_ref[...] = jnp.dot(hidden, w_ref[...], preferred_element_type=jnp.float32).astype(jnp.bfloat16)
+
+
+def output_parts(hidden, w_out, own_class):
+    part = jax.ShapeDtypeStruct((SLOT_ROWS, w_out.shape[1]), jnp.bfloat16)
     return pl.pallas_call(
         output_kernel,
-        in_specs=[pl.BlockSpec(memory_space=pltpu.VMEM)] * 2,
-        out_shape=jax.ShapeDtypeStruct((ROWS, w_out.shape[1]), jnp.bfloat16),
+        in_specs=[
+            pl.BlockSpec(memory_space=pltpu.SMEM),
+            pl.BlockSpec(memory_space=pltpu.VMEM),
+            pl.BlockSpec(memory_space=pltpu.VMEM),
+        ],
+        out_shape=[part] * CLASSES,
         compiler_params=pltpu.CompilerParams(vmem_limit_bytes=10 << 20),
         name="output_parts",
-    )(hidden, w_out)
+    )(own_class.reshape(1), hidden, w_out)
 
 
 def flags(condition):
@@ -466,9 +467,11 @@
     pieces = lax.all_to_all(core_summed(own, other), "y", split_axis=0, concat_axis=0, tiled=True)
     gathered = lax.all_to_all(silu_copies(pieces), "y", split_axis=0, concat_axis=0, tiled=True)
     gathered = lax.all_gather(gathered, "core", axis=0, tiled=True)
-    results = output_parts(gathered, w_out)
-
-    class_out = summed_at_owner(results.reshape(CLASSES, SLOT_ROWS, width), "zn").astype(jnp.bfloat16)
+    parts = output_parts(gathered, w_out, own_class)
+    shares = [parts[0]]
+    for k in (2, 3, 1):
+        shares.append(lax.ppermute(parts[k], "zn", [(i, i ^ k) for i in range(CLASSES)]))
+    class_out = sum(share.astype(jnp.float32) for share in shares).astype(jnp.bfloat16)
     returned = jnp.dot(
         back[:, :SLOT_ROWS], class_out, preferred_element_type=jnp.float32
     ).astype(jnp.bfloat16)

time: 156 us -> 156 us (level)
  blocking collectives: 95.3 us -> 77.4 us
  starting transfers between devices: 20.7 us -> 29.9 us
  waiting for transfers between devices: 27.2 us -> 35.2 us
    all_to_all x1 -> x0, blocking collectives: 19 us -> none  [summed_at_owner(): lax.all_to_all(pieces, axis, split_axis=0, concat_axis=0, tiled=True)]
    ppermute x0 -> x3, starting transfers between devices: none -> 9.21 us  [shards(): lax.ppermute(parts[k], 'zn', [(i, i ^ k) for i in range(CLASSES)])]
    ppermute x0 -> x3, waiting for transfers between devices: none -> 8.02 us  [shards(): lax.ppermute(parts[k], 'zn', [(i, i ^ k) for i in range(CLASSES)])]
  transfers between devices with their start and end apart: 2 -> 5, of which waited for: 2 -> 4; matrix products, arithmetic and copies ran while one was open for 1% -> 1% of each run, Pallas kernels for 1% -> 1%
where the time goes in v9:
time: 156 us; the launch traced here: 155 us
  blocking collectives  77.4 us (50%)
  waiting for transfers between devices  35.2 us (23%)
  starting transfers between devices  29.9 us (19%)
  Pallas kernels  10.1 us (6%)
  other arithmetic  1.81 us (1%)
    all_to_all x1, blocking collectives, shards(): lax.all_to_all(returned.reshape(BLOCKS, PER_CLASS, width), DP, split_axis...  34.4 us
    all_to_all x1, waiting for transfers between devices, shards(): lax.all_to_all(outgoing, DP, split_axis=0, concat_axis=0, tiled=True)  27 us
    all_to_all x1, starting transfers between devices, shards(): lax.all_to_all(outgoing, DP, split_axis=0, concat_axis=0, tiled=True)  18.8 us
    all_gather x1, blocking collectives, shards(): rows = lax.all_gather(class_rows, 'zn', axis=0, tiled=True)  17.4 us
    all_to_all x1, blocking collectives, shards(): lax.all_to_all(core_summed(own, other), 'y', split_axis=0, concat_axis=0,...  13 us
    all_to_all x1, blocking collectives, shards(): lax.all_to_all(silu_copies(pieces), 'y', split_axis=0, concat_axis=0, til...  10.3 us
    ppermute x3, starting transfers between devices, shards(): lax.ppermute(parts[k], 'zn', [(i, i ^ k) for i in range(CLASSES)])  9.21 us
    ppermute x3, waiting for transfers between devices, shards(): lax.ppermute(parts[k], 'zn', [(i, i ^ k) for i in range(CLASSES)])  8.02 us
  transfers between devices with their start and end apart: 5, of which 4 were waited for; matrix products, arithmetic and copies ran while one was open for 1% of the time, Pallas kernels for 1%

profile of v9, /device:TPU:6, one launch (start us, length us, event | category | flops | bytes accessed | tf_op | source)
XLA Modules:
  0.0 155.1 jit_solution(9343322419459581113)
XLA Ops:
  0.0 0.0 copy-start.3
  0.0 3.6 %tokens_packed.1 = (f32[32,768]{1,0:T(8,128)S(1)}, bf16[64,4,896]{2,1,0:T(4,128)(2,1)}) custom-call(s32[1]{0:T(128)} %bitcast.block_ref, s32[32]{0:T(128)} %lengths_ref.1, s32[2,32]{1,0:T(2,128)} %bitcast.5, bf16[32,768]{1,0:T(8,128)(2,1)} %residual_ref.1, bf16[32,768]{1,0:T(8,128)(2,1)} %queries_ref.1, bf16[32,128,128]{2,1,0:T(8,128)(2,1)} %keys_ref.1, ...), custom_call_target="tpu_custom_call" | custom-call | tf_op jit(solution)/shard_map/tokens_packed/pallas_call | solution.py:124
  3.6 18.8 %all-to-all-start = ((bf16[64,4,896]{2,1,0:T(4,128)(2,1)}), bf16[64,4,896]{2,1,0:T(4,128)(2,1)S(1)}, u32[]{:S(2)}, u32[]{:S(2)}) async-start(bf16[64,4,896]{2,1,0:T(4,128)(2,1)} %get-tuple-element.24), calls=%async_computation | async-start | bytes 917504 | tf_op jit(solution)/shard_map/all_to_all | solution.py:457
  22.4 0.0 copy-done.3
  22.4 0.1 pad_add_fusion.here_ref
  22.5 1.7 %multiply_convert_fusion.w_ref = bf16[768,1024]{1,0:T(8,128)(2,1)S(1)} fusion(bf16[768,1024]{1,0:T(8,128)(2,1)} %param.18, f32[768]{0:T(1024)S(1)} %convert_element_type.28), kind=kLoop, calls=%fused_computation | loop fusion | flops 2359296 | bytes 3148800 | tf_op jit(solution)/shard_map/convert_element_type | solution.py:456
  24.2 27.0 %all-to-all-done.received_ref = bf16[64,4,896]{2,1,0:T(4,128)(2,1)S(1)} async-done(((bf16[64,4,896]{2,1,0:T(4,128)(2,1)}), bf16[64,4,896]{2,1,0:T(4,128)(2,1)S(1)}, u32[]{:S(2)}, u32[]{:S(2)}) %all-to-all-start) | async-done | bytes 458784 | tf_op jit(solution)/shard_map/all_to_all | solution.py:457
  51.2 1.8 %compacted.1 = (bf16[120,768]{1,0:T(8,128)(2,1)S(1)}, bf16[480,384]{1,0:T(8,128)(2,1)S(1)}, bf16[256,128]{1,0:T(8,128)(2,1)S(1)}) custom-call(s32[2]{0:T(128)S(1)} %pad_add_fusion.here_ref, bf16[64,4,896]{2,1,0:T(4,128)(2,1)S(1)} %all-to-all-done.received_ref), custom_call_target="tpu_custom_call" | custom-call | tf_op jit(solution)/shard_map/compacted/pallas_call | solution.py:361
  53.0 17.4 %all_gather.6.gathered_ref = bf16[480,768]{1,0:T(8,128)(2,1)S(1)} all-gather(bf16[120,768]{1,0:T(8,128)(2,1)S(1)} %get-tuple-element.26), channel_id=1, replica_groups=mesh['x'=4,'zh'=2,'zq'=2,'zn'=4,'y'=4,'core'=2] {'zn'}, dimensions={0}, use_global_device_ids=true | all-gather | bytes 921600 | tf_op jit(solution)/shard_map/all_gather | solution.py:459
  70.4 0.8 sent_pieces.1
  71.3 0.0 copy-start.1
  71.3 0.0 copy-start.2
  71.3 1.9 %collective-permute-start = (bf16[4,400,128]{2,1,0:T(8,128)(2,1)S(1)}, bf16[4,400,128]{2,1,0:T(8,128)(2,1)S(1)}, u32[]{:S(2)}, u32[]{:S(2)}) collective-permute-start(bf16[4,400,128]{2,1,0:T(8,128)(2,1)S(1)} %get-tuple-element.35), channel_id=1, source_target_pairs={{0,1},{1,0},{2,3},{3,2},{4,5},{5,4},{6,7},{7,6},{8,9},{9,8},{10,11... | collective-permute-start | bytes 1228808 | tf_op jit(solution)/shard_map/ppermute | solution.py:462
  73.2 0.5 kept_pieces.1.own_ref
  73.7 0.0 copy-done.1
  73.7 0.0 copy-done.2
  73.7 1.0 way_back.1
  74.8 0.2 collective-permute-done.other_ref
  74.9 0.1 core_summed.1
  75.0 13.0 %all_to_all.20.in_ref = bf16[4,400,128]{2,1,0:T(8,128)(2,1)S(1)} all-to-all(bf16[4,400,128]{2,1,0:T(8,128)(2,1)S(1)} %core_summed.1), channel_id=1, replica_groups=mesh['x'=4,'zh'=2,'zq'=2,'zn'=4,'y'=4,'core'=2] {'y'}, dimensions={0} | all-to-all | bytes 819200 | tf_op jit(solution)/shard_map/all_to_all | solution.py:467
  88.1 0.0 copy-start
  88.1 0.2 silu_copies.1
  88.2 10.3 %all_to_all.21 = bf16[4,384,128]{2,1,0:T(8,128)(2,1)S(1)} all-to-all(bf16[4,384,128]{2,1,0:T(8,128)(2,1)S(1)} %silu_copies.1), channel_id=1, replica_groups=mesh['x'=4,'zh'=2,'zq'=2,'zn'=4,'y'=4,'core'=2] {'y'}, dimensions={0} | all-to-all | bytes 786432 | tf_op jit(solution)/shard_map/all_to_all | solution.py:468
  98.5 2.4 %all_gather.7.hidden_ref = bf16[8,384,128]{2,1,0:T(8,128)(2,1)S(1)} all-gather(bf16[4,384,128]{2,1,0:T(8,128)(2,1)S(1)} %all_to_all.21), channel_id=1, replica_groups=mesh['x'=4,'zh'=2,'zq'=2,'zn'=4,'y'=4,'core'=2] {'core'}, dimensions={0}, use_global_device_ids=true | all-gather | bytes 1179648 | tf_op jit(solution)/shard_map/all_gather | solution.py:469
  100.9 0.0 copy-done
  100.9 1.2 output_parts.1
  102.0 2.7 %collective-permute-start.1 = (bf16[96,768]{1,0:T(8,128)(2,1)S(1)}, bf16[96,768]{1,0:T(8,128)(2,1)S(1)}, u32[]{:S(2)}, u32[]{:S(2)}) collective-permute-start(bf16[96,768]{1,0:T(8,128)(2,1)S(1)} %get-tuple-element.37), channel_id=1, source_target_pairs={{0,16},{8,24},{16,0},{24,8},{1,17},{9,25},{17,1},{25,9},{2,18},{10... | collective-permute-start | bytes 442376 | tf_op jit(solution)/shard_map/ppermute | solution.py:473
  104.8 3.1 %collective-permute-start.2 = (bf16[96,768]{1,0:T(8,128)(2,1)S(1)}, bf16[96,768]{1,0:T(8,128)(2,1)S(1)}, u32[]{:S(2)}, u32[]{:S(2)}) collective-permute-start(bf16[96,768]{1,0:T(8,128)(2,1)S(1)} %get-tuple-element.38), channel_id=1, source_target_pairs={{0,24},{8,16},{16,8},{24,0},{1,25},{9,17},{17,9},{25,1},{2,26},{10... | collective-permute-start | bytes 442376 | tf_op jit(solution)/shard_map/ppermute | solution.py:473
  107.9 3.4 %collective-permute-start.3 = (bf16[96,768]{1,0:T(8,128)(2,1)S(1)}, bf16[96,768]{1,0:T(8,128)(2,1)S(1)}, u32[]{:S(2)}, u32[]{:S(2)}) collective-permute-start(bf16[96,768]{1,0:T(8,128)(2,1)S(1)} %get-tuple-element.39), channel_id=1, source_target_pairs={{0,8},{8,0},{16,24},{24,16},{1,9},{9,1},{17,25},{25,17},{2,10},{10... | collective-permute-start | bytes 442376 | tf_op jit(solution)/shard_map/ppermute | solution.py:473
  111.3 5.0 %collective-permute-done.1 = bf16[96,768]{1,0:T(8,128)(2,1)S(1)} collective-permute-done((bf16[96,768]{1,0:T(8,128)(2,1)S(1)}, bf16[96,768]{1,0:T(8,128)(2,1)S(1)}, u32[]{:S(2)}, u32[]{:S(2)}) %collective-permute-start.1) | collective-permute-done | bytes 147488 | tf_op jit(solution)/shard_map/ppermute | solution.py:473
  116.3 0.0 collective-permute-done.2
  116.3 3.0 %collective-permute-done.3 = bf16[96,768]{1,0:T(8,128)(2,1)S(1)} collective-permute-done((bf16[96,768]{1,0:T(8,128)(2,1)S(1)}, bf16[96,768]{1,0:T(8,128)(2,1)S(1)}, u32[]{:S(2)}, u32[]{:S(2)}) %collective-permute-start.3) | collective-permute-done | bytes 147488 | tf_op jit(solution)/shard_map/ppermute | solution.py:473
  119.3 0.3 convolution_convert_fusion
  119.6 0.1 reshape.14
  119.7 34.4 %all_to_all.22.combined_ref = bf16[64,4,768]{2,1,0:T(4,128)(2,1)S(1)} all-to-all(bf16[64,4,768]{2,1,0:T(4,128)(2,1)S(1)} %reshape.14), channel_id=1, replica_groups=mesh['x'=4,'zh'=2,'zq'=2,'zn'=4,'y'=4,'core'=2] {'x','zh','zq','zn'}, dimensions={0} | all-to-all | bytes 786432 | tf_op jit(solution)/shard_map/all_to_all | solution.py:478
  154.1 1.0 final_rows.1
  (1 shorter events, 0.0 us)
Async XLA Ops:
  0.0 22.4 %copy-start.3 = (bf16[768]{0:T(1024)(128)(2,1)S(1)}, bf16[768]{0:T(1024)(128)(2,1)}, u32[]{:S(2)}) copy-start(bf16[768]{0:T(1024)(128)(2,1)} %param.15) | copy-start | bytes 4612
  3.6 47.7 %all-to-all-start = ((bf16[64,4,896]{2,1,0:T(4,128)(2,1)}), bf16[64,4,896]{2,1,0:T(4,128)(2,1)S(1)}, u32[]{:S(2)}, u32[]{:S(2)}) async-start(bf16[64,4,896]{2,1,0:T(4,128)(2,1)} %get-tuple-element.24), calls=%async_computation | async-start | bytes 917504 | tf_op jit(solution)/shard_map/all_to_all | solution.py:457
  71.3 2.4 %copy-start.1 = (s32[32,2]{0,1:T(2,128)S(1)}, s32[32,2]{0,1:T(2,128)}, u32[]{:S(2)}) copy-start(s32[32,2]{0,1:T(2,128)} %param.16) | copy-start | bytes 772
  71.3 2.4 %copy-start.2 = (f32[32,2]{0,1:T(2,128)S(1)}, f32[32,2]{0,1:T(2,128)}, u32[]{:S(2)}) copy-start(f32[32,2]{0,1:T(2,128)} %param.17) | copy-start | bytes 772
  71.3 3.6 %collective-permute-start = (bf16[4,400,128]{2,1,0:T(8,128)(2,1)S(1)}, bf16[4,400,128]{2,1,0:T(8,128)(2,1)S(1)}, u32[]{:S(2)}, u32[]{:S(2)}) collective-permute-start(bf16[4,400,128]{2,1,0:T(8,128)(2,1)S(1)} %get-tuple-element.35), channel_id=1, source_target_pairs={{0,1},{1,0},{2,3},{3,2},{4,5},{5,4},{6,7},{7,6},{8,9},{9,8},{10,11... | collective-permute-start | bytes 1228808 | tf_op jit(solution)/shard_map/ppermute | solution.py:462
  88.1 12.8 %copy-start = (bf16[1024,768]{1,0:T(8,128)(2,1)S(1)}, bf16[1024,768]{1,0:T(8,128)(2,1)}, u32[]{:S(2)}) copy-start(bf16[1024,768]{1,0:T(8,128)(2,1)} %w_ref.1) | copy-start | bytes 4718596
  102.0 14.2 %collective-permute-start.1 = (bf16[96,768]{1,0:T(8,128)(2,1)S(1)}, bf16[96,768]{1,0:T(8,128)(2,1)S(1)}, u32[]{:S(2)}, u32[]{:S(2)}) collective-permute-start(bf16[96,768]{1,0:T(8,128)(2,1)S(1)} %get-tuple-element.37), channel_id=1, source_target_pairs={{0,16},{8,24},{16,0},{24,8},{1,17},{9,25},{17,1},{25,9},{2,18},{10... | collective-permute-start | bytes 442376 | tf_op jit(solution)/shard_map/ppermute | solution.py:473
  104.8 11.5 %collective-permute-start.2 = (bf16[96,768]{1,0:T(8,128)(2,1)S(1)}, bf16[96,768]{1,0:T(8,128)(2,1)S(1)}, u32[]{:S(2)}, u32[]{:S(2)}) collective-permute-start(bf16[96,768]{1,0:T(8,128)(2,1)S(1)} %get-tuple-element.38), channel_id=1, source_target_pairs={{0,24},{8,16},{16,8},{24,0},{1,25},{9,17},{17,9},{25,1},{2,26},{10... | collective-permute-start | bytes 442376 | tf_op jit(solution)/shard_map/ppermute | solution.py:473
  107.9 11.4 %collective-permute-start.3 = (bf16[96,768]{1,0:T(8,128)(2,1)S(1)}, bf16[96,768]{1,0:T(8,128)(2,1)S(1)}, u32[]{:S(2)}, u32[]{:S(2)}) collective-permute-start(bf16[96,768]{1,0:T(8,128)(2,1)S(1)} %get-tuple-element.39), channel_id=1, source_target_pairs={{0,8},{8,0},{16,24},{24,16},{1,9},{9,1},{17,25},{25,17},{2,10},{10... | collective-permute-start | bytes 442376 | tf_op jit(solution)/shard_map/ppermute | solution.py:473

commit v10 on v9

--- a/solution.py
+++ b/solution.py
@@ -274,11 +274,13 @@
     )(pieces)
 
 
-def output_kernel(class_ref, hidden_ref, w_ref, *out_refs):
+def output_kernel(class_ref, hidden_ref, w_ref, *refs):
+    *out_refs, whole_ref = refs
+    hidden = jnp.concatenate([hidden_ref[piece] for piece in range(hidden_ref.shape[0])], axis=1)
+    whole_ref[...] = jnp.dot(hidden, w_ref[...], preferred_element_type=jnp.float32).astype(jnp.bfloat16)
     for k, out_ref in enumerate(out_refs):
-        rows = pl.ds(pl.multiple_of((class_ref[0] ^ k) * SLOT_ROWS, SLOT_ROWS), SLOT_ROWS)
-        hidden = jnp.concatenate([hidden_ref[piece, rows] for piece in range(hidden_ref.shape[0])], axis=1)
-        out_ref[...] = jnp.dot(hidden, w_ref[...], preferred_element_type=jnp.float32).astype(jnp.bfloat16)
+        start = pl.multiple_of((class_ref[0] ^ k) * SLOT_ROWS, SLOT_ROWS)
+        out_ref[...] = whole_ref[pl.ds(start, SLOT_ROWS)]
 
 
 def output_parts(hidden, w_out, own_class):
@@ -291,6 +293,7 @@
             pl.BlockSpec(memory_space=pltpu.VMEM),
         ],
         out_shape=[part] * CLASSES,
+        scratch_shapes=[pltpu.VMEM((ROWS, w_out.shape[1]), jnp.bfloat16)],
         compiler_params=pltpu.CompilerParams(vmem_limit_bytes=10 << 20),
         name="output_parts",
     )(own_class.reshape(1), hidden, w_out)

time: 156 us -> 155 us (level)
  no operation moved by 1% of the time
where the time goes in v10:
time: 155 us
  blocking collectives  77.4 us (50%)
  waiting for transfers between devices  35.2 us (23%)
  starting transfers between devices  29.9 us (19%)
  Pallas kernels  9.76 us (6%)
  other arithmetic  1.81 us (1%)
    all_to_all x1, blocking collectives, shards(): lax.all_to_all(returned.reshape(BLOCKS, PER_CLASS, width), DP, split_axis...  34.4 us
    all_to_all x1, waiting for transfers between devices, shards(): lax.all_to_all(outgoing, DP, split_axis=0, concat_axis=0, tiled=True)  27 us
    all_to_all x1, starting transfers between devices, shards(): lax.all_to_all(outgoing, DP, split_axis=0, concat_axis=0, tiled=True)  18.8 us
    all_gather x1, blocking collectives, shards(): rows = lax.all_gather(class_rows, 'zn', axis=0, tiled=True)  17.4 us
    all_to_all x1, blocking collectives, shards(): lax.all_to_all(core_summed(own, other), 'y', split_axis=0, concat_axis=0,...  13 us
    all_to_all x1, blocking collectives, shards(): lax.all_to_all(silu_copies(pieces), 'y', split_axis=0, concat_axis=0, til...  10.3 us
    ppermute x3, starting transfers between devices, shards(): lax.ppermute(parts[k], 'zn', [(i, i ^ k) for i in range(CLASSES)])  9.21 us
    ppermute x3, waiting for transfers between devices, shards(): lax.ppermute(parts[k], 'zn', [(i, i ^ k) for i in range(CLASSES)])  8.01 us
  transfers between devices with their start and end apart: 5, of which 4 were waited for; matrix products, arithmetic and copies ran while one was open for 1% of the time, Pallas kernels for 1%

profile of v10, /device:TPU:6, one launch (start us, length us, event | category | flops | bytes accessed | tf_op | source)
XLA Modules:
  0.0 154.7 jit_solution(14669105262544275037)
XLA Ops:
  0.0 0.0 copy-start.3
  0.0 3.6 %tokens_packed.1 = (f32[32,768]{1,0:T(8,128)S(1)}, bf16[64,4,896]{2,1,0:T(4,128)(2,1)}) custom-call(s32[1]{0:T(128)} %bitcast.block_ref, s32[32]{0:T(128)} %lengths_ref.1, s32[2,32]{1,0:T(2,128)} %bitcast.5, bf16[32,768]{1,0:T(8,128)(2,1)} %residual_ref.1, bf16[32,768]{1,0:T(8,128)(2,1)} %queries_ref.1, bf16[32,128,128]{2,1,0:T(8,128)(2,1)} %keys_ref.1, ...), custom_call_target="tpu_custom_call" | custom-call | tf_op jit(solution)/shard_map/tokens_packed/pallas_call | solution.py:124
  3.6 18.8 %all-to-all-start = ((bf16[64,4,896]{2,1,0:T(4,128)(2,1)}), bf16[64,4,896]{2,1,0:T(4,128)(2,1)S(1)}, u32[]{:S(2)}, u32[]{:S(2)}) async-start(bf16[64,4,896]{2,1,0:T(4,128)(2,1)} %get-tuple-element.24), calls=%async_computation | async-start | bytes 917504 | tf_op jit(solution)/shard_map/all_to_all | solution.py:460
  22.4 0.0 copy-done.3
  22.4 0.1 pad_add_fusion.here_ref
  22.5 1.7 %multiply_convert_fusion.w_ref = bf16[768,1024]{1,0:T(8,128)(2,1)S(1)} fusion(bf16[768,1024]{1,0:T(8,128)(2,1)} %param.18, f32[768]{0:T(1024)S(1)} %convert_element_type.28), kind=kLoop, calls=%fused_computation | loop fusion | flops 2359296 | bytes 3148800 | tf_op jit(solution)/shard_map/convert_element_type | solution.py:459
  24.2 27.0 %all-to-all-done.received_ref = bf16[64,4,896]{2,1,0:T(4,128)(2,1)S(1)} async-done(((bf16[64,4,896]{2,1,0:T(4,128)(2,1)}), bf16[64,4,896]{2,1,0:T(4,128)(2,1)S(1)}, u32[]{:S(2)}, u32[]{:S(2)}) %all-to-all-start) | async-done | bytes 458784 | tf_op jit(solution)/shard_map/all_to_all | solution.py:460
  51.2 1.8 %compacted.1 = (bf16[120,768]{1,0:T(8,128)(2,1)S(1)}, bf16[480,384]{1,0:T(8,128)(2,1)S(1)}, bf16[256,128]{1,0:T(8,128)(2,1)S(1)}) custom-call(s32[2]{0:T(128)S(1)} %pad_add_fusion.here_ref, bf16[64,4,896]{2,1,0:T(4,128)(2,1)S(1)} %all-to-all-done.received_ref), custom_call_target="tpu_custom_call" | custom-call | tf_op jit(solution)/shard_map/compacted/pallas_call | solution.py:364
  53.0 17.4 %all_gather.6.gathered_ref = bf16[480,768]{1,0:T(8,128)(2,1)S(1)} all-gather(bf16[120,768]{1,0:T(8,128)(2,1)S(1)} %get-tuple-element.26), channel_id=1, replica_groups=mesh['x'=4,'zh'=2,'zq'=2,'zn'=4,'y'=4,'core'=2] {'zn'}, dimensions={0}, use_global_device_ids=true | all-gather | bytes 921600 | tf_op jit(solution)/shard_map/all_gather | solution.py:462
  70.4 0.8 sent_pieces.1
  71.3 0.0 copy-start.1
  71.3 0.0 copy-start.2
  71.3 1.9 %collective-permute-start = (bf16[4,400,128]{2,1,0:T(8,128)(2,1)S(1)}, bf16[4,400,128]{2,1,0:T(8,128)(2,1)S(1)}, u32[]{:S(2)}, u32[]{:S(2)}) collective-permute-start(bf16[4,400,128]{2,1,0:T(8,128)(2,1)S(1)} %get-tuple-element.35), channel_id=1, source_target_pairs={{0,1},{1,0},{2,3},{3,2},{4,5},{5,4},{6,7},{7,6},{8,9},{9,8},{10,11... | collective-permute-start | bytes 1228808 | tf_op jit(solution)/shard_map/ppermute | solution.py:465
  73.2 0.5 kept_pieces.1.own_ref
  73.7 0.0 copy-done.1
  73.7 0.0 copy-done.2
  73.7 1.0 way_back.1
  74.8 0.2 collective-permute-done.other_ref
  74.9 0.1 core_summed.1
  75.0 13.0 %all_to_all.20.in_ref = bf16[4,400,128]{2,1,0:T(8,128)(2,1)S(1)} all-to-all(bf16[4,400,128]{2,1,0:T(8,128)(2,1)S(1)} %core_summed.1), channel_id=1, replica_groups=mesh['x'=4,'zh'=2,'zq'=2,'zn'=4,'y'=4,'core'=2] {'y'}, dimensions={0} | all-to-all | bytes 819200 | tf_op jit(solution)/shard_map/all_to_all | solution.py:470
  88.1 0.0 copy-start
  88.1 0.2 silu_copies.1
  88.2 10.3 %all_to_all.21 = bf16[4,384,128]{2,1,0:T(8,128)(2,1)S(1)} all-to-all(bf16[4,384,128]{2,1,0:T(8,128)(2,1)S(1)} %silu_copies.1), channel_id=1, replica_groups=mesh['x'=4,'zh'=2,'zq'=2,'zn'=4,'y'=4,'core'=2] {'y'}, dimensions={0} | all-to-all | bytes 786432 | tf_op jit(solution)/shard_map/all_to_all | solution.py:471
  98.5 2.4 %all_gather.7.hidden_ref = bf16[8,384,128]{2,1,0:T(8,128)(2,1)S(1)} all-gather(bf16[4,384,128]{2,1,0:T(8,128)(2,1)S(1)} %all_to_all.21), channel_id=1, replica_groups=mesh['x'=4,'zh'=2,'zq'=2,'zn'=4,'y'=4,'core'=2] {'core'}, dimensions={0}, use_global_device_ids=true | all-gather | bytes 1179648 | tf_op jit(solution)/shard_map/all_gather | solution.py:472
  100.9 0.0 copy-done
  100.9 0.8 output_parts.1
  101.7 2.7 %collective-permute-start.1 = (bf16[96,768]{1,0:T(8,128)(2,1)S(1)}, bf16[96,768]{1,0:T(8,128)(2,1)S(1)}, u32[]{:S(2)}, u32[]{:S(2)}) collective-permute-start(bf16[96,768]{1,0:T(8,128)(2,1)S(1)} %get-tuple-element.37), channel_id=1, source_target_pairs={{0,16},{8,24},{16,0},{24,8},{1,17},{9,25},{17,1},{25,9},{2,18},{10... | collective-permute-start | bytes 442376 | tf_op jit(solution)/shard_map/ppermute | solution.py:476
  104.4 3.1 %collective-permute-start.2 = (bf16[96,768]{1,0:T(8,128)(2,1)S(1)}, bf16[96,768]{1,0:T(8,128)(2,1)S(1)}, u32[]{:S(2)}, u32[]{:S(2)}) collective-permute-start(bf16[96,768]{1,0:T(8,128)(2,1)S(1)} %get-tuple-element.38), channel_id=1, source_target_pairs={{0,24},{8,16},{16,8},{24,0},{1,25},{9,17},{17,9},{25,1},{2,26},{10... | collective-permute-start | bytes 442376 | tf_op jit(solution)/shard_map/ppermute | solution.py:476
  107.6 3.4 %collective-permute-start.3 = (bf16[96,768]{1,0:T(8,128)(2,1)S(1)}, bf16[96,768]{1,0:T(8,128)(2,1)S(1)}, u32[]{:S(2)}, u32[]{:S(2)}) collective-permute-start(bf16[96,768]{1,0:T(8,128)(2,1)S(1)} %get-tuple-element.39), channel_id=1, source_target_pairs={{0,8},{8,0},{16,24},{24,16},{1,9},{9,1},{17,25},{25,17},{2,10},{10... | collective-permute-start | bytes 442376 | tf_op jit(solution)/shard_map/ppermute | solution.py:476
  110.9 5.0 %collective-permute-done.1 = bf16[96,768]{1,0:T(8,128)(2,1)S(1)} collective-permute-done((bf16[96,768]{1,0:T(8,128)(2,1)S(1)}, bf16[96,768]{1,0:T(8,128)(2,1)S(1)}, u32[]{:S(2)}, u32[]{:S(2)}) %collective-permute-start.1) | collective-permute-done | bytes 147488 | tf_op jit(solution)/shard_map/ppermute | solution.py:476
  115.9 0.0 collective-permute-done.2
  115.9 3.0 %collective-permute-done.3 = bf16[96,768]{1,0:T(8,128)(2,1)S(1)} collective-permute-done((bf16[96,768]{1,0:T(8,128)(2,1)S(1)}, bf16[96,768]{1,0:T(8,128)(2,1)S(1)}, u32[]{:S(2)}, u32[]{:S(2)}) %collective-permute-start.3) | collective-permute-done | bytes 147488 | tf_op jit(solution)/shard_map/ppermute | solution.py:476
  119.0 0.3 convolution_convert_fusion
  119.3 0.1 reshape.14
  119.4 34.4 %all_to_all.22.combined_ref = bf16[64,4,768]{2,1,0:T(4,128)(2,1)S(1)} all-to-all(bf16[64,4,768]{2,1,0:T(4,128)(2,1)S(1)} %reshape.14), channel_id=1, replica_groups=mesh['x'=4,'zh'=2,'zq'=2,'zn'=4,'y'=4,'core'=2] {'x','zh','zq','zn'}, dimensions={0} | all-to-all | bytes 786432 | tf_op jit(solution)/shard_map/all_to_all | solution.py:481
  153.8 1.0 final_rows.1
  (1 shorter events, 0.0 us)
Async XLA Ops:
  0.0 22.4 %copy-start.3 = (bf16[768]{0:T(1024)(128)(2,1)S(1)}, bf16[768]{0:T(1024)(128)(2,1)}, u32[]{:S(2)}) copy-start(bf16[768]{0:T(1024)(128)(2,1)} %param.15) | copy-start | bytes 4612
  3.6 47.7 %all-to-all-start = ((bf16[64,4,896]{2,1,0:T(4,128)(2,1)}), bf16[64,4,896]{2,1,0:T(4,128)(2,1)S(1)}, u32[]{:S(2)}, u32[]{:S(2)}) async-start(bf16[64,4,896]{2,1,0:T(4,128)(2,1)} %get-tuple-element.24), calls=%async_computation | async-start | bytes 917504 | tf_op jit(solution)/shard_map/all_to_all | solution.py:460
  71.3 2.4 %copy-start.1 = (s32[32,2]{0,1:T(2,128)S(1)}, s32[32,2]{0,1:T(2,128)}, u32[]{:S(2)}) copy-start(s32[32,2]{0,1:T(2,128)} %param.16) | copy-start | bytes 772
  71.3 2.4 %copy-start.2 = (f32[32,2]{0,1:T(2,128)S(1)}, f32[32,2]{0,1:T(2,128)}, u32[]{:S(2)}) copy-start(f32[32,2]{0,1:T(2,128)} %param.17) | copy-start | bytes 772
  71.3 3.6 %collective-permute-start = (bf16[4,400,128]{2,1,0:T(8,128)(2,1)S(1)}, bf16[4,400,128]{2,1,0:T(8,128)(2,1)S(1)}, u32[]{:S(2)}, u32[]{:S(2)}) collective-permute-start(bf16[4,400,128]{2,1,0:T(8,128)(2,1)S(1)} %get-tuple-element.35), channel_id=1, source_target_pairs={{0,1},{1,0},{2,3},{3,2},{4,5},{5,4},{6,7},{7,6},{8,9},{9,8},{10,11... | collective-permute-start | bytes 1228808 | tf_op jit(solution)/shard_map/ppermute | solution.py:465
  88.1 12.8 %copy-start = (bf16[1024,768]{1,0:T(8,128)(2,1)S(1)}, bf16[1024,768]{1,0:T(8,128)(2,1)}, u32[]{:S(2)}) copy-start(bf16[1024,768]{1,0:T(8,128)(2,1)} %w_ref.1) | copy-start | bytes 4718596
  101.7 14.2 %collective-permute-start.1 = (bf16[96,768]{1,0:T(8,128)(2,1)S(1)}, bf16[96,768]{1,0:T(8,128)(2,1)S(1)}, u32[]{:S(2)}, u32[]{:S(2)}) collective-permute-start(bf16[96,768]{1,0:T(8,128)(2,1)S(1)} %get-tuple-element.37), channel_id=1, source_target_pairs={{0,16},{8,24},{16,0},{24,8},{1,17},{9,25},{17,1},{25,9},{2,18},{10... | collective-permute-start | bytes 442376 | tf_op jit(solution)/shard_map/ppermute | solution.py:476
  104.4 11.5 %collective-permute-start.2 = (bf16[96,768]{1,0:T(8,128)(2,1)S(1)}, bf16[96,768]{1,0:T(8,128)(2,1)S(1)}, u32[]{:S(2)}, u32[]{:S(2)}) collective-permute-start(bf16[96,768]{1,0:T(8,128)(2,1)S(1)} %get-tuple-element.38), channel_id=1, source_target_pairs={{0,24},{8,16},{16,8},{24,0},{1,25},{9,17},{17,9},{25,1},{2,26},{10... | collective-permute-start | bytes 442376 | tf_op jit(solution)/shard_map/ppermute | solution.py:476
  107.6 11.4 %collective-permute-start.3 = (bf16[96,768]{1,0:T(8,128)(2,1)S(1)}, bf16[96,768]{1,0:T(8,128)(2,1)S(1)}, u32[]{:S(2)}, u32[]{:S(2)}) collective-permute-start(bf16[96,768]{1,0:T(8,128)(2,1)S(1)} %get-tuple-element.39), channel_id=1, source_target_pairs={{0,8},{8,0},{16,24},{24,16},{1,9},{9,1},{17,25},{25,17},{2,10},{10... | collective-permute-start | bytes 442376 | tf_op jit(solution)/shard_map/ppermute | solution.py:476
